TPU v7x, 512 devices: a whole 4x8x8 slice. The times are simulated.
512 devices in a mesh: seq: 64 (over x, z, core), rep: 8 (over y).
Axes of the slice: x: 4, y: 8, z: 8, core: 2. Of those that a mesh axis runs over, the one named last changes fastest.
Arguments:
- token_ids: int32 [32, 4], P('rep'), parts along dimension 0, may hold values from 0 to 24703
- cache_lengths: int32 [32], P('rep'), parts along dimension 0, may hold values from 1 to 8192, 8216 in all
- embed_table: bfloat16 [2048, 24704], P('seq'), may hold values from -0.119628906 to 0.119628906
- key_cache: bfloat16 [32, 8192, 512], P('rep', 'seq'), parts along dimension 0, may hold values from -4000 to 4000
- value_cache: bfloat16 [32, 8192, 512], P('rep', 'seq'), parts along dimension 0, may hold values from -24 to 24
- norm_attn: bfloat16 [2048], replicated, may hold values from 0.25 to 1.75
- norm_mlp: bfloat16 [2048], replicated, may hold values from 0.25 to 1.75
- w_qkv: bfloat16 [2048, 3072], P(None, 'seq'), may hold values from -0.125 to 0.125
- w_out: bfloat16 [2048, 2048], P(None, 'seq'), may hold values from -0.125 to 0.125
- w_gate: bfloat16 [2048, 8192], P(None, 'seq'), may hold values from -0.125 to 0.125
- w_up: bfloat16 [2048, 8192], P(None, 'seq'), may hold values from -0.125 to 0.125
- w_down: bfloat16 [8192, 2048], P('seq'), may hold values from -0.0625 to 0.0625
Outputs:
- layer_out: bfloat16 [32, 4, 2048], P('rep'), parts along dimension 0
There are 8 independent parts, one for each index of `rep`. A program takes and returns all parts, laid end to end along the dimension named above; an argument that names none is the same for every part. Nothing has to cross between parts.
All inputs are finite; a program needn't handle non-finite values.
Results may differ from a plain program's by a relative error of at most 0.012.
The roundings to bfloat16 on the way count: a program that leaves them out, or rounds other values in their place, can miss the bound.
Values may be sent and summed in bfloat16 or wider, within the bound.
A program may use at most 128 MiB of HBM per device.

v0:
```python
import jax
import jax.numpy as jnp
from jax import lax
from jax.sharding import PartitionSpec as P

H = 32
KVH = 8
HD = 64
STEPS = 4


norm_epsilon = 1e-05
embed_factor = 12.0
score_factor = 0.015625
branch_factor = 0.22
rope_base = 10000000.0
masked_floor = -1e30


def joined(part, axis, combine):
    gathered = jax.tree.map(lambda a: lax.all_gather(a, axis), part)

    def take(source):
        return jax.tree.map(lambda a: lax.dynamic_index_in_dim(a, source, 0, False), gathered)

    return lax.fori_loop(
        1, lax.axis_size(axis), lambda source, state: combine(state, take(source)), take(0)
    )


def rms_scale(resid, gain):
    mean_square = jnp.mean(resid * resid, axis=-1, keepdims=True)
    return resid * lax.rsqrt(mean_square + norm_epsilon) * gain.astype(jnp.float32)


def rotate(vectors, where):
    half = vectors.shape[-1] // 2
    freqs = rope_base ** (-2.0 * jnp.arange(half, dtype=jnp.float32) / vectors.shape[-1])
    angle = where[..., None] * freqs
    cosine = jnp.cos(angle)
    sine = jnp.sin(angle)
    first_half = vectors[..., :half]
    second_half = vectors[..., half:]
    return jnp.concatenate(
        [first_half * cosine - second_half * sine, second_half * cosine + first_half * sine],
        axis=-1,
    )


def partial_softmax(queries, keys, values, valid):
    scores = (
        jnp.einsum("rskgd,rpkd->rskgp", queries, keys, preferred_element_type=jnp.float32)
        * score_factor
    )
    maxima = jnp.max(jnp.where(valid, scores, masked_floor), axis=-1)
    expo = jnp.exp(jnp.where(valid, scores - maxima[..., None], masked_floor))
    totals = jnp.sum(expo, axis=-1)
    outputs = jnp.einsum(
        "rskgp,rpkd->rskgd", expo.astype(jnp.bfloat16), values, preferred_element_type=jnp.float32
    )
    return (maxima, totals, outputs)


def pair_merge(first_part, second_part):
    max_first, total_first, out_first = first_part
    max_second, total_second, out_second = second_part
    overall = jnp.maximum(max_first, max_second)
    scale_first = jnp.exp(max_first - overall)
    scale_second = jnp.exp(max_second - overall)
    return (
        overall,
        scale_first * total_first + scale_second * total_second,
        scale_first[..., None] * out_first + scale_second[..., None] * out_second,
    )


def finish(cache_part, fresh_part):
    overall, totals, outputs = pair_merge(cache_part, fresh_part)
    return outputs / totals[..., None]


def shards(
    token_ids,
    cache_lengths,
    embed_table,
    key_cache,
    value_cache,
    norm_attn,
    norm_mlp,
    w_qkv,
    w_out,
    w_gate,
    w_up,
    w_down,
):
    place = lax.axis_index("seq")
    req_all = token_ids.shape[0]
    ctx_own = key_cache.shape[1]
    att_width = H * HD
    kv_width = KVH * HD
    group = H // KVH
    picked = jnp.take(embed_table, token_ids.reshape(-1), axis=1).reshape(
        embed_table.shape[0], req_all, STEPS
    )
    whole = lax.all_gather(picked, "seq", axis=0, tiled=True)
    embedded = jnp.transpose(whole, (1, 2, 0)).astype(jnp.float32) * embed_factor
    slot_pos = place * ctx_own + jnp.arange(ctx_own, dtype=jnp.int32)
    cache_valid = (slot_pos[None, :] < cache_lengths[:, None]).reshape(req_all, 1, 1, 1, ctx_own)
    cache_keys = key_cache.reshape(req_all, ctx_own, KVH, HD)
    cache_values = value_cache.reshape(req_all, ctx_own, KVH, HD)
    fresh_keys = jnp.zeros((req_all, STEPS, KVH, HD), jnp.bfloat16)
    fresh_values = jnp.zeros((req_all, STEPS, KVH, HD), jnp.bfloat16)
    spans = [(step_index, 1) for step_index in range(STEPS)]
    results = []
    for first_step, step_count in spans:
        resid = embedded[:, first_step : first_step + step_count, :]
        normed = rms_scale(resid, norm_attn).astype(jnp.bfloat16)
        qkv_cols = jnp.einsum(
            "rsd,dc->rsc", normed, w_qkv, preferred_element_type=jnp.float32
        ).astype(jnp.bfloat16)
        qkv_all = lax.all_gather(qkv_cols, "seq", axis=2, tiled=True)
        where = (
            cache_lengths[:, None] + first_step + jnp.arange(step_count, dtype=jnp.int32)[None, :]
        ).astype(jnp.float32)
        queries = rotate(
            qkv_all[..., :att_width].reshape(req_all, step_count, H, HD).astype(jnp.float32),
            where[..., None],
        ).astype(jnp.bfloat16)
        keys_new = rotate(
            qkv_all[..., att_width : att_width + kv_width]
            .reshape(req_all, step_count, KVH, HD)
            .astype(jnp.float32),
            where[..., None],
        ).astype(jnp.bfloat16)
        values_new = qkv_all[..., att_width + kv_width :].reshape(req_all, step_count, KVH, HD)
        grouped = queries.reshape(req_all, step_count, KVH, group, HD)
        cache_max, cache_total, cache_out = partial_softmax(
            grouped, cache_keys, cache_values, cache_valid
        )
        fresh_valid = (
            jnp.arange(STEPS, dtype=jnp.int32)[None, :]
            <= first_step + jnp.arange(step_count, dtype=jnp.int32)[:, None]
        ).reshape(1, step_count, 1, 1, STEPS)
        fresh_keys = fresh_keys.at[:, first_step : first_step + step_count].set(keys_new)
        fresh_values = fresh_values.at[:, first_step : first_step + step_count].set(values_new)
        fresh_part = partial_softmax(grouped, fresh_keys, fresh_values, fresh_valid)
        merged = joined((cache_max, cache_total, cache_out), "seq", pair_merge)
        attention = (
            finish(merged, fresh_part).astype(jnp.bfloat16).reshape(req_all, step_count, att_width)
        )
        proj_cols = jnp.einsum(
            "rsa,ac->rsc", attention, w_out, preferred_element_type=jnp.float32
        ).astype(jnp.bfloat16)
        projected = lax.all_gather(proj_cols, "seq", axis=2, tiled=True)
        middle = resid + branch_factor * projected.astype(jnp.float32)
        normed_mlp = rms_scale(middle, norm_mlp).astype(jnp.bfloat16)
        gate = jnp.einsum("rsd,df->rsf", normed_mlp, w_gate, preferred_element_type=jnp.float32)
        upward = jnp.einsum("rsd,df->rsf", normed_mlp, w_up, preferred_element_type=jnp.float32)
        hidden = (jax.nn.silu(gate) * upward).astype(jnp.bfloat16)
        down_part = jnp.einsum("rsf,fd->rsd", hidden, w_down, preferred_element_type=jnp.float32)
        down = lax.psum(down_part, "seq")
        results.append((middle + branch_factor * down).astype(jnp.bfloat16))
    stacked_out = jnp.concatenate(results, axis=1)
    return stacked_out


def solution(mesh):
    return jax.shard_map(
        shards,
        mesh=mesh,
        in_specs=(
            P("rep", None),
            P("rep"),
            P("seq", None),
            P("rep", "seq", None),
            P("rep", "seq", None),
            P(),
            P(),
            P(None, "seq"),
            P(None, "seq"),
            P(None, "seq"),
            P(None, "seq"),
            P("seq", None),
        ),
        out_specs=P("rep", None, None),
        check_vma=False,
    )
```

profile of v0, /device:TPU:1, one launch (start us, length us, event | category | flops | bytes accessed | tf_op | source)
XLA Modules:
  0.0 1510.8 jit_solution(3654583654004366891)
XLA Ops:
  8.1 6.4 copy.224
  14.4 4.2 gather_fusion
  18.9 58.3 %all_gather.99 = bf16[2048,4,4]{2,1,0:T(4,128)(2,1)S(1)} all-gather(bf16[32,4,4]{2,1,0:T(4,128)(2,1)S(1)} %copy.225), channel_id=1, replica_groups=mesh['seq'=64,'rep'=8] {'seq'}, dimensions={0}, use_global_device_ids=true | all-gather | bytes 66560 | tf_op jit(solution)/shard_map/all_gather | solution.py:105
  77.2 1.3 copy.226
  78.7 1.1 fusion.56
  79.9 42.8 %all-gather.20 = bf16[64,48,4]{1,2,0:T(4,128)(2,1)S(1)} all-gather(bf16[1,48,4]{1,2,0:T(4,128)(2,1)S(1)} %fusion.56), channel_id=2, replica_groups=mesh['seq'=64,'rep'=8] {'seq'}, dimensions={0}, use_global_device_ids=true | all-gather | bytes 24960 | tf_op jit(solution)/shard_map/all_gather | solution.py:121
  122.9 1.1 fusion.58
  124.0 41.3 %all-gather.22 = bf16[64,48,4]{1,2,0:T(4,128)(2,1)S(1)} all-gather(bf16[1,48,4]{1,2,0:T(4,128)(2,1)S(1)} %fusion.58), channel_id=7, replica_groups=mesh['seq'=64,'rep'=8] {'seq'}, dimensions={0}, use_global_device_ids=true | all-gather | bytes 24960 | tf_op jit(solution)/shard_map/all_gather | solution.py:121
  165.7 1.1 fusion.60
  166.9 42.8 %all-gather.24 = bf16[64,48,4]{1,2,0:T(4,128)(2,1)S(1)} all-gather(bf16[1,48,4]{1,2,0:T(4,128)(2,1)S(1)} %fusion.60), channel_id=12, replica_groups=mesh['seq'=64,'rep'=8] {'seq'}, dimensions={0}, use_global_device_ids=true | all-gather | bytes 24960 | tf_op jit(solution)/shard_map/all_gather | solution.py:121
  209.9 1.1 fusion.62
  211.0 41.3 %all-gather.26 = bf16[64,48,4]{1,2,0:T(4,128)(2,1)S(1)} all-gather(bf16[1,48,4]{1,2,0:T(4,128)(2,1)S(1)} %fusion.62), channel_id=17, replica_groups=mesh['seq'=64,'rep'=8] {'seq'}, dimensions={0}, use_global_device_ids=true | all-gather | bytes 24960 | tf_op jit(solution)/shard_map/all_gather | solution.py:121
  265.5 49.3 %all-gather.17 = f32[256,8,4]{1,2,0:T(4,128)S(1)} all-gather(f32[4,8,4]{1,2,0:T(4,128)S(1)} %copy.285), channel_id=19, replica_groups=mesh['seq'=64,'rep'=8] {'seq'}, dimensions={0}, use_global_device_ids=true | all-gather | bytes 33280 | tf_op jit(solution)/shard_map/all_gather | solution.py:21
  315.6 47.9 %all-gather.16 = f32[256,8,4]{1,2,0:T(4,128)S(1)} all-gather(f32[4,8,4]{1,2,0:T(4,128)S(1)} %copy.284), channel_id=18, replica_groups=mesh['seq'=64,'rep'=8] {'seq'}, dimensions={0}, use_global_device_ids=true | all-gather | bytes 33280 | tf_op jit(solution)/shard_map/all_gather | solution.py:21
  365.0 49.2 %all-gather.12 = f32[256,8,4]{1,2,0:T(4,128)S(1)} all-gather(f32[4,8,4]{1,2,0:T(4,128)S(1)} %copy.267), channel_id=14, replica_groups=mesh['seq'=64,'rep'=8] {'seq'}, dimensions={0}, use_global_device_ids=true | all-gather | bytes 33280 | tf_op jit(solution)/shard_map/all_gather | solution.py:21
  415.0 47.9 %all-gather.11 = f32[256,8,4]{1,2,0:T(4,128)S(1)} all-gather(f32[4,8,4]{1,2,0:T(4,128)S(1)} %copy.266), channel_id=13, replica_groups=mesh['seq'=64,'rep'=8] {'seq'}, dimensions={0}, use_global_device_ids=true | all-gather | bytes 33280 | tf_op jit(solution)/shard_map/all_gather | solution.py:21
  464.5 49.4 %all-gather.7 = f32[256,8,4]{1,2,0:T(4,128)S(1)} all-gather(f32[4,8,4]{1,2,0:T(4,128)S(1)} %copy.249), channel_id=9, replica_groups=mesh['seq'=64,'rep'=8] {'seq'}, dimensions={0}, use_global_device_ids=true | all-gather | bytes 33280 | tf_op jit(solution)/shard_map/all_gather | solution.py:21
  513.9 47.9 %all-gather.6 = f32[256,8,4]{1,2,0:T(4,128)S(1)} all-gather(f32[4,8,4]{1,2,0:T(4,128)S(1)} %copy.248), channel_id=8, replica_groups=mesh['seq'=64,'rep'=8] {'seq'}, dimensions={0}, use_global_device_ids=true | all-gather | bytes 33280 | tf_op jit(solution)/shard_map/all_gather | solution.py:21
  564.0 49.2 %all-gather.2 = f32[256,8,4]{1,2,0:T(4,128)S(1)} all-gather(f32[4,8,4]{1,2,0:T(4,128)S(1)} %copy.230), channel_id=4, replica_groups=mesh['seq'=64,'rep'=8] {'seq'}, dimensions={0}, use_global_device_ids=true | all-gather | bytes 33280 | tf_op jit(solution)/shard_map/all_gather | solution.py:21
  614.1 47.8 %all-gather.1 = f32[256,8,4]{1,2,0:T(4,128)S(1)} all-gather(f32[4,8,4]{1,2,0:T(4,128)} %copy.229), channel_id=3, replica_groups=mesh['seq'=64,'rep'=8] {'seq'}, dimensions={0}, use_global_device_ids=true | all-gather | bytes 33280 | tf_op jit(solution)/shard_map/all_gather | solution.py:21
  661.9 1.3 convert_element_type.368
  664.2 129.6 %while.87 = (s32[]{:T(128)}, f32[4,1,8,4]{2,3,0,1:T(4,128)S(1)}, f32[4,1,8,4]{2,3,0,1:T(4,128)S(1)}, f32[4,1,8,4,64]{4,3,2,1,0:T(4,128)S(1)}, f32[64,4,1,8,4]{3,...) while((s32[]{:T(128)}, f32[4,1,8,4]{2,3,0,1:T(4,128)S(1)}, ...), condition=%wide.region_31.32_spmd, body=%wide.region_30.31_spmd.sunk | while | flops 25477 | bytes 173723 | solution.py:26
  795.0 129.7 %while.86 = (s32[]{:T(128)}, f32[4,1,8,4]{2,3,0,1:T(4,128)S(1)}, f32[4,1,8,4]{2,3,0,1:T(4,128)S(1)}, f32[4,1,8,4,64]{4,3,2,1,0:T(4,128)S(1)}, f32[64,4,1,8,4]{3,...) while((s32[]{:T(128)}, f32[4,1,8,4]{2,3,0,1:T(4,128)S(1)}, ...), condition=%wide.region_22.23_spmd, body=%wide.region_21.22_spmd.sunk | while | flops 25477 | bytes 173723 | solution.py:26
  925.6 85.8 %while.85 = (s32[]{:T(128)}, f32[4,1,8,4]{2,3,0,1:T(4,128)S(1)}, f32[4,1,8,4]{2,3,0,1:T(4,128)S(1)}, f32[4,1,8,4,64]{4,3,2,1,0:T(4,128)S(1)}, f32[64,4,1,8,4]{3,...) while((s32[]{:T(128)}, f32[4,1,8,4]{2,3,0,1:T(4,128)S(1)}, ...), condition=%wide.region_13.14_spmd, body=%wide.region_12.13_spmd.sunk | while | flops 25477 | bytes 173723 | solution.py:26
  1014.4 42.7 %all-gather.27 = bf16[64,32,4]{1,2,0:T(4,128)(2,1)S(1)} all-gather(bf16[1,32,4]{1,2,0:T(4,128)(2,1)S(1)} %fusion.63), channel_id=21, replica_groups=mesh['seq'=64,'rep'=8] {'seq'}, dimensions={0}, use_global_device_ids=true | all-gather | bytes 16640 | tf_op jit(solution)/shard_map/all_gather | solution.py:154
  1057.6 41.4 %all-gather.25 = bf16[64,32,4]{1,2,0:T(4,128)(2,1)S(1)} all-gather(bf16[1,32,4]{1,2,0:T(4,128)(2,1)S(1)} %fusion.61), channel_id=16, replica_groups=mesh['seq'=64,'rep'=8] {'seq'}, dimensions={0}, use_global_device_ids=true | all-gather | bytes 16640 | tf_op jit(solution)/shard_map/all_gather | solution.py:154
  1099.5 42.7 %all-gather.23 = bf16[64,32,4]{1,2,0:T(4,128)(2,1)S(1)} all-gather(bf16[1,32,4]{1,2,0:T(4,128)(2,1)S(1)} %fusion.59), channel_id=11, replica_groups=mesh['seq'=64,'rep'=8] {'seq'}, dimensions={0}, use_global_device_ids=true | all-gather | bytes 16640 | tf_op jit(solution)/shard_map/all_gather | solution.py:154
  1143.5 129.6 %while.84 = (s32[]{:T(128)}, f32[4,1,8,4]{2,3,0,1:T(4,128)S(1)}, f32[4,1,8,4]{2,3,0,1:T(4,128)S(1)}, f32[4,1,8,4,64]{4,3,2,1,0:T(4,128)S(1)}, f32[64,4,1,8,4]{3,...) while((s32[]{:T(128)}, f32[4,1,8,4]{2,3,0,1:T(4,128)S(1)}, ...), condition=%wide.region_4.5_spmd, body=%wide.region_3.4_spmd.sunk | while | flops 25477 | bytes 173723 | solution.py:26
  1274.0 41.4 %all-gather.21 = bf16[64,32,4]{1,2,0:T(4,128)(2,1)S(1)} all-gather(bf16[1,32,4]{1,2,0:T(4,128)(2,1)S(1)} %fusion.57), channel_id=6, replica_groups=mesh['seq'=64,'rep'=8] {'seq'}, dimensions={0}, use_global_device_ids=true | all-gather | bytes 16640 | tf_op jit(solution)/shard_map/all_gather | solution.py:154
  1316.5 1.0 convolution_bitcast_fusion.3
  1319.7 1.0 convolution_bitcast_fusion
  1320.7 181.8 %all-reduce.5.cloned.1.call-done = (f32[4,1,2048]{2,0,1:T(4,128)}, f32[4,1,2048]{2,0,1:T(4,128)}, f32[4,1,2048]{2,0,1:T(4,128)}, f32[4,1,2048]{2,0,1:T(4,128)}) async-done(((f32[4,1,2048]{2,0,1:T(4,128)}, f32[4,1,2048]{2,0,1:T(4,128)}, f32[4,1,2048]{2,0,1:T(4,128)}, f32[4,1,2048]{2,0,1:T(4,128)}), (f32[4,1,2048]{2,0,1:T(4,128)}, f32[4,1,2048]{2,0,1:T(4,128)}, f32[4,1,2048]{2,0,1:T(4,128)}, ...) | async-done | bytes 131088 | tf_op jit(solution)/shard_map/psum | solution.py:161
  (2045 shorter events, 501.8 us)
Async XLA Ops:
  6.5 1309.9 %copy-start = (bf16[128,2048]{1,0:T(8,128)(2,1)S(1)}, bf16[128,2048]{1,0:T(8,128)(2,1)}, u32[]{:S(2)}) copy-start(bf16[128,2048]{1,0:T(8,128)(2,1)} %param.47) | copy-start | bytes 1572868
  6.5 656.8 %all-gather.39.cloned.1.call-start = ((), (), s32[]{:S(2)}) async-start(), calls=%async_computation.3 | async-start | bytes 4259840 | tf_op jit(solution)/shard_map/all_gather | solution.py:21
  14.4 238.3 %copy-start.6 = (bf16[4,128,512]{2,1,0:T(8,128)(2,1)S(1)}, bf16[4,128,512]{2,1,0:T(8,128)(2,1)}, u32[]{:S(2)}) copy-start(bf16[4,128,512]{2,1,0:T(8,128)(2,1)} %param.39) | copy-start | bytes 1572868
  256.2 537.9 %all-gather.37.cloned.1.call-start = ((), (), s32[]{:S(2)}) async-start(), calls=%async_computation.2 | async-start | bytes 4259840 | tf_op jit(solution)/shard_map/all_gather | solution.py:21
  257.3 667.4 %all-gather.35.cloned.1.call-start = ((), (), s32[]{:S(2)}) async-start(), calls=%async_computation.1 | async-start | bytes 4259840 | tf_op jit(solution)/shard_map/all_gather | solution.py:21
  258.5 884.1 %all-gather.33.cloned.1.call-start = ((), (), s32[]{:S(2)}) async-start(), calls=%async_computation | async-start | bytes 4259840 | tf_op jit(solution)/shard_map/all_gather | solution.py:21
  259.6 1242.8 %all-reduce.5.cloned.1.call-start = ((), (), s32[]{:S(2)}) async-start(), calls=%async_computation.4 | async-start | bytes 262144 | tf_op jit(solution)/shard_map/psum | solution.py:161
  259.7 302.1 %copy-start.40 = (pred[4]{0:T(512)(128)(4,1)}, pred[4]{0:T(512)(128)(4,1)S(1)}, u32[]{:S(2)}) copy-start(pred[4]{0:T(512)(128)(4,1)S(1)} %iota_compare_fusion.3) | copy-start | bytes 16
  259.8 302.0 %copy-start.38 = (pred[4]{0:T(512)(128)(4,1)}, pred[4]{0:T(512)(128)(4,1)S(1)}, u32[]{:S(2)}) copy-start(pred[4]{0:T(512)(128)(4,1)S(1)} %iota_compare_fusion.2) | copy-start | bytes 16
  259.8 302.0 %copy-start.36 = (pred[4]{0:T(512)(128)(4,1)}, pred[4]{0:T(512)(128)(4,1)S(1)}, u32[]{:S(2)}) copy-start(pred[4]{0:T(512)(128)(4,1)S(1)} %iota_compare_fusion.1) | copy-start | bytes 16
  260.5 352.7 %copy-start.34 = (pred[4]{0:T(512)(128)(4,1)}, pred[4]{0:T(512)(128)(4,1)S(1)}, u32[]{:S(2)}) copy-start(pred[4]{0:T(512)(128)(4,1)S(1)} %iota_compare_fusion.4) | copy-start | bytes 16
  262.3 351.0 %copy-start.10 = (f32[4,8,4,1,4]{4,2,1,0,3:T(4,128)}, f32[4,8,4,1,4]{4,2,1,0,3:T(4,128)S(1)}, u32[]{:S(2)}) copy-start(f32[4,8,4,1,4]{4,2,1,0,3:T(4,128)S(1)} %get-tuple-element.1095) | copy-start | bytes 6148
  262.3 351.0 %copy-start.16 = (f32[4,8,4]{2,1,0:T(8,128)}, f32[4,8,4]{2,1,0:T(8,128)S(1)}, u32[]{:S(2)}) copy-start(f32[4,8,4]{2,1,0:T(8,128)S(1)} %get-tuple-element.1094) | copy-start | bytes 1540
  263.8 349.4 %copy-start.12 = (f32[4,8,4,1,4]{4,2,1,0,3:T(4,128)}, f32[4,8,4,1,4]{4,2,1,0,3:T(4,128)S(1)}, u32[]{:S(2)}) copy-start(f32[4,8,4,1,4]{4,2,1,0,3:T(4,128)S(1)} %get-tuple-element.1099) | copy-start | bytes 6148
  263.8 349.4 %copy-start.18 = (f32[4,8,4]{2,1,0:T(8,128)}, f32[4,8,4]{2,1,0:T(8,128)S(1)}, u32[]{:S(2)}) copy-start(f32[4,8,4]{2,1,0:T(8,128)S(1)} %get-tuple-element.1098) | copy-start | bytes 1540
  664.2 348.2 %copy-start.17 = (f32[4,8,4]{2,1,0:T(8,128)S(1)}, f32[4,8,4]{2,1,0:T(8,128)}, u32[]{:S(2)}) copy-start(f32[4,8,4]{2,1,0:T(8,128)} %copy-done.16) | copy-start | bytes 1540
  793.9 218.5 %copy-start.11 = (f32[4,8,4,1,4]{4,2,1,0,3:T(4,128)S(1)}, f32[4,8,4,1,4]{4,2,1,0,3:T(4,128)}, u32[]{:S(2)}) copy-start(f32[4,8,4,1,4]{4,2,1,0,3:T(4,128)} %copy-done.10) | copy-start | bytes 6148
  794.0 218.5 %copy-start.31 = (bf16[4,4,8,64]{3,1,2,0:T(4,128)(2,1)S(1)}, bf16[4,4,8,64]{3,1,2,0:T(4,128)(2,1)}, u32[]{:S(2)}) copy-start(bf16[4,4,8,64]{3,1,2,0:T(4,128)(2,1)} %copy-done.30) | copy-start | bytes 49156
  794.0 219.2 %copy-start.15 = (f32[4,8,4,1,4]{4,2,1,0,3:T(4,128)S(1)}, f32[4,8,4,1,4]{4,2,1,0,3:T(4,128)}, u32[]{:S(2)}) copy-start(f32[4,8,4,1,4]{4,2,1,0,3:T(4,128)} %copy-done.14) | copy-start | bytes 6148
  794.0 219.2 %copy-start.21 = (f32[4,8,4]{2,1,0:T(8,128)S(1)}, f32[4,8,4]{2,1,0:T(8,128)}, u32[]{:S(2)}) copy-start(f32[4,8,4]{2,1,0:T(8,128)} %copy-done.20) | copy-start | bytes 1540
  794.0 219.2 %copy-start.39 = (pred[4]{0:T(512)(128)(4,1)S(1)}, pred[4]{0:T(512)(128)(4,1)}, u32[]{:S(2)}) copy-start(pred[4]{0:T(512)(128)(4,1)} %copy-done.38) | copy-start | bytes 16
  795.0 218.8 %copy-start.13 = (f32[4,8,4,1,4]{4,2,1,0,3:T(4,128)S(1)}, f32[4,8,4,1,4]{4,2,1,0,3:T(4,128)}, u32[]{:S(2)}) copy-start(f32[4,8,4,1,4]{4,2,1,0,3:T(4,128)} %copy-done.12) | copy-start | bytes 6148
  795.0 218.8 %copy-start.19 = (f32[4,8,4]{2,1,0:T(8,128)S(1)}, f32[4,8,4]{2,1,0:T(8,128)}, u32[]{:S(2)}) copy-start(f32[4,8,4]{2,1,0:T(8,128)} %copy-done.18) | copy-start | bytes 1540
  795.0 218.8 %copy-start.37 = (pred[4]{0:T(512)(128)(4,1)S(1)}, pred[4]{0:T(512)(128)(4,1)}, u32[]{:S(2)}) copy-start(pred[4]{0:T(512)(128)(4,1)} %copy-done.36) | copy-start | bytes 16
  795.0 219.3 %copy-start.43 = (bf16[2048,32]{0,1:T(8,128)(2,1)S(1)}, bf16[2048,32]{0,1:T(8,128)(2,1)}, u32[]{:S(2)}) copy-start(bf16[2048,32]{0,1:T(8,128)(2,1)} %param.44) | copy-start | bytes 393220
  1012.4 260.6 %copy-start.22 = (f32[4,8,4]{1,2,0:T(4,128)S(1)}, f32[4,8,4]{1,2,0:T(4,128)}, u32[]{:S(2)}) copy-start(f32[4,8,4]{1,2,0:T(4,128)} %copy.237) | copy-start | bytes 1540
  1012.5 260.6 %copy-start.23 = (f32[4,8,4]{1,2,0:T(4,128)S(1)}, f32[4,8,4]{1,2,0:T(4,128)}, u32[]{:S(2)}) copy-start(f32[4,8,4]{1,2,0:T(4,128)} %copy.243) | copy-start | bytes 1540
  1012.5 261.0 %copy-start.9 = (f32[4,8,4,1,4]{4,2,1,0,3:T(4,128)S(1)}, f32[4,8,4,1,4]{4,2,1,0,3:T(4,128)}, u32[]{:S(2)}) copy-start(f32[4,8,4,1,4]{4,2,1,0,3:T(4,128)} %copy-done.8) | copy-start | bytes 6148
  1012.5 261.0 %copy-start.35 = (pred[4]{0:T(512)(128)(4,1)S(1)}, pred[4]{0:T(512)(128)(4,1)}, u32[]{:S(2)}) copy-start(pred[4]{0:T(512)(128)(4,1)} %copy-done.34) | copy-start | bytes 16
  1013.8 302.2 %copy-start.32 = (f32[2048]{0:T(1024)S(1)}, f32[2048]{0:T(1024)}, u32[]{:S(2)}) copy-start(f32[2048]{0:T(1024)} %convert_element_type.368) | copy-start | bytes 24580
  1014.1 301.9 %copy-start.1 = (bf16[2048,128]{1,0:T(8,128)(2,1)S(1)}, bf16[2048,128]{1,0:T(8,128)(2,1)}, u32[]{:S(2)}) copy-start(bf16[2048,128]{1,0:T(8,128)(2,1)} %param.45) | copy-start | bytes 1572868
  1057.5 259.0 %copy-start.2 = (bf16[2048,128]{1,0:T(8,128)(2,1)S(1)}, bf16[2048,128]{1,0:T(8,128)(2,1)}, u32[]{:S(2)}) copy-start(bf16[2048,128]{1,0:T(8,128)(2,1)} %param.46) | copy-start | bytes 1572868
  (17 other events, 2223.9 us)
Sparse Core Ops, SparseCore 0:
  256.3 81.2 all-gather.38
  340.9 82.0 all-gather.36
  426.4 82.1 all-gather.34
  511.9 81.9 all-gather.32
  1320.8 181.6 all-reduce.4
where the time goes:
time: 1540 us; the launch traced here: 1510 us
  blocking collectives  783 us (51%)
  local copies, waits for them, and re-layouts  298 us (19%)
  other arithmetic  208 us (14%)
  waiting for transfers between devices  182 us (12%)
    all_gather x8, blocking collectives, joined(): gathered = jax.tree.map(lambda a: lax.all_gather(a, axis), part)  389 us
    dynamic_slice x256, local copies, waits for them, and re-layouts, take(): lax.dynamic_index_in_dim(a, source, 0, False)  216 us
    psum x1, waiting for transfers between devices, shards(): down = lax.psum(down_part, 'seq')  182 us
    all_gather x4, blocking collectives, shards(): projected = lax.all_gather(proj_cols, 'seq', axis=2, tiled=True)  168 us
    all_gather x4, blocking collectives, shards(): qkv_all = lax.all_gather(qkv_cols, 'seq', axis=2, tiled=True)  168 us
    mul x252, other arithmetic, pair_merge(): scale_second[..., None] * out_second  139 us
    add x252, other arithmetic, pair_merge(): scale_first[..., None] * out_first + scale_second[..., None] * out_second  58.9 us
    all_gather x1, blocking collectives, shards(): whole = lax.all_gather(picked, 'seq', axis=0, tiled=True)  58.3 us
  transfers between devices with their start and end apart: 5, of which 1 were waited for; matrix products, arithmetic and copies ran while one was open for 24% of the time, Pallas kernels for 0%

commit v1 on v0

v1 whole, which is shorter than its diff:
```python
import jax
import jax.numpy as jnp
from jax import lax
from jax.sharding import PartitionSpec as P

H = 32
KVH = 8
HD = 64
STEPS = 4


norm_epsilon = 1e-05
embed_factor = 12.0
score_factor = 0.015625
branch_factor = 0.22
rope_base = 10000000.0
masked_floor = -1e30


def rms_scale(resid, gain):
    mean_square = jnp.mean(resid * resid, axis=-1, keepdims=True)
    return resid * lax.rsqrt(mean_square + norm_epsilon) * gain.astype(jnp.float32)


def rotate(vectors, where):
    half = vectors.shape[-1] // 2
    freqs = rope_base ** (-2.0 * jnp.arange(half, dtype=jnp.float32) / vectors.shape[-1])
    angle = where[..., None] * freqs
    cosine = jnp.cos(angle)
    sine = jnp.sin(angle)
    first_half = vectors[..., :half]
    second_half = vectors[..., half:]
    return jnp.concatenate(
        [first_half * cosine - second_half * sine, second_half * cosine + first_half * sine],
        axis=-1,
    )


def partial_softmax(queries, keys, values, valid):
    scores = (
        jnp.einsum("rskgd,rpkd->rskgp", queries, keys, preferred_element_type=jnp.float32)
        * score_factor
    )
    maxima = jnp.max(jnp.where(valid, scores, masked_floor), axis=-1)
    expo = jnp.exp(jnp.where(valid, scores - maxima[..., None], masked_floor))
    totals = jnp.sum(expo, axis=-1)
    outputs = jnp.einsum(
        "rskgp,rpkd->rskgd", expo.astype(jnp.bfloat16), values, preferred_element_type=jnp.float32
    )
    return (maxima, totals, outputs)


def shards(
    token_ids,
    cache_lengths,
    embed_table,
    key_cache,
    value_cache,
    norm_attn,
    norm_mlp,
    w_qkv,
    w_out,
    w_gate,
    w_up,
    w_down,
):
    place = lax.axis_index("seq")
    req_all = token_ids.shape[0]
    steps = token_ids.shape[1]
    ctx_own = key_cache.shape[1]
    att_width = H * HD
    kv_width = KVH * HD
    group = H // KVH
    picked = jnp.take(embed_table, token_ids.reshape(-1), axis=1)
    whole = lax.all_gather(picked, "seq", axis=0, tiled=True)
    resid = jnp.transpose(whole, (1, 0)).reshape(req_all, steps, -1).astype(jnp.float32) * embed_factor
    slot_pos = place * ctx_own + jnp.arange(ctx_own, dtype=jnp.int32)
    cache_valid = (slot_pos[None, :] < cache_lengths[:, None]).reshape(req_all, 1, 1, 1, ctx_own)
    cache_keys = key_cache.reshape(req_all, ctx_own, KVH, HD)
    cache_values = value_cache.reshape(req_all, ctx_own, KVH, HD)

    normed = rms_scale(resid, norm_attn).astype(jnp.bfloat16)
    qkv_cols = jnp.einsum(
        "rsd,dc->rsc", normed, w_qkv, preferred_element_type=jnp.float32
    ).astype(jnp.bfloat16)
    qkv_all = lax.all_gather(qkv_cols, "seq", axis=2, tiled=True)
    where = (cache_lengths[:, None] + jnp.arange(steps, dtype=jnp.int32)[None, :]).astype(
        jnp.float32
    )
    queries = rotate(
        qkv_all[..., :att_width].reshape(req_all, steps, H, HD).astype(jnp.float32),
        where[..., None],
    ).astype(jnp.bfloat16)
    keys_new = rotate(
        qkv_all[..., att_width : att_width + kv_width]
        .reshape(req_all, steps, KVH, HD)
        .astype(jnp.float32),
        where[..., None],
    ).astype(jnp.bfloat16)
    values_new = qkv_all[..., att_width + kv_width :].reshape(req_all, steps, KVH, HD)
    grouped = queries.reshape(req_all, steps, KVH, group, HD)
    cache_max, cache_total, cache_out = partial_softmax(
        grouped, cache_keys, cache_values, cache_valid
    )
    fresh_valid = (
        jnp.arange(steps, dtype=jnp.int32)[None, :] <= jnp.arange(steps, dtype=jnp.int32)[:, None]
    ).reshape(1, steps, 1, 1, steps)
    fresh_max, fresh_total, fresh_out = partial_softmax(grouped, keys_new, values_new, fresh_valid)

    overall = jnp.maximum(lax.pmax(cache_max, "seq"), fresh_max)
    cache_scale = jnp.exp(cache_max - overall)
    packed = jnp.concatenate(
        [cache_scale[..., None] * cache_out, (cache_scale * cache_total)[..., None]], axis=-1
    )
    summed = lax.psum(packed, "seq")
    fresh_scale = jnp.exp(fresh_max - overall)
    numer = summed[..., :HD] + fresh_scale[..., None] * fresh_out
    denom = summed[..., HD] + fresh_scale * fresh_total
    attention = (numer / denom[..., None]).astype(jnp.bfloat16).reshape(req_all, steps, att_width)

    proj_cols = jnp.einsum(
        "rsa,ac->rsc", attention, w_out, preferred_element_type=jnp.float32
    ).astype(jnp.bfloat16)
    projected = lax.all_gather(proj_cols, "seq", axis=2, tiled=True)
    middle = resid + branch_factor * projected.astype(jnp.float32)
    normed_mlp = rms_scale(middle, norm_mlp).astype(jnp.bfloat16)
    gate = jnp.einsum("rsd,df->rsf", normed_mlp, w_gate, preferred_element_type=jnp.float32)
    upward = jnp.einsum("rsd,df->rsf", normed_mlp, w_up, preferred_element_type=jnp.float32)
    hidden = (jax.nn.silu(gate) * upward).astype(jnp.bfloat16)
    down_part = jnp.einsum("rsf,fd->rsd", hidden, w_down, preferred_element_type=jnp.float32)
    down = lax.psum(down_part, "seq")
    return (middle + branch_factor * down).astype(jnp.bfloat16)


def solution(mesh):
    return jax.shard_map(
        shards,
        mesh=mesh,
        in_specs=(
            P("rep", None),
            P("rep"),
            P("seq", None),
            P("rep", "seq", None),
            P("rep", "seq", None),
            P(),
            P(),
            P(None, "seq"),
            P(None, "seq"),
            P(None, "seq"),
            P(None, "seq"),
            P("seq", None),
        ),
        out_specs=P("rep", None, None),
        check_vma=False,
    )
```

time: 1540 us -> 812 us (0.53); the launches traced: 1510 us -> 812 us
  blocking collectives: 783 us -> 394 us
  local copies, waits for them, and re-layouts: 298 us -> 24.9 us
  other arithmetic: 208 us -> 4.51 us
  waiting for transfers between devices: 182 us -> 368 us
    all_gather x8 -> x0, blocking collectives: 389 us -> none  [joined(): gathered = jax.tree.map(lambda a: lax.all_gather(a, axis), part)]
    pmax x0 -> x1, blocking collectives: none -> 243 us  [shards(): overall = jnp.maximum(lax.pmax(cache_max, 'seq'), fresh_max)]
    dynamic_slice x256 -> x0, local copies, waits for them, and re-layouts: 216 us -> none  [take(): lax.dynamic_index_in_dim(a, source, 0, False)]
    psum x0 -> x1, waiting for transfers between devices: none -> 185 us  [shards(): summed = lax.psum(packed, 'seq')]
    mul x513 -> x1, other arithmetic: 143 us -> 0.01 us  [rms_scale(): resid * lax.rsqrt(mean_square + norm_epsilon) * gain.astype(jnp.float32)]
    all_gather x4 -> x1, blocking collectives: 168 us -> 48.3 us  [shards(): projected = lax.all_gather(proj_cols, 'seq', axis=2, tiled=True)]
    all_gather x4 -> x1, blocking collectives: 168 us -> 51.1 us  [shards(): qkv_all = lax.all_gather(qkv_cols, 'seq', axis=2, tiled=True)]
    add x252 -> x1, other arithmetic: 58.9 us -> 0.05 us  [shards(): denom = summed[..., HD] + fresh_scale * fresh_total]
  transfers between devices with their start and end apart: 5 -> 2, of which waited for: 1 -> 2; matrix products, arithmetic and copies ran while one was open for 24% -> 0% of each run, Pallas kernels for 0% -> 0%
where the time goes in v1:
time: 812 us
  blocking collectives  394 us (49%)
  waiting for transfers between devices  368 us (45%)
  local copies, waits for them, and re-layouts  24.9 us (3%)
  between operations  13.7 us (2%)
    pmax x1, blocking collectives, shards(): overall = jnp.maximum(lax.pmax(cache_max, 'seq'), fresh_max)  243 us
    psum x1, waiting for transfers between devices, shards(): summed = lax.psum(packed, 'seq')  185 us
    psum x1, waiting for transfers between devices, shards(): down = lax.psum(down_part, 'seq')  182 us
    all_gather x1, blocking collectives, shards(): whole = lax.all_gather(picked, 'seq', axis=0, tiled=True)  51.6 us
    all_gather x1, blocking collectives, shards(): qkv_all = lax.all_gather(qkv_cols, 'seq', axis=2, tiled=True)  51.1 us
    all_gather x1, blocking collectives, shards(): projected = lax.all_gather(proj_cols, 'seq', axis=2, tiled=True)  48.3 us
  transfers between devices with their start and end apart: 2, of which 2 were waited for; matrix products, arithmetic and copies ran while one was open for 0% of the time, Pallas kernels for 0%

profile of v1, /device:TPU:1, one launch (start us, length us, event | category | flops | bytes accessed | tf_op | source)
XLA Modules:
  0.0 811.6 jit_solution(16249509916441426397)
XLA Ops:
  6.5 0.8 reshape.176
  7.4 0.8 reshape.175
  8.2 6.4 copy.89
  14.6 4.2 gather_fusion
  18.9 51.6 %all-gather = bf16[64,32,16]{1,2,0:T(8,128)(2,1)S(1)} all-gather(bf16[1,32,16]{1,2,0:T(8,128)(2,1)S(1)} %select_bitcast_fusion), channel_id=1, replica_groups=mesh['seq'=64,'rep'=8] {'seq'}, dimensions={0}, use_global_device_ids=true | all-gather | bytes 66560 | tf_op jit(solution)/shard_map/all_gather | solution.py:75
  70.4 0.3 copy.90
  71.9 51.1 %all_gather.10 = bf16[4,4,3072]{1,0,2:T(4,128)(2,1)S(1)} all-gather(bf16[4,4,48]{1,0,2:T(4,128)(2,1)S(1)} %copy.92), channel_id=1, replica_groups=mesh['seq'=64,'rep'=8] {'seq'}, dimensions={2}, use_global_device_ids=true | all-gather | bytes 99840 | tf_op jit(solution)/shard_map/all_gather | solution.py:86
  123.0 0.7 slice.38
  123.8 1.2 fusion.44
  124.9 2.2 copy.124
  127.1 1.0 reshape.182
  128.2 0.3 copy.125
  128.8 1.3 copy.96
  130.6 0.4 select_reduce_fusion.1
  131.0 243.2 %pmax.7 = f32[4,4,8,4]{3,1,2,0:T(4,128)S(1)} all-reduce(f32[4,4,8,4]{3,1,2,0:T(4,128)S(1)} %get-tuple-element.19), channel_id=1, replica_groups=mesh['seq'=64,'rep'=8] {'seq'}, use_global_device_ids=true, to_apply=%region_2.3 | all-reduce | flops 512 | bytes 4096 | tf_op jit(solution)/shard_map/pmax | solution.py:110
  374.2 0.4 fusion.16
  374.7 0.3 copy.100
  375.0 1.3 select_reduce_fusion
  376.4 0.9 copy.102
  377.3 0.5 fusion.1
  377.7 0.9 pad_maximum_fusion
  378.9 0.4 fusion.18
  379.3 185.2 %all-reduce.3.cloned.1.call-done = f32[4,4,8,4,65]{4,3,1,2,0:T(4,128)} async-done(((f32[4,4,8,4,65]{4,3,1,2,0:T(4,128)}), f32[4,4,8,4,65]{4,3,1,2,0:T(4,128)}) %all-reduce.3.cloned.1.call-update) | async-done | bytes 133136 | tf_op jit(solution)/shard_map/psum | solution.py:115
  564.5 1.1 slice.46
  565.7 0.9 copy.123
  566.6 1.6 fusion.6
  568.7 48.3 %all_gather.11 = bf16[4,4,2048]{1,0,2:T(4,128)(2,1)S(1)} all-gather(bf16[4,4,32]{1,0,2:T(4,128)(2,1)S(1)} %copy.109), channel_id=1, replica_groups=mesh['seq'=64,'rep'=8] {'seq'}, dimensions={2}, use_global_device_ids=true | all-gather | bytes 66560 | tf_op jit(solution)/shard_map/all_gather | solution.py:124
  617.0 1.3 copy.110
  618.5 1.3 fusion.12
  619.8 1.1 fusion.8
  620.9 182.2 %all-reduce.5.cloned.1.call-done = f32[4,4,2048]{2,1,0:T(4,128)} async-done(((f32[4,4,2048]{2,1,0:T(4,128)}), f32[4,4,2048]{2,1,0:T(4,128)}) %all-reduce.5.cloned.1.call-update) | async-done | bytes 131088 | tf_op jit(solution)/shard_map/psum | solution.py:131
  803.2 1.6 add_convert_fusion.1
  (55 shorter events, 3.1 us)
Async XLA Ops:
  6.5 613.2 %copy-start = (bf16[128,2048]{1,0:T(8,128)(2,1)S(1)}, bf16[128,2048]{1,0:T(8,128)(2,1)}, u32[]{:S(2)}) copy-start(bf16[128,2048]{1,0:T(8,128)(2,1)} %param.23) | copy-start | bytes 1572868
  6.5 558.0 %all-reduce.3.cloned.1.call-start = ((), (), s32[]{:S(2)}) async-start(), calls=%async_computation | async-start | bytes 524288 | tf_op jit(solution)/shard_map/psum | solution.py:115
  8.1 63.3 %copy-start.4 = (bf16[2048]{0:T(1024)(128)(2,1)S(1)}, bf16[2048]{0:T(1024)(128)(2,1)}, u32[]{:S(2)}) copy-start(bf16[2048]{0:T(1024)(128)(2,1)} %param.17) | copy-start | bytes 12292
  8.1 63.3 %copy-start.7 = (bf16[2048,48]{0,1:T(8,128)(2,1)S(1)}, bf16[2048,48]{0,1:T(8,128)(2,1)}, u32[]{:S(2)}) copy-start(bf16[2048,48]{0,1:T(8,128)(2,1)} %param.19) | copy-start | bytes 589828
  123.8 4.4 copy-start.6
  127.1 247.6 %copy-start.1 = (bf16[4,128,512]{2,1,0:T(8,128)(2,1)S(1)}, bf16[4,128,512]{2,1,0:T(8,128)(2,1)}, u32[]{:S(2)}) copy-start(bf16[4,128,512]{2,1,0:T(8,128)(2,1)} %param.16) | copy-start | bytes 1572868
  376.3 3.0 copy-start.5
  377.3 189.3 %copy-start.3 = (bf16[4,4,512]{1,0,2:T(4,128)(2,1)S(1)}, bf16[4,4,512]{1,0,2:T(4,128)(2,1)}, u32[]{:S(2)}) copy-start(bf16[4,4,512]{1,0,2:T(4,128)(2,1)} %get-tuple-element.10) | copy-start | bytes 49156
  378.7 424.5 %all-reduce.5.cloned.1.call-start = ((), (), s32[]{:S(2)}) async-start(), calls=%async_computation.1 | async-start | bytes 262144 | tf_op jit(solution)/shard_map/psum | solution.py:131
  379.3 189.1 %copy-start.8 = (bf16[2048,32]{0,1:T(8,128)(2,1)S(1)}, bf16[2048,32]{0,1:T(8,128)(2,1)}, u32[]{:S(2)}) copy-start(bf16[2048,32]{0,1:T(8,128)(2,1)} %param.20) | copy-start | bytes 393220
  568.2 51.6 %copy-start.2 = (bf16[2048,128]{1,0:T(8,128)(2,1)S(1)}, bf16[2048,128]{1,0:T(8,128)(2,1)}, u32[]{:S(2)}) copy-start(bf16[2048,128]{1,0:T(8,128)(2,1)} %param.22) | copy-start | bytes 1572868
Sparse Core Ops, SparseCore 0:
  378.8 185.6 all-reduce.2
  621.0 182.0 all-reduce.4

commit v2 on v1

--- a/solution.py
+++ b/solution.py
@@ -1,14 +1,98 @@
+import functools
+
 import jax
 import jax.numpy as jnp
 from jax import lax
+from jax.experimental import pallas as pl
+from jax.experimental.pallas import tpu as pltpu
 from jax.sharding import PartitionSpec as P
 
 H = 32
 KVH = 8
 HD = 64
+
+MESH_ID = pl.DeviceIdType.MESH
+
+
+def _exchange_kernel(n, gather, x_ref, o_ref, buf, send_sems, recv_sems, local_sem):
+    me = lax.axis_index("seq")
+    rep = lax.axis_index("rep")
+    barrier = pltpu.get_barrier_semaphore()
+
+    def greet(k, carry):
+        peer = lax.rem(me + k, n)
+        pl.semaphore_signal(barrier, inc=1, device_id=(peer, rep), device_id_type=MESH_ID)
+        return carry
+
+    lax.fori_loop(1, n, greet, 0)
+    pl.semaphore_wait(barrier, n - 1)
+
+    def source(peer):
+        return x_ref if gather else x_ref.at[peer]
+
+    def outgoing(peer):
+        return pltpu.make_async_remote_copy(
+            src_ref=source(peer),
+            dst_ref=buf.at[me],
+            send_sem=send_sems.at[peer],
+            recv_sem=recv_sems.at[me],
+            device_id=(peer, rep),
+            device_id_type=MESH_ID,
+        )
+
+    def incoming(peer):
+        return pltpu.make_async_remote_copy(
+            src_ref=source(peer),
+            dst_ref=buf.at[peer],
+            send_sem=send_sems.at[peer],
+            recv_sem=recv_sems.at[peer],
+            device_id=(peer, rep),
+            device_id_type=MESH_ID,
+        )
+
+    def send(k, carry):
+        outgoing(lax.rem(me + k, n)).start()
+        return carry
+
+    lax.fori_loop(1, n, send, 0)
+    local = pltpu.make_async_copy(source(me), buf.at[me], local_sem)
+    local.start()
+
+    def finish(k, carry):
+        peer = lax.rem(me + k, n)
+        outgoing(peer).wait_send()
+        incoming(peer).wait_recv()
+        return carry
+
+    lax.fori_loop(1, n, finish, 0)
+    local.wait()
+    o_ref[...] = buf[...]
+
+
+def exchange(x, n, gather, cid):
+    blk = x.shape if gather else x.shape[1:]
+    shape = (n,) + tuple(blk)
+    nbytes = int(jnp.dtype(x.dtype).itemsize) * n
+    for d in blk:
+        nbytes *= int(d)
+    return pl.pallas_call(
+        functools.partial(_exchange_kernel, n, gather),
+        out_shape=jax.ShapeDtypeStruct(shape, x.dtype),
+        in_specs=[pl.BlockSpec(memory_space=pltpu.VMEM)],
+        out_specs=pl.BlockSpec(memory_space=pltpu.VMEM),
+        scratch_shapes=[
+            pltpu.VMEM(shape, x.dtype),
+            pltpu.SemaphoreType.DMA((n,)),
+            pltpu.SemaphoreType.DMA((n,)),
+            pltpu.SemaphoreType.DMA(()),
+        ],
+        compiler_params=pltpu.CompilerParams(collective_id=cid, has_side_effects=True),
+        cost_estimate=pl.CostEstimate(flops=0, transcendentals=0, bytes_accessed=2 * nbytes),
+        name="exchange_%d" % cid,
+    )(x)
+
+
 STEPS = 4
-
-
 norm_epsilon = 1e-05
 embed_factor = 12.0
 score_factor = 0.015625
@@ -64,26 +148,30 @@
     w_up,
     w_down,
 ):
+    n = lax.axis_size("seq")
     place = lax.axis_index("seq")
     req_all = token_ids.shape[0]
     steps = token_ids.shape[1]
+    rows = req_all * steps
     ctx_own = key_cache.shape[1]
+    width = embed_table.shape[0] * n
     att_width = H * HD
     kv_width = KVH * HD
     group = H // KVH
+
     picked = jnp.take(embed_table, token_ids.reshape(-1), axis=1)
-    whole = lax.all_gather(picked, "seq", axis=0, tiled=True)
-    resid = jnp.transpose(whole, (1, 0)).reshape(req_all, steps, -1).astype(jnp.float32) * embed_factor
+    whole = exchange(jnp.transpose(picked, (1, 0)), n, True, 0)
+    resid = jnp.transpose(whole, (1, 0, 2)).reshape(rows, width).astype(jnp.float32) * embed_factor
+
     slot_pos = place * ctx_own + jnp.arange(ctx_own, dtype=jnp.int32)
     cache_valid = (slot_pos[None, :] < cache_lengths[:, None]).reshape(req_all, 1, 1, 1, ctx_own)
     cache_keys = key_cache.reshape(req_all, ctx_own, KVH, HD)
     cache_values = value_cache.reshape(req_all, ctx_own, KVH, HD)
 
     normed = rms_scale(resid, norm_attn).astype(jnp.bfloat16)
-    qkv_cols = jnp.einsum(
-        "rsd,dc->rsc", normed, w_qkv, preferred_element_type=jnp.float32
-    ).astype(jnp.bfloat16)
-    qkv_all = lax.all_gather(qkv_cols, "seq", axis=2, tiled=True)
+    qkv_cols = jnp.dot(normed, w_qkv, preferred_element_type=jnp.float32).astype(jnp.bfloat16)
+    qkv_got = exchange(qkv_cols, n, True, 1)
+    qkv_all = jnp.transpose(qkv_got, (1, 0, 2)).reshape(req_all, steps, -1)
     where = (cache_lengths[:, None] + jnp.arange(steps, dtype=jnp.int32)[None, :]).astype(
         jnp.float32
     )
@@ -107,29 +195,48 @@
     ).reshape(1, steps, 1, 1, steps)
     fresh_max, fresh_total, fresh_out = partial_softmax(grouped, keys_new, values_new, fresh_valid)
 
-    overall = jnp.maximum(lax.pmax(cache_max, "seq"), fresh_max)
-    cache_scale = jnp.exp(cache_max - overall)
+    pairs = rows * H // n
+    lanes = 128
     packed = jnp.concatenate(
-        [cache_scale[..., None] * cache_out, (cache_scale * cache_total)[..., None]], axis=-1
-    )
-    summed = lax.psum(packed, "seq")
-    fresh_scale = jnp.exp(fresh_max - overall)
-    numer = summed[..., :HD] + fresh_scale[..., None] * fresh_out
-    denom = summed[..., HD] + fresh_scale * fresh_total
-    attention = (numer / denom[..., None]).astype(jnp.bfloat16).reshape(req_all, steps, att_width)
-
-    proj_cols = jnp.einsum(
-        "rsa,ac->rsc", attention, w_out, preferred_element_type=jnp.float32
-    ).astype(jnp.bfloat16)
-    projected = lax.all_gather(proj_cols, "seq", axis=2, tiled=True)
+        [
+            cache_out.reshape(n, pairs, HD),
+            cache_max.reshape(n, pairs, 1),
+            cache_total.reshape(n, pairs, 1),
+            jnp.zeros((n, pairs, lanes - HD - 2), jnp.float32),
+        ],
+        axis=-1,
+    )
+    got = exchange(packed, n, False, 2)
+    block_max = got[:, :, HD]
+    block_total = got[:, :, HD + 1]
+    block_out = got[:, :, :HD]
+    own_fresh_max = lax.dynamic_index_in_dim(fresh_max.reshape(n, pairs), place, 0, False)
+    own_fresh_total = lax.dynamic_index_in_dim(fresh_total.reshape(n, pairs), place, 0, False)
+    own_fresh_out = lax.dynamic_index_in_dim(fresh_out.reshape(n, pairs, HD), place, 0, False)
+    overall = jnp.maximum(jnp.max(block_max, axis=0), own_fresh_max)
+    block_scale = jnp.exp(block_max - overall[None, :])
+    fresh_scale = jnp.exp(own_fresh_max - overall)
+    numer = jnp.sum(block_scale[..., None] * block_out, axis=0) + fresh_scale[:, None] * own_fresh_out
+    denom = jnp.sum(block_scale * block_total, axis=0) + fresh_scale * own_fresh_total
+    attention_own = (numer / denom[:, None]).astype(jnp.bfloat16).reshape(1, pairs * HD)
+    attention = exchange(attention_own, n, True, 3).reshape(rows, att_width)
+
+    proj_cols = jnp.dot(attention, w_out, preferred_element_type=jnp.float32).astype(jnp.bfloat16)
+    proj_got = exchange(proj_cols, n, True, 4)
+    projected = jnp.transpose(proj_got, (1, 0, 2)).reshape(rows, width)
     middle = resid + branch_factor * projected.astype(jnp.float32)
     normed_mlp = rms_scale(middle, norm_mlp).astype(jnp.bfloat16)
-    gate = jnp.einsum("rsd,df->rsf", normed_mlp, w_gate, preferred_element_type=jnp.float32)
-    upward = jnp.einsum("rsd,df->rsf", normed_mlp, w_up, preferred_element_type=jnp.float32)
+    gate = jnp.dot(normed_mlp, w_gate, preferred_element_type=jnp.float32)
+    upward = jnp.dot(normed_mlp, w_up, preferred_element_type=jnp.float32)
     hidden = (jax.nn.silu(gate) * upward).astype(jnp.bfloat16)
-    down_part = jnp.einsum("rsf,fd->rsd", hidden, w_down, preferred_element_type=jnp.float32)
-    down = lax.psum(down_part, "seq")
-    return (middle + branch_factor * down).astype(jnp.bfloat16)
+    down_part = jnp.dot(hidden, w_down, preferred_element_type=jnp.float32)
+    cols = width // n
+    down_got = exchange(jnp.transpose(down_part.reshape(rows, n, cols), (1, 0, 2)), n, False, 5)
+    down_own = jnp.sum(down_got, axis=0)
+    middle_own = lax.dynamic_slice_in_dim(middle, place * cols, cols, axis=1)
+    out_own = (middle_own + branch_factor * down_own).astype(jnp.bfloat16)
+    out_got = exchange(out_own, n, True, 6)
+    return jnp.transpose(out_got, (1, 0, 2)).reshape(req_all, steps, width)
 
 
 def solution(mesh):

time: 812 us -> 178 us (0.22)
  blocking collectives: 394 us -> 0 us
  waiting for transfers between devices: 368 us -> 0 us
  Pallas kernels: 0 us -> 139 us
  between operations: 13.7 us -> 0.46 us
  other arithmetic: 4.51 us -> 13.9 us
    psum x2 -> x0, waiting for transfers between devices: 367 us -> none  [the longest x1 185 us: shards(): summed = lax.psum(packed, 'seq')]
    pmax x1 -> x0, blocking collectives: 243 us -> none  [shards(): overall = jnp.maximum(lax.pmax(cache_max, 'seq'), fresh_max)]
    all_gather x3 -> x0, blocking collectives: 151 us -> none  [the longest x1 51.6 us: shards(): whole = lax.all_gather(picked, 'seq', axis=0, tiled=True)]
    pallas_call x0 -> x7, Pallas kernels: none -> 139 us  [exchange(): pl.pallas_call(functools.partial(_exchange_kernel, n, gather), out_shape=...]
  transfers between devices with their start and end apart: 2 -> 0, of which waited for: 2 -> 0; matrix products, arithmetic and copies ran while one was open for 0% -> 0% of each run, Pallas kernels for 0% -> 0%
where the time goes in v2:
time: 178 us
  Pallas kernels  139 us (78%)
  local copies, waits for them, and re-layouts  19.1 us (11%)
  other arithmetic  13.9 us (8%)
  matrix products  4.74 us (3%)
    pallas_call x7, Pallas kernels, exchange(): pl.pallas_call(functools.partial(_exchange_kernel, n, gather), out_shape=...  139 us
    unnamed x27, local copies, waits for them, and re-layouts  7.04 us
    gather x1, local copies, waits for them, and re-layouts, shards(): picked = jnp.take(embed_table, token_ids.reshape(-1), axis=1)  4.24 us

profile of v2, /device:TPU:1, one launch (start us, length us, event | category | flops | bytes accessed | tf_op | source)
XLA Modules:
  0.0 177.5 jit_solution(5336541251856998406)
XLA Ops:
  0.0 6.4 %copy.95 = bf16[32,24704]{0,1:T(8,128)(2,1)} copy(bf16[32,24704]{1,0:T(8,128)(2,1)} %param.14) | data formatting | bytes 3162112 | tf_op args[2]
  6.6 4.2 %gather_fusion = bf16[16,32]{1,0:T(8,128)(2,1)S(1)} fusion(bf16[32,24704]{0,1:T(8,128)(2,1)} %copy.95, s32[1024]{0:T(1024)S(1)} %pad_clamp_fusion), kind=kCustom, calls=%fused_computation | custom fusion | bytes 2112 | tf_op jit(solution)/shard_map/jit(_take)/gather | solution.py:162
  10.9 0.7 broadcast_select_fusion.x_ref
  11.6 26.0 %exchange_0.1 = bf16[64,16,32]{2,1,0:T(8,128)(2,1)} custom-call(bf16[16,32]{1,0:T(8,128)(2,1)} %broadcast_select_fusion.x_ref), custom_call_target="tpu_custom_call" | custom-call | bytes 131072 | tf_op jit(solution)/shard_map/exchange_0/pallas_call | solution.py:78
  37.6 1.0 convert_bitcast_fusion
  39.0 1.2 fusion.6
  40.2 0.8 convolution_convert_fusion.1.x_ref
  41.1 17.6 %exchange_1.1 = bf16[64,16,48]{2,1,0:T(8,128)(2,1)} custom-call(bf16[16,48]{1,0:T(8,128)(2,1)} %convolution_convert_fusion.1.x_ref), custom_call_target="tpu_custom_call" | custom-call | bytes 196608 | tf_op jit(solution)/shard_map/exchange_1/pallas_call | solution.py:78
  58.7 1.0 copy.97
  61.1 1.3 select_reduce_fusion
  64.1 0.5 convolution_bitcast_fusion
  64.6 0.4 fusion.10
  65.4 0.9 maximum_maximum_fusion.x_ref
  66.3 18.8 %exchange_2.1 = f32[64,8,128]{2,1,0:T(8,128)} custom-call(f32[64,8,128]{2,1,0:T(8,128)} %maximum_maximum_fusion.x_ref), custom_call_target="tpu_custom_call" | custom-call | bytes 524288 | tf_op jit(solution)/shard_map/exchange_2/pallas_call | solution.py:78
  85.1 1.2 slice_reduce_fusion
  86.4 1.2 subtract_exponential_fusion
  87.7 0.4 copy.128
  88.1 1.1 multiply_reduce_fusion
  90.6 0.6 fusion.37.x_ref
  91.2 15.7 %exchange_3.1 = bf16[64,1,512]{2,1,0:T(2,128)(2,1)} custom-call(bf16[1,512]{1,0:T(2,128)(2,1)} %fusion.37.x_ref), custom_call_target="tpu_custom_call" | custom-call | bytes 131072 | tf_op jit(solution)/shard_map/exchange_3/pallas_call | solution.py:78
  106.9 1.3 reduce.5
  108.2 0.8 convolution_convert_fusion.x_ref
  108.9 18.2 %exchange_4.1 = bf16[64,16,32]{2,1,0:T(8,128)(2,1)} custom-call(bf16[16,32]{1,0:T(8,128)(2,1)} %convolution_convert_fusion.x_ref), custom_call_target="tpu_custom_call" | custom-call | bytes 131072 | tf_op jit(solution)/shard_map/exchange_4/pallas_call | solution.py:78
  127.2 1.2 fusion.8
  129.1 0.4 fusion.3
  129.7 1.1 copy.148
  130.8 24.3 %exchange_5.1 = f32[64,16,32]{2,1,0:T(8,128)} custom-call(f32[64,16,32]{2,1,0:T(8,128)} %bitcast.84), custom_call_target="tpu_custom_call" | custom-call | bytes 262144 | tf_op jit(solution)/shard_map/exchange_5/pallas_call | solution.py:78
  155.1 1.1 reduce_sum.72
  156.2 0.7 add_convert_fusion.2.x_ref
  156.9 18.7 %exchange_6.1 = bf16[64,16,32]{2,1,0:T(8,128)(2,1)} custom-call(bf16[16,32]{1,0:T(8,128)(2,1)} %add_convert_fusion.2.x_ref), custom_call_target="tpu_custom_call" | custom-call | bytes 131072 | tf_op jit(solution)/shard_map/exchange_6/pallas_call | solution.py:78
  175.6 1.0 copy.121
  176.6 0.9 reshape.286
  (86 shorter events, 6.3 us)
Async XLA Ops:
  0.0 129.1 %copy-start = (bf16[128,2048]{1,0:T(8,128)(2,1)S(1)}, bf16[128,2048]{1,0:T(8,128)(2,1)}, u32[]{:S(2)}) copy-start(bf16[128,2048]{1,0:T(8,128)(2,1)} %param.23) | copy-start | bytes 1572868
  0.0 6.5 %copy-start.8 = (s32[4,4]{1,0:T(4,128)S(1)}, s32[4,4]{1,0:T(4,128)}, u32[]{:S(2)}) copy-start(s32[4,4]{1,0:T(4,128)} %param.12) | copy-start | bytes 196
  0.0 40.2 %copy-start.9 = (bf16[2048]{0:T(1024)(128)(2,1)S(1)}, bf16[2048]{0:T(1024)(128)(2,1)}, u32[]{:S(2)}) copy-start(bf16[2048]{0:T(1024)(128)(2,1)} %param.17) | copy-start | bytes 12292
  0.0 40.2 %copy-start.6 = (bf16[2048,48]{0,1:T(8,128)(2,1)S(1)}, bf16[2048,48]{0,1:T(8,128)(2,1)}, u32[]{:S(2)}) copy-start(bf16[2048,48]{0,1:T(8,128)(2,1)} %param.19) | copy-start | bytes 589828
  0.0 60.2 %copy-start.11 = (s32[4]{0:T(128)S(1)}, s32[4]{0:T(128)}, u32[]{:S(2)}) copy-start(s32[4]{0:T(128)} %param.13) | copy-start | bytes 52
  6.5 56.7 %copy-start.3 = (bf16[4,128,512]{2,1,0:T(8,128)(2,1)S(1)}, bf16[4,128,512]{2,1,0:T(8,128)(2,1)}, u32[]{:S(2)}) copy-start(bf16[4,128,512]{2,1,0:T(8,128)(2,1)} %param.15) | copy-start | bytes 1572868
  6.5 57.3 %copy-start.4 = (bf16[4,128,512]{2,1,0:T(8,128)(2,1)S(1)}, bf16[4,128,512]{2,1,0:T(8,128)(2,1)}, u32[]{:S(2)}) copy-start(bf16[4,128,512]{2,1,0:T(8,128)(2,1)} %param.16) | copy-start | bytes 1572868
  63.0 45.2 %copy-start.7 = (bf16[2048,32]{0,1:T(8,128)(2,1)S(1)}, bf16[2048,32]{0,1:T(8,128)(2,1)}, u32[]{:S(2)}) copy-start(bf16[2048,32]{0,1:T(8,128)(2,1)} %param.20) | copy-start | bytes 393220
  63.1 64.0 %copy-start.1 = (bf16[64,16,32]{2,1,0:T(8,128)(2,1)S(1)}, bf16[64,16,32]{2,1,0:T(8,128)(2,1)}, u32[]{:S(2)}) copy-start(bf16[64,16,32]{2,1,0:T(8,128)(2,1)} %exchange_0.1) | copy-start | bytes 196612
  64.1 64.8 %copy-start.10 = (bf16[2048]{0:T(1024)(128)(2,1)S(1)}, bf16[2048]{0:T(1024)(128)(2,1)}, u32[]{:S(2)}) copy-start(bf16[2048]{0:T(1024)(128)(2,1)} %param.18) | copy-start | bytes 12292
  64.1 64.8 %copy-start.5 = (bf16[2048,128]{1,0:T(8,128)(2,1)S(1)}, bf16[2048,128]{1,0:T(8,128)(2,1)}, u32[]{:S(2)}) copy-start(bf16[2048,128]{1,0:T(8,128)(2,1)} %param.21) | copy-start | bytes 1572868
  64.6 64.6 %copy-start.2 = (bf16[2048,128]{1,0:T(8,128)(2,1)S(1)}, bf16[2048,128]{1,0:T(8,128)(2,1)}, u32[]{:S(2)}) copy-start(bf16[2048,128]{1,0:T(8,128)(2,1)} %param.22) | copy-start | bytes 1572868

commit v3 on v2

--- a/solution.py
+++ b/solution.py
@@ -14,9 +14,7 @@
 MESH_ID = pl.DeviceIdType.MESH
 
 
-def _exchange_kernel(n, gather, x_ref, o_ref, buf, send_sems, recv_sems, local_sem):
-    me = lax.axis_index("seq")
-    rep = lax.axis_index("rep")
+def _greet(n, me, rep):
     barrier = pltpu.get_barrier_semaphore()
 
     def greet(k, carry):
@@ -27,9 +25,8 @@
     lax.fori_loop(1, n, greet, 0)
     pl.semaphore_wait(barrier, n - 1)
 
-    def source(peer):
-        return x_ref if gather else x_ref.at[peer]
-
+
+def _spread(n, me, rep, source, buf, send_sems, recv_sems, local_sem):
     def outgoing(peer):
         return pltpu.make_async_remote_copy(
             src_ref=source(peer),
@@ -66,15 +63,28 @@
 
     lax.fori_loop(1, n, finish, 0)
     local.wait()
+
+
+def _exchange_kernel(n, gather, x_ref, o_ref, buf, send_sems, recv_sems, local_sem):
+    me = lax.axis_index("seq")
+    rep = lax.axis_index("rep")
+    _greet(n, me, rep)
+    source = (lambda peer: x_ref) if gather else (lambda peer: x_ref.at[peer])
+    _spread(n, me, rep, source, buf, send_sems, recv_sems, local_sem)
     o_ref[...] = buf[...]
+
+
+def _nbytes(shape, dtype):
+    size = int(jnp.dtype(dtype).itemsize)
+    for d in shape:
+        size *= int(d)
+    return size
 
 
 def exchange(x, n, gather, cid):
     blk = x.shape if gather else x.shape[1:]
     shape = (n,) + tuple(blk)
-    nbytes = int(jnp.dtype(x.dtype).itemsize) * n
-    for d in blk:
-        nbytes *= int(d)
+    nbytes = _nbytes(shape, x.dtype)
     return pl.pallas_call(
         functools.partial(_exchange_kernel, n, gather),
         out_shape=jax.ShapeDtypeStruct(shape, x.dtype),
@@ -90,6 +100,64 @@
         cost_estimate=pl.CostEstimate(flops=0, transcendentals=0, bytes_accessed=2 * nbytes),
         name="exchange_%d" % cid,
     )(x)
+
+
+def _two_phase_kernel(n, combine, n_extra, *refs):
+    x_ref = refs[0]
+    extras = refs[1 : 1 + n_extra]
+    o_ref = refs[1 + n_extra]
+    buf1, own, buf2, s1, r1, l1, s2, r2, l2 = refs[2 + n_extra :]
+    me = lax.axis_index("seq")
+    rep = lax.axis_index("rep")
+    _greet(n, me, rep)
+    _spread(n, me, rep, lambda peer: x_ref.at[peer], buf1, s1, r1, l1)
+    own[...] = combine(buf1, *extras)
+    _spread(n, me, rep, lambda peer: own, buf2, s2, r2, l2)
+    o_ref[...] = buf2[...]
+
+
+def two_phase(x, extras, combine, own_shape, own_dtype, n, cid):
+    first = x.shape
+    shape = (n,) + tuple(own_shape)
+    nbytes = _nbytes(first, x.dtype) + _nbytes(shape, own_dtype)
+    return pl.pallas_call(
+        functools.partial(_two_phase_kernel, n, combine, len(extras)),
+        out_shape=jax.ShapeDtypeStruct(shape, own_dtype),
+        in_specs=[pl.BlockSpec(memory_space=pltpu.VMEM)] * (1 + len(extras)),
+        out_specs=pl.BlockSpec(memory_space=pltpu.VMEM),
+        scratch_shapes=[
+            pltpu.VMEM(first, x.dtype),
+            pltpu.VMEM(tuple(own_shape), own_dtype),
+            pltpu.VMEM(shape, own_dtype),
+            pltpu.SemaphoreType.DMA((n,)),
+            pltpu.SemaphoreType.DMA((n,)),
+            pltpu.SemaphoreType.DMA(()),
+            pltpu.SemaphoreType.DMA((n,)),
+            pltpu.SemaphoreType.DMA((n,)),
+            pltpu.SemaphoreType.DMA(()),
+        ],
+        compiler_params=pltpu.CompilerParams(collective_id=cid, has_side_effects=True),
+        cost_estimate=pl.CostEstimate(flops=0, transcendentals=0, bytes_accessed=2 * nbytes),
+        name="two_phase_%d" % cid,
+    )(x, *extras)
+
+
+def _merge_combine(buf1, fresh_ref):
+    blocks = buf1[...]
+    fresh = fresh_ref[...]
+    block_max = blocks[:, :, HD : HD + 1]
+    fresh_max = fresh[:, HD : HD + 1]
+    overall = jnp.maximum(jnp.max(block_max, axis=0), fresh_max)
+    block_scale = jnp.exp(block_max - overall[None])
+    fresh_scale = jnp.exp(fresh_max - overall)
+    weighted = jnp.sum(block_scale * blocks, axis=0) + fresh_scale * fresh
+    numer = weighted[:, :HD]
+    denom = weighted[:, HD + 1 : HD + 2]
+    return (numer / denom).astype(jnp.bfloat16)
+
+
+def _down_combine(buf1, middle_ref):
+    return (middle_ref[...] + branch_factor * jnp.sum(buf1[...], axis=0)).astype(jnp.bfloat16)
 
 
 STEPS = 4
@@ -159,8 +227,14 @@
     kv_width = KVH * HD
     group = H // KVH
 
-    picked = jnp.take(embed_table, token_ids.reshape(-1), axis=1)
-    whole = exchange(jnp.transpose(picked, (1, 0)), n, True, 0)
+    vocab = embed_table.shape[1]
+    onehot = (
+        token_ids.reshape(-1)[:, None] == jnp.arange(vocab, dtype=jnp.int32)[None, :]
+    ).astype(embed_table.dtype)
+    picked = lax.dot_general(
+        onehot, embed_table, (((1,), (1,)), ((), ())), preferred_element_type=jnp.float32
+    ).astype(embed_table.dtype)
+    whole = exchange(picked, n, True, 0)
     resid = jnp.transpose(whole, (1, 0, 2)).reshape(rows, width).astype(jnp.float32) * embed_factor
 
     slot_pos = place * ctx_own + jnp.arange(ctx_own, dtype=jnp.int32)
@@ -206,23 +280,24 @@
         ],
         axis=-1,
     )
-    got = exchange(packed, n, False, 2)
-    block_max = got[:, :, HD]
-    block_total = got[:, :, HD + 1]
-    block_out = got[:, :, :HD]
     own_fresh_max = lax.dynamic_index_in_dim(fresh_max.reshape(n, pairs), place, 0, False)
     own_fresh_total = lax.dynamic_index_in_dim(fresh_total.reshape(n, pairs), place, 0, False)
     own_fresh_out = lax.dynamic_index_in_dim(fresh_out.reshape(n, pairs, HD), place, 0, False)
-    overall = jnp.maximum(jnp.max(block_max, axis=0), own_fresh_max)
-    block_scale = jnp.exp(block_max - overall[None, :])
-    fresh_scale = jnp.exp(own_fresh_max - overall)
-    numer = jnp.sum(block_scale[..., None] * block_out, axis=0) + fresh_scale[:, None] * own_fresh_out
-    denom = jnp.sum(block_scale * block_total, axis=0) + fresh_scale * own_fresh_total
-    attention_own = (numer / denom[:, None]).astype(jnp.bfloat16).reshape(1, pairs * HD)
-    attention = exchange(attention_own, n, True, 3).reshape(rows, att_width)
+    fresh_packed = jnp.concatenate(
+        [
+            own_fresh_out,
+            own_fresh_max[:, None],
+            own_fresh_total[:, None],
+            jnp.zeros((pairs, lanes - HD - 2), jnp.float32),
+        ],
+        axis=-1,
+    )
+    attention = two_phase(
+        packed, [fresh_packed], _merge_combine, (pairs, HD), jnp.bfloat16, n, 2
+    ).reshape(rows, att_width)
 
     proj_cols = jnp.dot(attention, w_out, preferred_element_type=jnp.float32).astype(jnp.bfloat16)
-    proj_got = exchange(proj_cols, n, True, 4)
+    proj_got = exchange(proj_cols, n, True, 3)
     projected = jnp.transpose(proj_got, (1, 0, 2)).reshape(rows, width)
     middle = resid + branch_factor * projected.astype(jnp.float32)
     normed_mlp = rms_scale(middle, norm_mlp).astype(jnp.bfloat16)
@@ -231,11 +306,9 @@
     hidden = (jax.nn.silu(gate) * upward).astype(jnp.bfloat16)
     down_part = jnp.dot(hidden, w_down, preferred_element_type=jnp.float32)
     cols = width // n
-    down_got = exchange(jnp.transpose(down_part.reshape(rows, n, cols), (1, 0, 2)), n, False, 5)
-    down_own = jnp.sum(down_got, axis=0)
     middle_own = lax.dynamic_slice_in_dim(middle, place * cols, cols, axis=1)
-    out_own = (middle_own + branch_factor * down_own).astype(jnp.bfloat16)
-    out_got = exchange(out_own, n, True, 6)
+    down_send = jnp.transpose(down_part.reshape(rows, n, cols), (1, 0, 2))
+    out_got = two_phase(down_send, [middle_own], _down_combine, (rows, cols), jnp.bfloat16, n, 4)
     return jnp.transpose(out_got, (1, 0, 2)).reshape(req_all, steps, width)
 
 

time: 178 us -> 154 us (0.87)
  Pallas kernels: 139 us -> 124 us
  local copies, waits for them, and re-layouts: 19.1 us -> 11.4 us
  other arithmetic: 13.9 us -> 7.15 us
  matrix products: 4.74 us -> 10.1 us
    pallas_call x7 -> x3, Pallas kernels: 139 us -> 62.4 us  [exchange(): pl.pallas_call(functools.partial(_exchange_kernel, n, gather), out_shape=...]
    pallas_call x0 -> x2, Pallas kernels: none -> 61.9 us  [two_phase(): pl.pallas_call(functools.partial(_two_phase_kernel, n, combine, len(extra...]
    unnamed x27 -> x32, local copies, waits for them, and re-layouts: 7.04 us -> 1.28 us
    gather x1 -> x0, local copies, waits for them, and re-layouts: 4.24 us -> none  [shards(): picked = jnp.take(embed_table, token_ids.reshape(-1), axis=1)]
    reduce_sum x3 -> x0, other arithmetic: 2.42 us -> none  [the longest x1 1.12 us: shards(): down_own = jnp.sum(down_got, axis=0)]
    dot_general x2, matrix products: 1.68 us -> 3.84 us  [partial_softmax(): jnp.einsum('rskgd,rpkd->rskgp', queries, keys, preferred_element_type=jnp...]
where the time goes in v3:
time: 154 us; the launch traced here: 153 us
  Pallas kernels  124 us (81%)
  local copies, waits for them, and re-layouts  11.4 us (7%)
  matrix products  10.1 us (7%)
  other arithmetic  7.15 us (5%)
    pallas_call x3, Pallas kernels, exchange(): pl.pallas_call(functools.partial(_exchange_kernel, n, gather), out_shape=...  62.4 us
    pallas_call x2, Pallas kernels, two_phase(): pl.pallas_call(functools.partial(_two_phase_kernel, n, combine, len(extra...  61.9 us
    dot_general x2, matrix products, partial_softmax(): jnp.einsum('rskgd,rpkd->rskgp', queries, keys, preferred_element_type=jnp...  3.84 us

profile of v3, /device:TPU:1, one launch (start us, length us, event | category | flops | bytes accessed | tf_op | source)
XLA Modules:
  0.0 153.3 jit_solution(9973815436876460387)
XLA Ops:
  0.0 0.9 eq.15
  0.9 0.5 copy-done
  1.4 1.2 fusion.3.x_ref
  2.6 26.1 %exchange_0.1 = bf16[64,16,32]{2,1,0:T(8,128)(2,1)} custom-call(bf16[16,32]{1,0:T(8,128)(2,1)} %fusion.3.x_ref), custom_call_target="tpu_custom_call" | custom-call | bytes 131072 | tf_op jit(solution)/shard_map/exchange_0/pallas_call | solution.py:88
  28.8 1.1 convert_bitcast_fusion
  30.5 0.8 convolution_convert_fusion.1.x_ref
  31.4 17.6 %exchange_1.1 = bf16[64,16,48]{2,1,0:T(8,128)(2,1)} custom-call(bf16[16,48]{1,0:T(8,128)(2,1)} %convolution_convert_fusion.1.x_ref), custom_call_target="tpu_custom_call" | custom-call | bytes 196608 | tf_op jit(solution)/shard_map/exchange_1/pallas_call | solution.py:88
  49.0 1.0 copy.45
  50.0 0.3 reshape.156
  51.4 1.3 select_reduce_fusion
  52.9 0.4 convolution_bitcast_fusion.1
  53.5 1.3 fusion.15
  54.8 0.8 copy.60
  56.0 0.7 maximum_maximum_fusion.1.refs_1_
  56.7 0.7 broadcast_compare_fusion
  57.4 0.3 copy.48
  57.7 2.5 %select_reduce_fusion.1 = (f32[4,4,8,4]{3,1,2,0:T(4,128)}, f32[4,4,8,4,128]{4,3,1,2,0:T(4,128)}) fusion(pred[4,128]{1,0:T(4,128)(4,1)S(1)} %broadcast_compare_fusion, bf16[4,128,8,64,1]{1,3,4,2,0:T(8,128)(2,1)S(1)} %bitcast.68, bf16[4,4,8,4,64]{4,3,2,1,0:T(4,128)(2,1)} %copy-done.10), kind=kOutput, calls=%fused_computation.29 | convolution fusion | flops 8584704 | bytes 854528 | tf_op jit(solution)/shard_map/rskgd,rpkd->rskgp/dot_general | solution.py:193
  60.5 1.4 convolution_bitcast_fusion
  62.0 0.4 fusion.13
  62.7 0.9 maximum_maximum_fusion.refs_0_
  63.6 28.4 %two_phase_2.1 = bf16[64,8,64]{2,1,0:T(8,128)(2,1)} custom-call(f32[64,8,128]{2,1,0:T(8,128)} %maximum_maximum_fusion.refs_0_, f32[8,128]{1,0:T(8,128)} %maximum_maximum_fusion.1.refs_1_), custom_call_target="tpu_custom_call" | custom-call | bytes 655360 | tf_op jit(solution)/shard_map/two_phase_2/pallas_call | solution.py:123
  92.1 1.1 reshape.166
  93.2 0.8 convolution_convert_fusion.x_ref
  93.9 18.7 %exchange_3.1 = bf16[64,16,32]{2,1,0:T(8,128)(2,1)} custom-call(bf16[16,32]{1,0:T(8,128)(2,1)} %convolution_convert_fusion.x_ref), custom_call_target="tpu_custom_call" | custom-call | bytes 131072 | tf_op jit(solution)/shard_map/exchange_3/pallas_call | solution.py:88
  112.6 1.2 fusion.11
  114.3 1.3 fusion.44
  115.6 0.4 fusion.5
  116.2 1.1 copy.92
  117.3 0.7 constant_dynamic-slice_fusion.refs_1_
  117.9 33.4 %two_phase_4.1 = bf16[64,16,32]{2,1,0:T(8,128)(2,1)} custom-call(f32[64,16,32]{2,1,0:T(8,128)} %bitcast.62, f32[16,32]{1,0:T(8,128)} %constant_dynamic-slice_fusion.refs_1_), custom_call_target="tpu_custom_call" | custom-call | bytes 393216 | tf_op jit(solution)/shard_map/two_phase_4/pallas_call | solution.py:123
  151.4 1.0 copy.66
  152.4 0.9 reshape.168
  (70 shorter events, 3.6 us)
Async XLA Ops:
  0.0 1.4 copy-start
  2.6 27.9 %copy-start.12 = (bf16[2048]{0:T(1024)(128)(2,1)S(1)}, bf16[2048]{0:T(1024)(128)(2,1)}, u32[]{:S(2)}) copy-start(bf16[2048]{0:T(1024)(128)(2,1)} %param.17) | copy-start | bytes 12292
  2.6 27.9 %copy-start.9 = (bf16[2048,48]{0,1:T(8,128)(2,1)S(1)}, bf16[2048,48]{0,1:T(8,128)(2,1)}, u32[]{:S(2)}) copy-start(bf16[2048,48]{0,1:T(8,128)(2,1)} %param.19) | copy-start | bytes 589828
  28.8 1.5 copy-start.1
  30.0 20.6 %copy-start.14 = (s32[4]{0:T(128)S(1)}, s32[4]{0:T(128)}, u32[]{:S(2)}) copy-start(s32[4]{0:T(128)} %param.13) | copy-start | bytes 52
  51.2 1.7 %copy-start.10 = (bf16[4,4,8,4,64]{4,3,2,1,0:T(4,128)(2,1)}, bf16[4,4,8,4,64]{4,3,2,1,0:T(4,128)(2,1)S(1)}, u32[]{:S(2)}) copy-start(bf16[4,4,8,4,64]{4,3,2,1,0:T(4,128)(2,1)S(1)} %pad_maximum_fusion) | copy-start | bytes 196612
  51.4 6.0 %copy-start.4 = (bf16[4,128,512]{2,1,0:T(8,128)(2,1)S(1)}, bf16[4,128,512]{2,1,0:T(8,128)(2,1)}, u32[]{:S(2)}) copy-start(bf16[4,128,512]{2,1,0:T(8,128)(2,1)} %param.15) | copy-start | bytes 1572868
  52.7 0.6 copy-start.7
  53.4 6.8 %copy-start.5 = (bf16[4,128,512]{2,1,0:T(8,128)(2,1)S(1)}, bf16[4,128,512]{2,1,0:T(8,128)(2,1)}, u32[]{:S(2)}) copy-start(bf16[4,128,512]{2,1,0:T(8,128)(2,1)} %param.16) | copy-start | bytes 1572868
  60.2 1.8 %copy-start.6 = (f32[4,4,8,4,128]{4,3,1,2,0:T(4,128)S(1)}, f32[4,4,8,4,128]{4,3,1,2,0:T(4,128)}, u32[]{:S(2)}) copy-start(f32[4,4,8,4,128]{4,3,1,2,0:T(4,128)} %get-tuple-element.18) | copy-start | bytes 786436
  60.2 1.8 %copy-start.8 = (f32[4,4,8,4]{3,1,2,0:T(4,128)S(1)}, f32[4,4,8,4]{3,1,2,0:T(4,128)}, u32[]{:S(2)}) copy-start(f32[4,4,8,4]{3,1,2,0:T(4,128)} %get-tuple-element.17) | copy-start | bytes 6148
  62.0 31.2 %copy-start.11 = (bf16[2048,32]{0,1:T(8,128)(2,1)S(1)}, bf16[2048,32]{0,1:T(8,128)(2,1)}, u32[]{:S(2)}) copy-start(bf16[2048,32]{0,1:T(8,128)(2,1)} %param.20) | copy-start | bytes 393220
  112.6 1.7 %copy-start.13 = (bf16[2048]{0:T(1024)(128)(2,1)S(1)}, bf16[2048]{0:T(1024)(128)(2,1)}, u32[]{:S(2)}) copy-start(bf16[2048]{0:T(1024)(128)(2,1)} %param.18) | copy-start | bytes 12292
  113.8 1.8 %copy-start.2 = (bf16[128,2048]{1,0:T(8,128)(2,1)S(1)}, bf16[128,2048]{1,0:T(8,128)(2,1)}, u32[]{:S(2)}) copy-start(bf16[128,2048]{1,0:T(8,128)(2,1)} %param.23) | copy-start | bytes 1572868
  113.8 1.8 %copy-start.3 = (bf16[2048,128]{1,0:T(8,128)(2,1)S(1)}, bf16[2048,128]{1,0:T(8,128)(2,1)}, u32[]{:S(2)}) copy-start(bf16[2048,128]{1,0:T(8,128)(2,1)} %param.22) | copy-start | bytes 1572868

commit v4 on v3

--- a/solution.py
+++ b/solution.py
@@ -100,6 +100,102 @@
         cost_estimate=pl.CostEstimate(flops=0, transcendentals=0, bytes_accessed=2 * nbytes),
         name="exchange_%d" % cid,
     )(x)
+
+
+def _split(n):
+    low = 1
+    for c in range(1, n + 1):
+        if n % c == 0 and c * c <= n:
+            low = c
+    return low
+
+
+def _stage(m, mine, dev_of, rep, source, buf, send_sems, recv_sems, local_sem):
+    def copy(j, slot):
+        return pltpu.make_async_remote_copy(
+            src_ref=source(j),
+            dst_ref=buf.at[slot],
+            send_sem=send_sems.at[j],
+            recv_sem=recv_sems.at[slot],
+            device_id=(dev_of(j), rep),
+            device_id_type=MESH_ID,
+        )
+
+    def send(k, carry):
+        j = lax.rem(mine + k, m)
+        copy(j, mine).start()
+        return carry
+
+    lax.fori_loop(1, m, send, 0)
+    local = pltpu.make_async_copy(source(mine), buf.at[mine], local_sem)
+    local.start()
+
+    def finish(k, carry):
+        j = lax.rem(mine + k, m)
+        copy(j, mine).wait_send()
+        copy(j, j).wait_recv()
+        return carry
+
+    lax.fori_loop(1, m, finish, 0)
+    local.wait()
+
+
+def _greet2(low, high, hi, lo, rep):
+    barrier = pltpu.get_barrier_semaphore()
+
+    def near(k, carry):
+        peer = hi * low + lax.rem(lo + k, low)
+        pl.semaphore_signal(barrier, inc=1, device_id=(peer, rep), device_id_type=MESH_ID)
+        return carry
+
+    def far(k, carry):
+        peer = lax.rem(hi + k, high) * low + lo
+        pl.semaphore_signal(barrier, inc=1, device_id=(peer, rep), device_id_type=MESH_ID)
+        return carry
+
+    lax.fori_loop(1, low, near, 0)
+    lax.fori_loop(1, high, far, 0)
+    pl.semaphore_wait(barrier, low + high - 2)
+
+
+def _gather2_kernel(n, low, x_ref, o_ref, buf1, buf2, s1, r1, l1, s2, r2, l2):
+    high = n // low
+    me = lax.axis_index("seq")
+    rep = lax.axis_index("rep")
+    hi = me // low
+    lo = lax.rem(me, low)
+    _greet2(low, high, hi, lo, rep)
+    _stage(low, lo, lambda j: hi * low + j, rep, lambda j: x_ref, buf1, s1, r1, l1)
+    _stage(high, hi, lambda j: j * low + lo, rep, lambda j: buf1, buf2, s2, r2, l2)
+    o_ref[...] = buf2[...]
+
+
+def gather2(x, n, cid):
+    low = _split(n)
+    high = n // low
+    blk = tuple(x.shape)
+    shape = (high, low) + blk
+    nbytes = _nbytes(shape, x.dtype)
+    out = pl.pallas_call(
+        functools.partial(_gather2_kernel, n, low),
+        out_shape=jax.ShapeDtypeStruct(shape, x.dtype),
+        in_specs=[pl.BlockSpec(memory_space=pltpu.VMEM)],
+        out_specs=pl.BlockSpec(memory_space=pltpu.VMEM),
+        scratch_shapes=[
+            pltpu.VMEM((low,) + blk, x.dtype),
+            pltpu.VMEM(shape, x.dtype),
+            pltpu.SemaphoreType.DMA((low,)),
+            pltpu.SemaphoreType.DMA((low,)),
+            pltpu.SemaphoreType.DMA(()),
+            pltpu.SemaphoreType.DMA((high,)),
+            pltpu.SemaphoreType.DMA((high,)),
+            pltpu.SemaphoreType.DMA(()),
+        ],
+        compiler_params=pltpu.CompilerParams(collective_id=cid, has_side_effects=True),
+        cost_estimate=pl.CostEstimate(flops=0, transcendentals=0, bytes_accessed=2 * nbytes),
+        name="gather2_%d" % cid,
+    )(x)
+    return out.reshape((n,) + blk)
 
 
 def _two_phase_kernel(n, combine, n_extra, *refs):
@@ -234,7 +330,7 @@
     picked = lax.dot_general(
         onehot, embed_table, (((1,), (1,)), ((), ())), preferred_element_type=jnp.float32
     ).astype(embed_table.dtype)
-    whole = exchange(picked, n, True, 0)
+    whole = gather2(picked, n, 0)
     resid = jnp.transpose(whole, (1, 0, 2)).reshape(rows, width).astype(jnp.float32) * embed_factor
 
     slot_pos = place * ctx_own + jnp.arange(ctx_own, dtype=jnp.int32)
@@ -244,7 +340,7 @@
 
     normed = rms_scale(resid, norm_attn).astype(jnp.bfloat16)
     qkv_cols = jnp.dot(normed, w_qkv, preferred_element_type=jnp.float32).astype(jnp.bfloat16)
-    qkv_got = exchange(qkv_cols, n, True, 1)
+    qkv_got = gather2(qkv_cols, n, 1)
     qkv_all = jnp.transpose(qkv_got, (1, 0, 2)).reshape(req_all, steps, -1)
     where = (cache_lengths[:, None] + jnp.arange(steps, dtype=jnp.int32)[None, :]).astype(
         jnp.float32
@@ -297,7 +393,7 @@
     ).reshape(rows, att_width)
 
     proj_cols = jnp.dot(attention, w_out, preferred_element_type=jnp.float32).astype(jnp.bfloat16)
-    proj_got = exchange(proj_cols, n, True, 3)
+    proj_got = gather2(proj_cols, n, 3)
     projected = jnp.transpose(proj_got, (1, 0, 2)).reshape(rows, width)
     middle = resid + branch_factor * projected.astype(jnp.float32)
     normed_mlp = rms_scale(middle, norm_mlp).astype(jnp.bfloat16)

time: 154 us -> 163 us (1.058)
  Pallas kernels: 124 us -> 131 us
    pallas_call x2, Pallas kernels: 61.9 us -> 67 us  [two_phase(): pl.pallas_call(functools.partial(_two_phase_kernel, n, combine, len(extra...]
    pallas_call x3, Pallas kernels: 62.4 us -> 64.2 us  [gather2(): pl.pallas_call(functools.partial(_gather2_kernel, n, low), out_shape=jax....]
where the time goes in v4:
time: 163 us; the launch traced here: 162 us
  Pallas kernels  131 us (80%)
  local copies, waits for them, and re-layouts  12.7 us (8%)
  matrix products  10.5 us (6%)
  other arithmetic  7.28 us (4%)
    pallas_call x2, Pallas kernels, two_phase(): pl.pallas_call(functools.partial(_two_phase_kernel, n, combine, len(extra...  67 us
    pallas_call x3, Pallas kernels, gather2(): pl.pallas_call(functools.partial(_gather2_kernel, n, low), out_shape=jax....  64.2 us
    dot_general x2, matrix products, partial_softmax(): jnp.einsum('rskgd,rpkd->rskgp', queries, keys, preferred_element_type=jnp...  3.41 us

profile of v4, /device:TPU:1, one launch (start us, length us, event | category | flops | bytes accessed | tf_op | source)
XLA Modules:
  0.0 162.1 jit_solution(13110907631246791307)
XLA Ops:
  0.0 0.9 eq.15
  0.9 0.5 copy-done
  1.4 1.2 fusion.3.x_ref
  2.6 24.7 %gather2_0.1 = bf16[8,8,16,32]{3,2,1,0:T(8,128)(2,1)} custom-call(bf16[16,32]{1,0:T(8,128)(2,1)} %fusion.3.x_ref), custom_call_target="tpu_custom_call" | custom-call | bytes 131072 | tf_op jit(solution)/shard_map/gather2_0/pallas_call | solution.py:179
  27.4 1.1 bitcast_convert_fusion
  29.4 0.8 convolution_convert_fusion.1.x_ref
  30.2 19.0 %gather2_1.1 = bf16[8,8,16,48]{3,2,1,0:T(8,128)(2,1)} custom-call(bf16[16,48]{1,0:T(8,128)(2,1)} %convolution_convert_fusion.1.x_ref), custom_call_target="tpu_custom_call" | custom-call | bytes 196608 | tf_op jit(solution)/shard_map/gather2_1/pallas_call | solution.py:179
  49.2 1.0 copy.98
  51.6 1.3 select_reduce_fusion
  53.1 0.5 copy-done.7
  53.6 0.4 convolution_bitcast_fusion.1
  54.1 1.4 fusion.12
  55.6 0.8 copy.60
  56.7 0.7 maximum_maximum_fusion.1.refs_1_
  57.4 0.7 broadcast_compare_fusion
  58.1 1.0 copy.48
  59.1 2.1 %select_reduce_fusion.1 = (f32[4,4,8,4]{3,1,2,0:T(4,128)}, f32[4,4,8,4,128]{4,3,1,2,0:T(4,128)S(1)}) fusion(pred[4,128]{1,0:T(4,128)(4,1)S(1)} %broadcast_compare_fusion, bf16[4,128,8,64,1]{1,3,4,2,0:T(8,128)(2,1)} %bitcast.91, bf16[4,4,8,4,64]{4,3,2,1,0:T(4,128)(2,1)} %copy-done.10), kind=kOutput, calls=%fused_computation.29 | convolution fusion | flops 8584704 | bytes 854528 | tf_op jit(solution)/shard_map/rskgd,rpkd->rskgp/dot_general | solution.py:289
  61.5 1.4 convolution_bitcast_fusion
  63.0 0.4 fusion.10
  63.7 0.9 maximum_maximum_fusion.refs_0_
  64.6 32.1 %two_phase_2.1 = bf16[64,8,64]{2,1,0:T(8,128)(2,1)} custom-call(f32[64,8,128]{2,1,0:T(8,128)} %maximum_maximum_fusion.refs_0_, f32[8,128]{1,0:T(8,128)} %maximum_maximum_fusion.1.refs_1_), custom_call_target="tpu_custom_call" | custom-call | bytes 655360 | tf_op jit(solution)/shard_map/two_phase_2/pallas_call | solution.py:219
  96.7 1.1 reshape.183
  97.8 1.7 %convolution_convert_fusion.x_ref = bf16[16,32]{1,0:T(8,128)(2,1)} fusion(bf16[16,2048]{1,0:T(8,128)(2,1)S(1)} %reshape.183, bf16[2048,32]{0,1:T(8,128)(2,1)} %param.20), kind=kOutput, calls=%fused_computation.10 | convolution fusion | flops 2097664 | bytes 197632 | tf_op jit(solution)/shard_map/dot_general | solution.py:395
  99.4 20.4 %gather2_3.1 = bf16[8,8,16,32]{3,2,1,0:T(8,128)(2,1)} custom-call(bf16[16,32]{1,0:T(8,128)(2,1)} %convolution_convert_fusion.x_ref), custom_call_target="tpu_custom_call" | custom-call | bytes 131072 | tf_op jit(solution)/shard_map/gather2_3/pallas_call | solution.py:179
  119.9 1.0 convert_multiply_fusion
  121.6 1.3 fusion.41
  122.9 0.4 fusion.5
  123.5 1.1 copy.95
  124.6 0.7 constant_dynamic-slice_fusion.refs_1_
  125.3 34.9 %two_phase_4.1 = bf16[64,16,32]{2,1,0:T(8,128)(2,1)} custom-call(f32[64,16,32]{2,1,0:T(8,128)} %bitcast.84, f32[16,32]{1,0:T(8,128)} %constant_dynamic-slice_fusion.refs_1_), custom_call_target="tpu_custom_call" | custom-call | bytes 393216 | tf_op jit(solution)/shard_map/two_phase_4/pallas_call | solution.py:219
  160.2 1.0 copy.66
  161.2 0.9 reshape.185
  (70 shorter events, 4.2 us)
Async XLA Ops:
  0.0 1.4 copy-start
  27.4 1.5 copy-start.1
  28.4 0.7 copy-start.11
  28.4 0.9 copy-start.9
  28.9 21.9 %copy-start.13 = (s32[4]{0:T(128)S(1)}, s32[4]{0:T(128)}, u32[]{:S(2)}) copy-start(s32[4]{0:T(128)} %param.13) | copy-start | bytes 52
  51.4 1.7 %copy-start.10 = (bf16[4,4,8,4,64]{4,3,2,1,0:T(4,128)(2,1)}, bf16[4,4,8,4,64]{4,3,2,1,0:T(4,128)(2,1)S(1)}, u32[]{:S(2)}) copy-start(bf16[4,4,8,4,64]{4,3,2,1,0:T(4,128)(2,1)S(1)} %pad_maximum_fusion) | copy-start | bytes 196612
  51.6 6.6 %copy-start.4 = (bf16[4,128,512]{2,1,0:T(8,128)(2,1)S(1)}, bf16[4,128,512]{2,1,0:T(8,128)(2,1)}, u32[]{:S(2)}) copy-start(bf16[4,128,512]{2,1,0:T(8,128)(2,1)} %param.15) | copy-start | bytes 1572868
  53.0 0.6 copy-start.7
  53.0 1.0 copy-start.6
  54.1 7.2 %copy-start.5 = (bf16[4,128,512]{2,1,0:T(8,128)(2,1)S(1)}, bf16[4,128,512]{2,1,0:T(8,128)(2,1)}, u32[]{:S(2)}) copy-start(bf16[4,128,512]{2,1,0:T(8,128)(2,1)} %param.16) | copy-start | bytes 1572868
  61.5 1.5 copy-start.8
  120.9 0.7 copy-start.12
  121.1 1.8 %copy-start.2 = (bf16[128,2048]{1,0:T(8,128)(2,1)S(1)}, bf16[128,2048]{1,0:T(8,128)(2,1)}, u32[]{:S(2)}) copy-start(bf16[128,2048]{1,0:T(8,128)(2,1)} %param.23) | copy-start | bytes 1572868
  121.1 1.8 %copy-start.3 = (bf16[2048,128]{1,0:T(8,128)(2,1)S(1)}, bf16[2048,128]{1,0:T(8,128)(2,1)}, u32[]{:S(2)}) copy-start(bf16[2048,128]{1,0:T(8,128)(2,1)} %param.22) | copy-start | bytes 1572868

commit v5 on v4

--- a/solution.py
+++ b/solution.py
@@ -26,51 +26,12 @@
     pl.semaphore_wait(barrier, n - 1)
 
 
-def _spread(n, me, rep, source, buf, send_sems, recv_sems, local_sem):
-    def outgoing(peer):
-        return pltpu.make_async_remote_copy(
-            src_ref=source(peer),
-            dst_ref=buf.at[me],
-            send_sem=send_sems.at[peer],
-            recv_sem=recv_sems.at[me],
-            device_id=(peer, rep),
-            device_id_type=MESH_ID,
-        )
-
-    def incoming(peer):
-        return pltpu.make_async_remote_copy(
-            src_ref=source(peer),
-            dst_ref=buf.at[peer],
-            send_sem=send_sems.at[peer],
-            recv_sem=recv_sems.at[peer],
-            device_id=(peer, rep),
-            device_id_type=MESH_ID,
-        )
-
-    def send(k, carry):
-        outgoing(lax.rem(me + k, n)).start()
-        return carry
-
-    lax.fori_loop(1, n, send, 0)
-    local = pltpu.make_async_copy(source(me), buf.at[me], local_sem)
-    local.start()
-
-    def finish(k, carry):
-        peer = lax.rem(me + k, n)
-        outgoing(peer).wait_send()
-        incoming(peer).wait_recv()
-        return carry
-
-    lax.fori_loop(1, n, finish, 0)
-    local.wait()
-
-
 def _exchange_kernel(n, gather, x_ref, o_ref, buf, send_sems, recv_sems, local_sem):
     me = lax.axis_index("seq")
     rep = lax.axis_index("rep")
     _greet(n, me, rep)
     source = (lambda peer: x_ref) if gather else (lambda peer: x_ref.at[peer])
-    _spread(n, me, rep, source, buf, send_sems, recv_sems, local_sem)
+    _stage(n, me, lambda j: j, rep, source, buf, send_sems, recv_sems, local_sem)
     o_ref[...] = buf[...]
 
 
@@ -92,8 +53,8 @@
         out_specs=pl.BlockSpec(memory_space=pltpu.VMEM),
         scratch_shapes=[
             pltpu.VMEM(shape, x.dtype),
-            pltpu.SemaphoreType.DMA((n,)),
-            pltpu.SemaphoreType.DMA((n,)),
+            pltpu.SemaphoreType.DMA(()),
+            pltpu.SemaphoreType.DMA(()),
             pltpu.SemaphoreType.DMA(()),
         ],
         compiler_params=pltpu.CompilerParams(collective_id=cid, has_side_effects=True),
@@ -110,13 +71,13 @@
     return low
 
 
-def _stage(m, mine, dev_of, rep, source, buf, send_sems, recv_sems, local_sem):
+def _stage(m, mine, dev_of, rep, source, buf, send_sem, recv_sem, local_sem):
     def copy(j, slot):
         return pltpu.make_async_remote_copy(
             src_ref=source(j),
             dst_ref=buf.at[slot],
-            send_sem=send_sems.at[j],
-            recv_sem=recv_sems.at[slot],
+            send_sem=send_sem,
+            recv_sem=recv_sem,
             device_id=(dev_of(j), rep),
             device_id_type=MESH_ID,
         )
@@ -129,14 +90,17 @@
     lax.fori_loop(1, m, send, 0)
     local = pltpu.make_async_copy(source(mine), buf.at[mine], local_sem)
     local.start()
-
-    def finish(k, carry):
-        j = lax.rem(mine + k, m)
-        copy(j, mine).wait_send()
-        copy(j, j).wait_recv()
-        return carry
-
-    lax.fori_loop(1, m, finish, 0)
+    rest = buf.at[pl.ds(0, m - 1)]
+    every = pltpu.make_async_remote_copy(
+        src_ref=rest,
+        dst_ref=rest,
+        send_sem=send_sem,
+        recv_sem=recv_sem,
+        device_id=(dev_of(lax.rem(mine + 1, m)), rep),
+        device_id_type=MESH_ID,
+    )
+    every.wait_send()
+    every.wait_recv()
     local.wait()
 
 
@@ -184,11 +148,11 @@
         scratch_shapes=[
             pltpu.VMEM((low,) + blk, x.dtype),
             pltpu.VMEM(shape, x.dtype),
-            pltpu.SemaphoreType.DMA((low,)),
-            pltpu.SemaphoreType.DMA((low,)),
-            pltpu.SemaphoreType.DMA(()),
-            pltpu.SemaphoreType.DMA((high,)),
-            pltpu.SemaphoreType.DMA((high,)),
+            pltpu.SemaphoreType.DMA(()),
+            pltpu.SemaphoreType.DMA(()),
+            pltpu.SemaphoreType.DMA(()),
+            pltpu.SemaphoreType.DMA(()),
+            pltpu.SemaphoreType.DMA(()),
             pltpu.SemaphoreType.DMA(()),
         ],
         compiler_params=pltpu.CompilerParams(collective_id=cid, has_side_effects=True),
@@ -206,9 +170,9 @@
     me = lax.axis_index("seq")
     rep = lax.axis_index("rep")
     _greet(n, me, rep)
-    _spread(n, me, rep, lambda peer: x_ref.at[peer], buf1, s1, r1, l1)
+    _stage(n, me, lambda j: j, rep, lambda peer: x_ref.at[peer], buf1, s1, r1, l1)
     own[...] = combine(buf1, *extras)
-    _spread(n, me, rep, lambda peer: own, buf2, s2, r2, l2)
+    _stage(n, me, lambda j: j, rep, lambda peer: own, buf2, s2, r2, l2)
     o_ref[...] = buf2[...]
 
 
@@ -225,11 +189,11 @@
             pltpu.VMEM(first, x.dtype),
             pltpu.VMEM(tuple(own_shape), own_dtype),
             pltpu.VMEM(shape, own_dtype),
-            pltpu.SemaphoreType.DMA((n,)),
-            pltpu.SemaphoreType.DMA((n,)),
-            pltpu.SemaphoreType.DMA(()),
-            pltpu.SemaphoreType.DMA((n,)),
-            pltpu.SemaphoreType.DMA((n,)),
+            pltpu.SemaphoreType.DMA(()),
+            pltpu.SemaphoreType.DMA(()),
+            pltpu.SemaphoreType.DMA(()),
+            pltpu.SemaphoreType.DMA(()),
+            pltpu.SemaphoreType.DMA(()),
             pltpu.SemaphoreType.DMA(()),
         ],
         compiler_params=pltpu.CompilerParams(collective_id=cid, has_side_effects=True),

time: 163 us -> 155 us (0.951)
  Pallas kernels: 131 us -> 123 us
    pallas_call x2, Pallas kernels: 67 us -> 60.3 us  [two_phase(): pl.pallas_call(functools.partial(_two_phase_kernel, n, combine, len(extra...]
where the time goes in v5:
time: 155 us; the launch traced here: 154 us
  Pallas kernels  123 us (79%)
  local copies, waits for them, and re-layouts  12.7 us (8%)
  matrix products  10.5 us (7%)
  other arithmetic  7.28 us (5%)
    pallas_call x3, Pallas kernels, gather2(): pl.pallas_call(functools.partial(_gather2_kernel, n, low), out_shape=jax....  63 us
    pallas_call x2, Pallas kernels, two_phase(): pl.pallas_call(functools.partial(_two_phase_kernel, n, combine, len(extra...  60.3 us
    dot_general x2, matrix products, partial_softmax(): jnp.einsum('rskgd,rpkd->rskgp', queries, keys, preferred_element_type=jnp...  3.41 us

profile of v5, /device:TPU:1, one launch (start us, length us, event | category | flops | bytes accessed | tf_op | source)
XLA Modules:
  0.0 154.3 jit_solution(17910209026457496255)
XLA Ops:
  0.0 0.9 eq.15
  0.9 0.5 copy-done
  1.4 1.2 fusion.3.x_ref
  2.6 24.4 %gather2_0.1 = bf16[8,8,16,32]{3,2,1,0:T(8,128)(2,1)} custom-call(bf16[16,32]{1,0:T(8,128)(2,1)} %fusion.3.x_ref), custom_call_target="tpu_custom_call" | custom-call | bytes 131072 | tf_op jit(solution)/shard_map/gather2_0/pallas_call | solution.py:143
  27.1 1.1 bitcast_convert_fusion
  29.1 0.8 convolution_convert_fusion.1.x_ref
  29.9 18.6 %gather2_1.1 = bf16[8,8,16,48]{3,2,1,0:T(8,128)(2,1)} custom-call(bf16[16,48]{1,0:T(8,128)(2,1)} %convolution_convert_fusion.1.x_ref), custom_call_target="tpu_custom_call" | custom-call | bytes 196608 | tf_op jit(solution)/shard_map/gather2_1/pallas_call | solution.py:143
  48.5 1.0 copy.98
  50.9 1.3 select_reduce_fusion
  52.4 0.5 copy-done.7
  52.9 0.4 convolution_bitcast_fusion.1
  53.4 1.4 fusion.12
  54.9 0.8 copy.60
  56.0 0.7 maximum_maximum_fusion.1.refs_1_
  56.7 0.7 broadcast_compare_fusion
  57.4 1.0 copy.48
  58.4 2.1 %select_reduce_fusion.1 = (f32[4,4,8,4]{3,1,2,0:T(4,128)}, f32[4,4,8,4,128]{4,3,1,2,0:T(4,128)S(1)}) fusion(pred[4,128]{1,0:T(4,128)(4,1)S(1)} %broadcast_compare_fusion, bf16[4,128,8,64,1]{1,3,4,2,0:T(8,128)(2,1)} %bitcast.91, bf16[4,4,8,4,64]{4,3,2,1,0:T(4,128)(2,1)} %copy-done.10), kind=kOutput, calls=%fused_computation.29 | convolution fusion | flops 8584704 | bytes 854528 | tf_op jit(solution)/shard_map/rskgd,rpkd->rskgp/dot_general | solution.py:253
  60.8 1.4 convolution_bitcast_fusion
  62.3 0.4 fusion.10
  63.0 0.9 maximum_maximum_fusion.refs_0_
  63.9 29.2 %two_phase_2.1 = bf16[64,8,64]{2,1,0:T(8,128)(2,1)} custom-call(f32[64,8,128]{2,1,0:T(8,128)} %maximum_maximum_fusion.refs_0_, f32[8,128]{1,0:T(8,128)} %maximum_maximum_fusion.1.refs_1_), custom_call_target="tpu_custom_call" | custom-call | bytes 655360 | tf_op jit(solution)/shard_map/two_phase_2/pallas_call | solution.py:183
  93.1 1.1 reshape.183
  94.2 1.7 %convolution_convert_fusion.x_ref = bf16[16,32]{1,0:T(8,128)(2,1)} fusion(bf16[16,2048]{1,0:T(8,128)(2,1)S(1)} %reshape.183, bf16[2048,32]{0,1:T(8,128)(2,1)} %param.20), kind=kOutput, calls=%fused_computation.10 | convolution fusion | flops 2097664 | bytes 197632 | tf_op jit(solution)/shard_map/dot_general | solution.py:359
  95.8 20.0 %gather2_3.1 = bf16[8,8,16,32]{3,2,1,0:T(8,128)(2,1)} custom-call(bf16[16,32]{1,0:T(8,128)(2,1)} %convolution_convert_fusion.x_ref), custom_call_target="tpu_custom_call" | custom-call | bytes 131072 | tf_op jit(solution)/shard_map/gather2_3/pallas_call | solution.py:143
  115.9 1.0 convert_multiply_fusion
  117.6 1.3 fusion.41
  118.9 0.4 fusion.5
  119.5 1.1 copy.95
  120.6 0.7 constant_dynamic-slice_fusion.refs_1_
  121.3 31.1 %two_phase_4.1 = bf16[64,16,32]{2,1,0:T(8,128)(2,1)} custom-call(f32[64,16,32]{2,1,0:T(8,128)} %bitcast.84, f32[16,32]{1,0:T(8,128)} %constant_dynamic-slice_fusion.refs_1_), custom_call_target="tpu_custom_call" | custom-call | bytes 393216 | tf_op jit(solution)/shard_map/two_phase_4/pallas_call | solution.py:183
  152.4 1.0 copy.66
  153.4 0.9 reshape.185
  (70 shorter events, 4.2 us)
Async XLA Ops:
  0.0 1.4 copy-start
  27.1 1.5 copy-start.1
  28.2 0.7 copy-start.11
  28.2 0.9 copy-start.9
  28.6 21.5 %copy-start.13 = (s32[4]{0:T(128)S(1)}, s32[4]{0:T(128)}, u32[]{:S(2)}) copy-start(s32[4]{0:T(128)} %param.13) | copy-start | bytes 52
  50.7 1.7 %copy-start.10 = (bf16[4,4,8,4,64]{4,3,2,1,0:T(4,128)(2,1)}, bf16[4,4,8,4,64]{4,3,2,1,0:T(4,128)(2,1)S(1)}, u32[]{:S(2)}) copy-start(bf16[4,4,8,4,64]{4,3,2,1,0:T(4,128)(2,1)S(1)} %pad_maximum_fusion) | copy-start | bytes 196612
  50.9 6.6 %copy-start.4 = (bf16[4,128,512]{2,1,0:T(8,128)(2,1)S(1)}, bf16[4,128,512]{2,1,0:T(8,128)(2,1)}, u32[]{:S(2)}) copy-start(bf16[4,128,512]{2,1,0:T(8,128)(2,1)} %param.15) | copy-start | bytes 1572868
  52.3 0.6 copy-start.7
  52.3 1.0 copy-start.6
  53.4 7.2 %copy-start.5 = (bf16[4,128,512]{2,1,0:T(8,128)(2,1)S(1)}, bf16[4,128,512]{2,1,0:T(8,128)(2,1)}, u32[]{:S(2)}) copy-start(bf16[4,128,512]{2,1,0:T(8,128)(2,1)} %param.16) | copy-start | bytes 1572868
  60.8 1.5 copy-start.8
  116.9 0.7 copy-start.12
  117.1 1.8 %copy-start.2 = (bf16[128,2048]{1,0:T(8,128)(2,1)S(1)}, bf16[128,2048]{1,0:T(8,128)(2,1)}, u32[]{:S(2)}) copy-start(bf16[128,2048]{1,0:T(8,128)(2,1)} %param.23) | copy-start | bytes 1572868
  117.1 1.8 %copy-start.3 = (bf16[2048,128]{1,0:T(8,128)(2,1)S(1)}, bf16[2048,128]{1,0:T(8,128)(2,1)}, u32[]{:S(2)}) copy-start(bf16[2048,128]{1,0:T(8,128)(2,1)} %param.22) | copy-start | bytes 1572868

commit v6 on v5

--- a/solution.py
+++ b/solution.py
@@ -200,6 +200,59 @@
         cost_estimate=pl.CostEstimate(flops=0, transcendentals=0, bytes_accessed=2 * nbytes),
         name="two_phase_%d" % cid,
     )(x, *extras)
+
+
+def _mlp_kernel(
+    n, proj_ref, resid_ref, gain_ref, gate_w_ref, up_w_ref, down_w_ref, o_ref,
+    pbuf, mid, dsend, dbuf, own, obuf, s1, r1, l1, s2, r2, l2, s3, r3, l3,
+):
+    me = lax.axis_index("seq")
+    rep = lax.axis_index("rep")
+    cols, rows = own.shape
+    _greet(n, me, rep)
+    _stage(n, me, lambda j: j, rep, lambda j: proj_ref, pbuf, s1, r1, l1)
+    projected = pbuf[...].astype(jnp.float32).reshape(n * cols, rows)
+    middle = resid_ref[...] + branch_factor * projected
+    mid[...] = middle.reshape(n, cols, rows)
+    mean_square = jnp.mean(middle * middle, axis=0, keepdims=True)
+    normed = (middle * lax.rsqrt(mean_square + norm_epsilon) * gain_ref[...]).astype(jnp.bfloat16)
+    gate = jnp.dot(gate_w_ref[...], normed, preferred_element_type=jnp.float32)
+    upward = jnp.dot(up_w_ref[...], normed, preferred_element_type=jnp.float32)
+    hidden = (gate / (1.0 + jnp.exp(-gate)) * upward).astype(jnp.bfloat16)
+    down = jnp.dot(down_w_ref[...], hidden, preferred_element_type=jnp.float32)
+    dsend[...] = down.reshape(n, cols, rows)
+    _stage(n, me, lambda j: j, rep, lambda j: dsend.at[j], dbuf, s2, r2, l2)
+    total = jnp.sum(dbuf[...], axis=0)
+    own[...] = (mid[me] + branch_factor * total).astype(jnp.bfloat16)
+    _stage(n, me, lambda j: j, rep, lambda j: own, obuf, s3, r3, l3)
+    o_ref[...] = obuf[...]
+
+
+def mlp_block(proj_t, resid_t, gain, gate_w_t, up_w_t, down_w_t, n, cid):
+    cols, rows = proj_t.shape
+    width = n * cols
+    sems = [pltpu.SemaphoreType.DMA(())] * 9
+    flops = 2 * rows * width * gate_w_t.shape[0] * 3
+    return pl.pallas_call(
+        functools.partial(_mlp_kernel, n),
+        out_shape=jax.ShapeDtypeStruct((n, cols, rows), jnp.bfloat16),
+        in_specs=[pl.BlockSpec(memory_space=pltpu.VMEM)] * 6,
+        out_specs=pl.BlockSpec(memory_space=pltpu.VMEM),
+        scratch_shapes=[
+            pltpu.VMEM((n, cols, rows), jnp.bfloat16),
+            pltpu.VMEM((n, cols, rows), jnp.float32),
+            pltpu.VMEM((n, cols, rows), jnp.float32),
+            pltpu.VMEM((n, cols, rows), jnp.float32),
+            pltpu.VMEM((cols, rows), jnp.bfloat16),
+            pltpu.VMEM((n, cols, rows), jnp.bfloat16),
+        ]
+        + sems,
+        compiler_params=pltpu.CompilerParams(collective_id=cid, has_side_effects=True),
+        cost_estimate=pl.CostEstimate(
+            flops=flops, transcendentals=rows * gate_w_t.shape[0], bytes_accessed=3 * 2 * width * gate_w_t.shape[0]
+        ),
+        name="mlp_block_%d" % cid,
+    )(proj_t, resid_t, gain, gate_w_t, up_w_t, down_w_t)
 
 
 def _merge_combine(buf1, fresh_ref):
@@ -294,7 +347,7 @@
     picked = lax.dot_general(
         onehot, embed_table, (((1,), (1,)), ((), ())), preferred_element_type=jnp.float32
     ).astype(embed_table.dtype)
-    whole = gather2(picked, n, 0)
+    whole = exchange(picked, n, True, 0)
     resid = jnp.transpose(whole, (1, 0, 2)).reshape(rows, width).astype(jnp.float32) * embed_factor
 
     slot_pos = place * ctx_own + jnp.arange(ctx_own, dtype=jnp.int32)
@@ -304,7 +357,7 @@
 
     normed = rms_scale(resid, norm_attn).astype(jnp.bfloat16)
     qkv_cols = jnp.dot(normed, w_qkv, preferred_element_type=jnp.float32).astype(jnp.bfloat16)
-    qkv_got = gather2(qkv_cols, n, 1)
+    qkv_got = exchange(qkv_cols, n, True, 1)
     qkv_all = jnp.transpose(qkv_got, (1, 0, 2)).reshape(req_all, steps, -1)
     where = (cache_lengths[:, None] + jnp.arange(steps, dtype=jnp.int32)[None, :]).astype(
         jnp.float32
@@ -357,19 +410,18 @@
     ).reshape(rows, att_width)
 
     proj_cols = jnp.dot(attention, w_out, preferred_element_type=jnp.float32).astype(jnp.bfloat16)
-    proj_got = gather2(proj_cols, n, 3)
-    projected = jnp.transpose(proj_got, (1, 0, 2)).reshape(rows, width)
-    middle = resid + branch_factor * projected.astype(jnp.float32)
-    normed_mlp = rms_scale(middle, norm_mlp).astype(jnp.bfloat16)
-    gate = jnp.dot(normed_mlp, w_gate, preferred_element_type=jnp.float32)
-    upward = jnp.dot(normed_mlp, w_up, preferred_element_type=jnp.float32)
-    hidden = (jax.nn.silu(gate) * upward).astype(jnp.bfloat16)
-    down_part = jnp.dot(hidden, w_down, preferred_element_type=jnp.float32)
     cols = width // n
-    middle_own = lax.dynamic_slice_in_dim(middle, place * cols, cols, axis=1)
-    down_send = jnp.transpose(down_part.reshape(rows, n, cols), (1, 0, 2))
-    out_got = two_phase(down_send, [middle_own], _down_combine, (rows, cols), jnp.bfloat16, n, 4)
-    return jnp.transpose(out_got, (1, 0, 2)).reshape(req_all, steps, width)
+    out_got = mlp_block(
+        jnp.transpose(proj_cols, (1, 0)),
+        jnp.transpose(resid, (1, 0)),
+        norm_mlp.astype(jnp.float32).reshape(width, 1),
+        jnp.transpose(w_gate, (1, 0)),
+        jnp.transpose(w_up, (1, 0)),
+        jnp.transpose(w_down, (1, 0)),
+        n,
+        3,
+    )
+    return jnp.transpose(out_got, (2, 0, 1)).reshape(req_all, steps, width)
 
 
 def solution(mesh):

time: 155 us -> 159 us (1.026)
  Pallas kernels: 123 us -> 132 us
  matrix products: 10.5 us -> 5.68 us
    pallas_call x3, Pallas kernels: 63 us -> 106 us  [the longest x1 65.8 us: mlp_block(): pl.pallas_call(functools.partial(_mlp_kernel, n), out_shape=jax.ShapeDtyp...]
    pallas_call x2 -> x1, Pallas kernels: 60.3 us -> 25.6 us  [two_phase(): pl.pallas_call(functools.partial(_two_phase_kernel, n, combine, len(extra...]
    dot_general x2 -> x0, matrix products: 1.68 us -> none  [the longest x1 1.28 us: shards(): gate = jnp.dot(normed_mlp, w_gate, preferred_element_type=jnp.float32)]
    unnamed x30 -> x27, local copies, waits for them, and re-layouts: 2.61 us -> 3.66 us
    reshape x4 -> x2, local copies, waits for them, and re-layouts: 3.22 us -> 2.31 us  [the longest x1 1.4 us: shards(): norm_mlp.astype(jnp.float32).reshape(width, 1)]
where the time goes in v6:
time: 159 us
  Pallas kernels  132 us (83%)
  local copies, waits for them, and re-layouts  13 us (8%)
  other arithmetic  7.93 us (5%)
  matrix products  5.68 us (4%)
    pallas_call x1, Pallas kernels, mlp_block(): pl.pallas_call(functools.partial(_mlp_kernel, n), out_shape=jax.ShapeDtyp...  65.8 us
    pallas_call x2, Pallas kernels, exchange(): pl.pallas_call(functools.partial(_exchange_kernel, n, gather), out_shape=...  40.4 us
    pallas_call x1, Pallas kernels, two_phase(): pl.pallas_call(functools.partial(_two_phase_kernel, n, combine, len(extra...  25.6 us
    unnamed x27, local copies, waits for them, and re-layouts  3.66 us

profile of v6, /device:TPU:1, one launch (start us, length us, event | category | flops | bytes accessed | tf_op | source)
XLA Modules:
  0.0 158.6 jit_solution(11256830167131435177)
XLA Ops:
  0.0 0.8 broadcast_compare_fusion
  0.9 0.8 eq.15
  1.7 0.7 add_convert_fusion.2
  2.5 1.2 fusion.3.x_ref
  3.8 24.3 %exchange_0.1 = bf16[64,16,32]{2,1,0:T(8,128)(2,1)} custom-call(bf16[16,32]{1,0:T(8,128)(2,1)} %fusion.3.x_ref), custom_call_target="tpu_custom_call" | custom-call | bytes 131072 | tf_op jit(solution)/shard_map/exchange_0/pallas_call | solution.py:49
  28.2 1.2 fusion.8
  29.4 1.0 convert_bitcast_fusion
  30.3 0.4 copy.77
  30.7 1.2 bitcast_multiply_fusion
  32.0 0.9 convolution_convert_fusion.1.x_ref
  32.9 16.0 %exchange_1.1 = bf16[64,16,48]{2,1,0:T(8,128)(2,1)} custom-call(bf16[16,48]{1,0:T(8,128)(2,1)} %convolution_convert_fusion.1.x_ref), custom_call_target="tpu_custom_call" | custom-call | bytes 196608 | tf_op jit(solution)/shard_map/exchange_1/pallas_call | solution.py:49
  48.9 1.0 copy.78
  49.9 0.3 reshape.145
  51.2 1.3 select_reduce_fusion
  52.5 0.4 fusion.11
  52.8 0.4 convolution_bitcast_fusion.1
  53.7 0.7 maximum_maximum_fusion.1.refs_1_
  54.6 1.3 select_reduce_fusion.1
  55.9 0.4 fusion.9
  56.6 0.3 copy.82
  56.9 0.5 convolution_bitcast_fusion
  57.5 0.9 maximum_maximum_fusion.refs_0_
  58.4 25.6 %two_phase_2.1 = bf16[64,8,64]{2,1,0:T(8,128)(2,1)} custom-call(f32[64,8,128]{2,1,0:T(8,128)} %maximum_maximum_fusion.refs_0_, f32[8,128]{1,0:T(8,128)} %maximum_maximum_fusion.1.refs_1_), custom_call_target="tpu_custom_call" | custom-call | bytes 655360 | tf_op jit(solution)/shard_map/two_phase_2/pallas_call | solution.py:183
  84.0 1.1 reshape.155
  85.2 0.7 copy.97
  85.9 1.0 copy.98
  86.9 1.0 copy.99
  88.0 1.0 copy.100
  89.0 1.4 copy.101.gain_ref
  90.4 65.8 %mlp_block_3.1 = bf16[64,32,16]{2,1,0:T(8,128)(2,1)} custom-call(bf16[32,16]{1,0:T(8,128)(2,1)} %bitcast.81, f32[2048,16]{1,0:T(8,128)} %bitcast.68, f32[2048,1]{1,0:T(8,128)} %copy.101.gain_ref, bf16[128,2048]{1,0:T(8,128)(2,1)} %bitcast.69, bf16[128,2048]{1,0:T(8,128)(2,1)} %bitcast.70, bf16[2048,128]{1,0:T(8,128)(2,1)} %bitcast.71), custom_call_target="tpu_custom_call" | custom-call | flops 25165824 | bytes 1572864 | tf_op jit(solution)/shard_map/mlp_block_3/pallas_call | solution.py:236
  156.2 1.5 copy.102
  157.7 0.9 reshape.158
  (56 shorter events, 2.3 us)
Async XLA Ops:
  0.0 2.5 %copy-start = (bf16[32,24704]{1,0:T(8,128)(2,1)S(1)}, bf16[32,24704]{1,0:T(8,128)(2,1)}, u32[]{:S(2)}) copy-start(bf16[32,24704]{1,0:T(8,128)(2,1)} %param.14) | copy-start | bytes 4743172
  0.0 3.7 %copy-start.10 = (bf16[2048]{0:T(1024)(128)(2,1)S(1)}, bf16[2048]{0:T(1024)(128)(2,1)}, u32[]{:S(2)}) copy-start(bf16[2048]{0:T(1024)(128)(2,1)} %param.18) | copy-start | bytes 12292
  0.0 3.7 %copy-start.9 = (bf16[2048]{0:T(1024)(128)(2,1)S(1)}, bf16[2048]{0:T(1024)(128)(2,1)}, u32[]{:S(2)}) copy-start(bf16[2048]{0:T(1024)(128)(2,1)} %param.17) | copy-start | bytes 12292
  30.7 1.3 copy-start.6
  51.0 3.4 %copy-start.1 = (bf16[4,128,512]{2,1,0:T(8,128)(2,1)S(1)}, bf16[4,128,512]{2,1,0:T(8,128)(2,1)}, u32[]{:S(2)}) copy-start(bf16[4,128,512]{2,1,0:T(8,128)(2,1)} %param.15) | copy-start | bytes 1572868
  51.2 2.1 %copy-start.7 = (bf16[4,4,8,4,64]{4,3,2,1,0:T(4,128)(2,1)}, bf16[4,4,8,4,64]{4,3,2,1,0:T(4,128)(2,1)S(1)}, u32[]{:S(2)}) copy-start(bf16[4,4,8,4,64]{4,3,2,1,0:T(4,128)(2,1)S(1)} %pad_maximum_fusion) | copy-start | bytes 196612
  54.4 2.3 %copy-start.2 = (bf16[4,128,512]{2,1,0:T(8,128)(2,1)S(1)}, bf16[4,128,512]{2,1,0:T(8,128)(2,1)}, u32[]{:S(2)}) copy-start(bf16[4,128,512]{2,1,0:T(8,128)(2,1)} %param.16) | copy-start | bytes 1572868
  57.4 27.7 %copy-start.8 = (bf16[2048,32]{0,1:T(8,128)(2,1)S(1)}, bf16[2048,32]{0,1:T(8,128)(2,1)}, u32[]{:S(2)}) copy-start(bf16[2048,32]{0,1:T(8,128)(2,1)} %param.20) | copy-start | bytes 393220
  57.4 28.5 %copy-start.3 = (bf16[2048,128]{1,0:T(8,128)(2,1)S(1)}, bf16[2048,128]{1,0:T(8,128)(2,1)}, u32[]{:S(2)}) copy-start(bf16[2048,128]{1,0:T(8,128)(2,1)} %param.21) | copy-start | bytes 1572868
  57.5 29.5 %copy-start.4 = (bf16[2048,128]{1,0:T(8,128)(2,1)S(1)}, bf16[2048,128]{1,0:T(8,128)(2,1)}, u32[]{:S(2)}) copy-start(bf16[2048,128]{1,0:T(8,128)(2,1)} %param.22) | copy-start | bytes 1572868
  58.4 29.6 %copy-start.5 = (bf16[128,2048]{1,0:T(8,128)(2,1)S(1)}, bf16[128,2048]{1,0:T(8,128)(2,1)}, u32[]{:S(2)}) copy-start(bf16[128,2048]{1,0:T(8,128)(2,1)} %param.23) | copy-start | bytes 1572868

commit v7 on v5

--- a/solution.py
+++ b/solution.py
@@ -294,7 +294,7 @@
     picked = lax.dot_general(
         onehot, embed_table, (((1,), (1,)), ((), ())), preferred_element_type=jnp.float32
     ).astype(embed_table.dtype)
-    whole = gather2(picked, n, 0)
+    whole = exchange(picked, n, True, 0)
     resid = jnp.transpose(whole, (1, 0, 2)).reshape(rows, width).astype(jnp.float32) * embed_factor
 
     slot_pos = place * ctx_own + jnp.arange(ctx_own, dtype=jnp.int32)
@@ -304,7 +304,7 @@
 
     normed = rms_scale(resid, norm_attn).astype(jnp.bfloat16)
     qkv_cols = jnp.dot(normed, w_qkv, preferred_element_type=jnp.float32).astype(jnp.bfloat16)
-    qkv_got = gather2(qkv_cols, n, 1)
+    qkv_got = exchange(qkv_cols, n, True, 1)
     qkv_all = jnp.transpose(qkv_got, (1, 0, 2)).reshape(req_all, steps, -1)
     where = (cache_lengths[:, None] + jnp.arange(steps, dtype=jnp.int32)[None, :]).astype(
         jnp.float32
@@ -357,7 +357,7 @@
     ).reshape(rows, att_width)
 
     proj_cols = jnp.dot(attention, w_out, preferred_element_type=jnp.float32).astype(jnp.bfloat16)
-    proj_got = gather2(proj_cols, n, 3)
+    proj_got = exchange(proj_cols, n, True, 3)
     projected = jnp.transpose(proj_got, (1, 0, 2)).reshape(rows, width)
     middle = resid + branch_factor * projected.astype(jnp.float32)
     normed_mlp = rms_scale(middle, norm_mlp).astype(jnp.bfloat16)

time: 155 us -> 143 us (0.923)
  Pallas kernels: 123 us -> 113 us
    pallas_call x3, Pallas kernels: 63 us -> 57.2 us  [exchange(): pl.pallas_call(functools.partial(_exchange_kernel, n, gather), out_shape=...]
    pallas_call x2, Pallas kernels: 60.3 us -> 55.9 us  [two_phase(): pl.pallas_call(functools.partial(_two_phase_kernel, n, combine, len(extra...]
where the time goes in v7:
time: 143 us; the launch traced here: 142 us
  Pallas kernels  113 us (79%)
  local copies, waits for them, and re-layouts  11.4 us (8%)
  matrix products  10.1 us (7%)
  other arithmetic  7.15 us (5%)
    pallas_call x3, Pallas kernels, exchange(): pl.pallas_call(functools.partial(_exchange_kernel, n, gather), out_shape=...  57.2 us
    pallas_call x2, Pallas kernels, two_phase(): pl.pallas_call(functools.partial(_two_phase_kernel, n, combine, len(extra...  55.9 us
    dot_general x2, matrix products, partial_softmax(): jnp.einsum('rskgd,rpkd->rskgp', queries, keys, preferred_element_type=jnp...  3.84 us

profile of v7, /device:TPU:1, one launch (start us, length us, event | category | flops | bytes accessed | tf_op | source)
XLA Modules:
  0.0 142.2 jit_solution(9664639667088447919)
XLA Ops:
  0.0 0.9 eq.15
  0.9 0.5 copy-done
  1.4 1.2 fusion.3.x_ref
  2.6 24.4 %exchange_0.1 = bf16[64,16,32]{2,1,0:T(8,128)(2,1)} custom-call(bf16[16,32]{1,0:T(8,128)(2,1)} %fusion.3.x_ref), custom_call_target="tpu_custom_call" | custom-call | bytes 131072 | tf_op jit(solution)/shard_map/exchange_0/pallas_call | solution.py:49
  27.1 1.1 convert_bitcast_fusion
  28.8 0.8 convolution_convert_fusion.1.x_ref
  29.7 16.1 %exchange_1.1 = bf16[64,16,48]{2,1,0:T(8,128)(2,1)} custom-call(bf16[16,48]{1,0:T(8,128)(2,1)} %convolution_convert_fusion.1.x_ref), custom_call_target="tpu_custom_call" | custom-call | bytes 196608 | tf_op jit(solution)/shard_map/exchange_1/pallas_call | solution.py:49
  45.7 1.0 copy.45
  46.8 0.3 reshape.156
  48.2 1.3 select_reduce_fusion
  49.6 0.4 convolution_bitcast_fusion.1
  50.2 1.3 fusion.15
  51.6 0.8 copy.60
  52.7 0.7 maximum_maximum_fusion.1.refs_1_
  53.4 0.7 broadcast_compare_fusion
  54.1 0.3 copy.48
  54.4 2.5 %select_reduce_fusion.1 = (f32[4,4,8,4]{3,1,2,0:T(4,128)}, f32[4,4,8,4,128]{4,3,1,2,0:T(4,128)}) fusion(pred[4,128]{1,0:T(4,128)(4,1)S(1)} %broadcast_compare_fusion, bf16[4,128,8,64,1]{1,3,4,2,0:T(8,128)(2,1)S(1)} %bitcast.68, bf16[4,4,8,4,64]{4,3,2,1,0:T(4,128)(2,1)} %copy-done.10), kind=kOutput, calls=%fused_computation.29 | convolution fusion | flops 8584704 | bytes 854528 | tf_op jit(solution)/shard_map/rskgd,rpkd->rskgp/dot_general | solution.py:253
  57.2 1.4 convolution_bitcast_fusion
  58.8 0.4 fusion.13
  59.5 0.9 maximum_maximum_fusion.refs_0_
  60.4 25.5 %two_phase_2.1 = bf16[64,8,64]{2,1,0:T(8,128)(2,1)} custom-call(f32[64,8,128]{2,1,0:T(8,128)} %maximum_maximum_fusion.refs_0_, f32[8,128]{1,0:T(8,128)} %maximum_maximum_fusion.1.refs_1_), custom_call_target="tpu_custom_call" | custom-call | bytes 655360 | tf_op jit(solution)/shard_map/two_phase_2/pallas_call | solution.py:183
  85.9 1.1 reshape.166
  86.9 0.8 convolution_convert_fusion.x_ref
  87.7 16.7 %exchange_3.1 = bf16[64,16,32]{2,1,0:T(8,128)(2,1)} custom-call(bf16[16,32]{1,0:T(8,128)(2,1)} %convolution_convert_fusion.x_ref), custom_call_target="tpu_custom_call" | custom-call | bytes 131072 | tf_op jit(solution)/shard_map/exchange_3/pallas_call | solution.py:49
  104.4 1.2 fusion.11
  106.1 1.3 fusion.44
  107.4 0.4 fusion.5
  108.0 1.1 copy.92
  109.1 0.7 constant_dynamic-slice_fusion.refs_1_
  109.8 30.5 %two_phase_4.1 = bf16[64,16,32]{2,1,0:T(8,128)(2,1)} custom-call(f32[64,16,32]{2,1,0:T(8,128)} %bitcast.62, f32[16,32]{1,0:T(8,128)} %constant_dynamic-slice_fusion.refs_1_), custom_call_target="tpu_custom_call" | custom-call | bytes 393216 | tf_op jit(solution)/shard_map/two_phase_4/pallas_call | solution.py:183
  140.2 1.0 copy.66
  141.3 0.9 reshape.168
  (70 shorter events, 3.6 us)
Async XLA Ops:
  0.0 1.4 %copy-start = (bf16[32,24704]{1,0:T(8,128)(2,1)S(1)}, bf16[32,24704]{1,0:T(8,128)(2,1)}, u32[]{:S(2)}) copy-start(bf16[32,24704]{1,0:T(8,128)(2,1)} %param.14) | copy-start | bytes 4743172
  2.6 26.2 %copy-start.12 = (bf16[2048]{0:T(1024)(128)(2,1)S(1)}, bf16[2048]{0:T(1024)(128)(2,1)}, u32[]{:S(2)}) copy-start(bf16[2048]{0:T(1024)(128)(2,1)} %param.17) | copy-start | bytes 12292
  2.6 26.2 %copy-start.9 = (bf16[2048,48]{0,1:T(8,128)(2,1)S(1)}, bf16[2048,48]{0,1:T(8,128)(2,1)}, u32[]{:S(2)}) copy-start(bf16[2048,48]{0,1:T(8,128)(2,1)} %param.19) | copy-start | bytes 589828
  27.1 1.5 %copy-start.1 = (bf16[64,16,32]{2,1,0:T(8,128)(2,1)S(1)}, bf16[64,16,32]{2,1,0:T(8,128)(2,1)}, u32[]{:S(2)}) copy-start(bf16[64,16,32]{2,1,0:T(8,128)(2,1)} %exchange_0.1) | copy-start | bytes 196612
  28.3 19.0 %copy-start.14 = (s32[4]{0:T(128)S(1)}, s32[4]{0:T(128)}, u32[]{:S(2)}) copy-start(s32[4]{0:T(128)} %param.13) | copy-start | bytes 52
  47.9 1.7 %copy-start.10 = (bf16[4,4,8,4,64]{4,3,2,1,0:T(4,128)(2,1)}, bf16[4,4,8,4,64]{4,3,2,1,0:T(4,128)(2,1)S(1)}, u32[]{:S(2)}) copy-start(bf16[4,4,8,4,64]{4,3,2,1,0:T(4,128)(2,1)S(1)} %pad_maximum_fusion) | copy-start | bytes 196612
  48.1 6.0 %copy-start.4 = (bf16[4,128,512]{2,1,0:T(8,128)(2,1)S(1)}, bf16[4,128,512]{2,1,0:T(8,128)(2,1)}, u32[]{:S(2)}) copy-start(bf16[4,128,512]{2,1,0:T(8,128)(2,1)} %param.15) | copy-start | bytes 1572868
  49.5 0.6 copy-start.7
  50.2 6.8 %copy-start.5 = (bf16[4,128,512]{2,1,0:T(8,128)(2,1)S(1)}, bf16[4,128,512]{2,1,0:T(8,128)(2,1)}, u32[]{:S(2)}) copy-start(bf16[4,128,512]{2,1,0:T(8,128)(2,1)} %param.16) | copy-start | bytes 1572868
  57.0 1.8 %copy-start.6 = (f32[4,4,8,4,128]{4,3,1,2,0:T(4,128)S(1)}, f32[4,4,8,4,128]{4,3,1,2,0:T(4,128)}, u32[]{:S(2)}) copy-start(f32[4,4,8,4,128]{4,3,1,2,0:T(4,128)} %get-tuple-element.18) | copy-start | bytes 786436
  57.0 1.8 %copy-start.8 = (f32[4,4,8,4]{3,1,2,0:T(4,128)S(1)}, f32[4,4,8,4]{3,1,2,0:T(4,128)}, u32[]{:S(2)}) copy-start(f32[4,4,8,4]{3,1,2,0:T(4,128)} %get-tuple-element.17) | copy-start | bytes 6148
  58.7 28.2 %copy-start.11 = (bf16[2048,32]{0,1:T(8,128)(2,1)S(1)}, bf16[2048,32]{0,1:T(8,128)(2,1)}, u32[]{:S(2)}) copy-start(bf16[2048,32]{0,1:T(8,128)(2,1)} %param.20) | copy-start | bytes 393220
  104.4 1.7 %copy-start.13 = (bf16[2048]{0:T(1024)(128)(2,1)S(1)}, bf16[2048]{0:T(1024)(128)(2,1)}, u32[]{:S(2)}) copy-start(bf16[2048]{0:T(1024)(128)(2,1)} %param.18) | copy-start | bytes 12292
  105.6 1.8 %copy-start.2 = (bf16[128,2048]{1,0:T(8,128)(2,1)S(1)}, bf16[128,2048]{1,0:T(8,128)(2,1)}, u32[]{:S(2)}) copy-start(bf16[128,2048]{1,0:T(8,128)(2,1)} %param.23) | copy-start | bytes 1572868
  105.6 1.8 %copy-start.3 = (bf16[2048,128]{1,0:T(8,128)(2,1)S(1)}, bf16[2048,128]{1,0:T(8,128)(2,1)}, u32[]{:S(2)}) copy-start(bf16[2048,128]{1,0:T(8,128)(2,1)} %param.22) | copy-start | bytes 1572868

commit v8 on v7

--- a/solution.py
+++ b/solution.py
@@ -200,6 +200,131 @@
         cost_estimate=pl.CostEstimate(flops=0, transcendentals=0, bytes_accessed=2 * nbytes),
         name="two_phase_%d" % cid,
     )(x, *extras)
+
+
+def _wait_all(view, rep, peer, send_sem, recv_sem, do_send, do_recv):
+    every = pltpu.make_async_remote_copy(
+        src_ref=view,
+        dst_ref=view,
+        send_sem=send_sem,
+        recv_sem=recv_sem,
+        device_id=(peer, rep),
+        device_id_type=MESH_ID,
+    )
+    if do_send:
+        every.wait_send()
+    if do_recv:
+        every.wait_recv()
+
+
+def _attend_kernel(
+    n, owners, x_ref, fresh_ref, w_ref, o_ref,
+    buf1, own, buf2, proj, buf3, s1, r1, l1, s2, r2, l2, s3, r3, l3,
+):
+    me = lax.axis_index("seq")
+    rep = lax.axis_index("rep")
+    other = lax.rem(me + 1, n)
+    _greet(n, me, rep)
+    is_owner = me < owners
+
+    def send_one(k, carry):
+        peer = lax.rem(me + k, n)
+
+        @pl.when(peer < owners)
+        def _():
+            pltpu.make_async_remote_copy(
+                src_ref=x_ref.at[peer],
+                dst_ref=buf1.at[me],
+                send_sem=s1,
+                recv_sem=r1,
+                device_id=(peer, rep),
+                device_id_type=MESH_ID,
+            ).start()
+
+        return carry
+
+    lax.fori_loop(1, n, send_one, 0)
+
+    @pl.when(is_owner)
+    def _():
+        local = pltpu.make_async_copy(x_ref.at[me], buf1.at[me], l1)
+        local.start()
+        _wait_all(buf1.at[pl.ds(0, owners - 1)], rep, other, s1, r1, True, False)
+        _wait_all(buf1.at[pl.ds(0, n - 1)], rep, other, s1, r1, False, True)
+        local.wait()
+        blocks = buf1[...]
+        fresh = fresh_ref[me]
+        block_max = blocks[:, :, HD : HD + 1]
+        fresh_max = fresh[:, HD : HD + 1]
+        overall = jnp.maximum(jnp.max(block_max, axis=0), fresh_max)
+        block_scale = jnp.exp(block_max - overall[None])
+        fresh_scale = jnp.exp(fresh_max - overall)
+        weighted = jnp.sum(block_scale * blocks, axis=0) + fresh_scale * fresh
+        own[...] = (weighted[:, :HD] / weighted[:, HD + 1 : HD + 2]).astype(jnp.bfloat16)
+
+        def spread(k, carry):
+            peer = lax.rem(me + k, n)
+            pltpu.make_async_remote_copy(
+                src_ref=own,
+                dst_ref=buf2.at[me],
+                send_sem=s2,
+                recv_sem=r2,
+                device_id=(peer, rep),
+                device_id_type=MESH_ID,
+            ).start()
+            return carry
+
+        lax.fori_loop(1, n, spread, 0)
+        local2 = pltpu.make_async_copy(own, buf2.at[me], l2)
+        local2.start()
+        _wait_all(buf2.at[pl.ds(0, n - 1)], rep, other, s2, r2, True, False)
+        _wait_all(buf2.at[pl.ds(0, owners - 1)], rep, other, s2, r2, False, True)
+        local2.wait()
+
+    @pl.when(jnp.logical_not(is_owner))
+    def _():
+        _wait_all(buf1.at[pl.ds(0, owners)], rep, other, s1, r1, True, False)
+        _wait_all(buf2.at[pl.ds(0, owners)], rep, other, s2, r2, False, True)
+
+    rows, cols = proj.shape
+
+    def head(h, acc):
+        start = pl.multiple_of(h * HD, HD)
+        return acc + jnp.dot(
+            buf2[h], w_ref[pl.ds(start, HD), :], preferred_element_type=jnp.float32
+        )
+
+    acc = lax.fori_loop(0, owners, head, jnp.zeros((rows, cols), jnp.float32))
+    proj[...] = acc.astype(jnp.bfloat16)
+    _stage(n, me, lambda j: j, rep, lambda j: proj, buf3, s3, r3, l3)
+    o_ref[...] = buf3[...]
+
+
+def attend(packed, fresh, w_out, n, cid):
+    owners, rows, lanes = packed.shape
+    cols = w_out.shape[1]
+    sems = [pltpu.SemaphoreType.DMA(())] * 9
+    return pl.pallas_call(
+        functools.partial(_attend_kernel, n, owners),
+        out_shape=jax.ShapeDtypeStruct((n, rows, cols), jnp.bfloat16),
+        in_specs=[pl.BlockSpec(memory_space=pltpu.VMEM)] * 3,
+        out_specs=pl.BlockSpec(memory_space=pltpu.VMEM),
+        scratch_shapes=[
+            pltpu.VMEM((n, rows, lanes), jnp.float32),
+            pltpu.VMEM((rows, HD), jnp.bfloat16),
+            pltpu.VMEM((n, rows, HD), jnp.bfloat16),
+            pltpu.VMEM((rows, cols), jnp.bfloat16),
+            pltpu.VMEM((n, rows, cols), jnp.bfloat16),
+        ]
+        + sems,
+        compiler_params=pltpu.CompilerParams(collective_id=cid, has_side_effects=True),
+        cost_estimate=pl.CostEstimate(
+            flops=2 * rows * owners * HD * cols,
+            transcendentals=n * rows,
+            bytes_accessed=2 * (_nbytes((n, rows, lanes), jnp.float32) + _nbytes(w_out.shape, w_out.dtype)),
+        ),
+        name="attend_%d" % cid,
+    )(packed, fresh, w_out)
 
 
 def _merge_combine(buf1, fresh_ref):
@@ -329,35 +454,26 @@
     ).reshape(1, steps, 1, 1, steps)
     fresh_max, fresh_total, fresh_out = partial_softmax(grouped, keys_new, values_new, fresh_valid)
 
-    pairs = rows * H // n
     lanes = 128
-    packed = jnp.concatenate(
-        [
-            cache_out.reshape(n, pairs, HD),
-            cache_max.reshape(n, pairs, 1),
-            cache_total.reshape(n, pairs, 1),
-            jnp.zeros((n, pairs, lanes - HD - 2), jnp.float32),
-        ],
-        axis=-1,
-    )
-    own_fresh_max = lax.dynamic_index_in_dim(fresh_max.reshape(n, pairs), place, 0, False)
-    own_fresh_total = lax.dynamic_index_in_dim(fresh_total.reshape(n, pairs), place, 0, False)
-    own_fresh_out = lax.dynamic_index_in_dim(fresh_out.reshape(n, pairs, HD), place, 0, False)
-    fresh_packed = jnp.concatenate(
-        [
-            own_fresh_out,
-            own_fresh_max[:, None],
-            own_fresh_total[:, None],
-            jnp.zeros((pairs, lanes - HD - 2), jnp.float32),
-        ],
-        axis=-1,
-    )
-    attention = two_phase(
-        packed, [fresh_packed], _merge_combine, (pairs, HD), jnp.bfloat16, n, 2
-    ).reshape(rows, att_width)
-
-    proj_cols = jnp.dot(attention, w_out, preferred_element_type=jnp.float32).astype(jnp.bfloat16)
-    proj_got = exchange(proj_cols, n, True, 3)
+
+    def by_head(out, top, total):
+        return jnp.concatenate(
+            [
+                jnp.transpose(out.reshape(rows, H, HD), (1, 0, 2)),
+                jnp.transpose(top.reshape(rows, H), (1, 0))[..., None],
+                jnp.transpose(total.reshape(rows, H), (1, 0))[..., None],
+                jnp.zeros((H, rows, lanes - HD - 2), jnp.float32),
+            ],
+            axis=-1,
+        )
+
+    proj_got = attend(
+        by_head(cache_out, cache_max, cache_total),
+        by_head(fresh_out, fresh_max, fresh_total),
+        w_out,
+        n,
+        2,
+    )
     projected = jnp.transpose(proj_got, (1, 0, 2)).reshape(rows, width)
     middle = resid + branch_factor * projected.astype(jnp.float32)
     normed_mlp = rms_scale(middle, norm_mlp).astype(jnp.bfloat16)
@@ -368,7 +484,7 @@
     cols = width // n
     middle_own = lax.dynamic_slice_in_dim(middle, place * cols, cols, axis=1)
     down_send = jnp.transpose(down_part.reshape(rows, n, cols), (1, 0, 2))
-    out_got = two_phase(down_send, [middle_own], _down_combine, (rows, cols), jnp.bfloat16, n, 4)
+    out_got = two_phase(down_send, [middle_own], _down_combine, (rows, cols), jnp.bfloat16, n, 3)
     return jnp.transpose(out_got, (1, 0, 2)).reshape(req_all, steps, width)
 
 

time: 143 us -> 144 us (level)
  local copies, waits for them, and re-layouts: 11.4 us -> 14.4 us
  Pallas kernels: 113 us -> 115 us
  other arithmetic: 7.15 us -> 5.16 us
    pallas_call x0 -> x1, Pallas kernels: none -> 41 us  [attend(): pl.pallas_call(functools.partial(_attend_kernel, n, owners), out_shape=ja...]
    pallas_call x2 -> x1, Pallas kernels: 55.9 us -> 33.4 us  [two_phase(): pl.pallas_call(functools.partial(_two_phase_kernel, n, combine, len(extra...]
    pallas_call x3 -> x2, Pallas kernels: 57.2 us -> 40.5 us  [exchange(): pl.pallas_call(functools.partial(_exchange_kernel, n, gather), out_shape=...]
    unnamed x32 -> x25, local copies, waits for them, and re-layouts: 1.28 us -> 4.81 us
where the time goes in v8:
time: 144 us
  Pallas kernels  115 us (80%)
  local copies, waits for them, and re-layouts  14.4 us (10%)
  matrix products  8.89 us (6%)
  other arithmetic  5.16 us (4%)
    pallas_call x1, Pallas kernels, attend(): pl.pallas_call(functools.partial(_attend_kernel, n, owners), out_shape=ja...  41 us
    pallas_call x2, Pallas kernels, exchange(): pl.pallas_call(functools.partial(_exchange_kernel, n, gather), out_shape=...  40.5 us
    pallas_call x1, Pallas kernels, two_phase(): pl.pallas_call(functools.partial(_two_phase_kernel, n, combine, len(extra...  33.4 us
    unnamed x25, local copies, waits for them, and re-layouts  4.81 us
    dot_general x2, matrix products, partial_softmax(): jnp.einsum('rskgd,rpkd->rskgp', queries, keys, preferred_element_type=jnp...  3.41 us

profile of v8, /device:TPU:1, one launch (start us, length us, event | category | flops | bytes accessed | tf_op | source)
XLA Modules:
  0.0 143.7 jit_solution(7796368745811621613)
XLA Ops:
  0.0 0.9 eq.15
  0.9 0.5 copy-done
  1.4 1.2 fusion.3.x_ref
  2.6 24.4 %exchange_0.1 = bf16[64,16,32]{2,1,0:T(8,128)(2,1)} custom-call(bf16[16,32]{1,0:T(8,128)(2,1)} %fusion.3.x_ref), custom_call_target="tpu_custom_call" | custom-call | bytes 131072 | tf_op jit(solution)/shard_map/exchange_0/pallas_call | solution.py:49
  27.1 1.1 convert_bitcast_fusion
  28.3 0.2 reshape.163
  28.6 0.2 fusion.9
  28.8 0.8 convolution_convert_fusion.x_ref
  29.7 16.0 %exchange_1.1 = bf16[64,16,48]{2,1,0:T(8,128)(2,1)} custom-call(bf16[16,48]{1,0:T(8,128)(2,1)} %convolution_convert_fusion.x_ref), custom_call_target="tpu_custom_call" | custom-call | bytes 196608 | tf_op jit(solution)/shard_map/exchange_1/pallas_call | solution.py:49
  45.7 1.0 copy.46
  46.7 0.3 reshape.151
  48.2 1.3 select_reduce_fusion
  49.6 0.4 convolution_bitcast_fusion.1
  50.0 0.4 fusion.15
  51.1 1.0 copy.49
  52.1 2.1 %select_reduce_fusion.1 = (f32[4,4,8,4]{3,1,2,0:T(4,128)}, f32[4,4,8,4,128]{4,3,1,2,0:T(4,128)S(1)}) fusion(pred[4,128]{1,0:T(4,128)(4,1)S(1)} %broadcast_compare_fusion, bf16[4,128,8,64,1]{1,3,4,2,0:T(8,128)(2,1)} %bitcast.77, bf16[4,4,8,4,64]{4,3,2,1,0:T(4,128)(2,1)} %copy-done.7), kind=kOutput, calls=%fused_computation.29 | convolution fusion | flops 8584704 | bytes 854528 | tf_op jit(solution)/shard_map/rskgd,rpkd->rskgp/dot_general | solution.py:378
  54.2 1.3 copy.50
  55.5 1.4 convolution_bitcast_fusion
  57.0 0.4 fusion.13
  57.7 0.8 copy.52
  59.0 1.1 maximum_maximum_fusion.1
  60.1 1.9 %copy.65.w_ref = bf16[2048,32]{1,0:T(8,128)(2,1)} copy(bf16[2048,32]{0,1:T(8,128)(2,1)} %param.20) | data formatting | bytes 262144 | tf_op args[8]
  62.0 41.0 %attend_2.1 = bf16[64,16,32]{2,1,0:T(8,128)(2,1)} custom-call(f32[32,16,128]{2,1,0:T(8,128)} %get-tuple-element.18.x_ref, f32[32,16,128]{2,1,0:T(8,128)} %get-tuple-element.17.fresh_ref, bf16[2048,32]{1,0:T(8,128)(2,1)} %copy.65.w_ref), custom_call_target="tpu_custom_call" | custom-call | flops 2097152 | bytes 1310720 | tf_op jit(solution)/shard_map/attend_2/pallas_call | solution.py:307
  103.0 1.2 fusion.11
  104.4 0.2 mul.226
  104.7 1.3 fusion.42
  106.0 0.4 fusion.5
  106.6 1.1 copy.94
  107.7 0.7 constant_dynamic-slice_fusion.refs_1_
  108.4 33.4 %two_phase_3.1 = bf16[64,16,32]{2,1,0:T(8,128)(2,1)} custom-call(f32[64,16,32]{2,1,0:T(8,128)} %bitcast.70, f32[16,32]{1,0:T(8,128)} %constant_dynamic-slice_fusion.refs_1_), custom_call_target="tpu_custom_call" | custom-call | bytes 393216 | tf_op jit(solution)/shard_map/two_phase_3/pallas_call | solution.py:183
  141.8 1.0 copy.68
  142.8 0.9 reshape.162
  (59 shorter events, 3.2 us)
Async XLA Ops:
  0.0 1.4 copy-start
  2.6 26.2 %copy-start.8 = (bf16[2048]{0:T(1024)(128)(2,1)S(1)}, bf16[2048]{0:T(1024)(128)(2,1)}, u32[]{:S(2)}) copy-start(bf16[2048]{0:T(1024)(128)(2,1)} %param.17) | copy-start | bytes 12292
  2.6 26.2 %copy-start.6 = (bf16[2048,48]{0,1:T(8,128)(2,1)S(1)}, bf16[2048,48]{0,1:T(8,128)(2,1)}, u32[]{:S(2)}) copy-start(bf16[2048,48]{0,1:T(8,128)(2,1)} %param.19) | copy-start | bytes 589828
  27.1 1.5 %copy-start.1 = (bf16[64,16,32]{2,1,0:T(8,128)(2,1)S(1)}, bf16[64,16,32]{2,1,0:T(8,128)(2,1)}, u32[]{:S(2)}) copy-start(bf16[64,16,32]{2,1,0:T(8,128)(2,1)} %exchange_0.1) | copy-start | bytes 196612
  28.3 19.0 %copy-start.10 = (s32[4]{0:T(128)S(1)}, s32[4]{0:T(128)}, u32[]{:S(2)}) copy-start(s32[4]{0:T(128)} %param.13) | copy-start | bytes 52
  47.9 1.7 %copy-start.7 = (bf16[4,4,8,4,64]{4,3,2,1,0:T(4,128)(2,1)}, bf16[4,4,8,4,64]{4,3,2,1,0:T(4,128)(2,1)S(1)}, u32[]{:S(2)}) copy-start(bf16[4,4,8,4,64]{4,3,2,1,0:T(4,128)(2,1)S(1)} %pad_maximum_fusion) | copy-start | bytes 196612
  48.1 3.0 %copy-start.4 = (bf16[4,128,512]{2,1,0:T(8,128)(2,1)S(1)}, bf16[4,128,512]{2,1,0:T(8,128)(2,1)}, u32[]{:S(2)}) copy-start(bf16[4,128,512]{2,1,0:T(8,128)(2,1)} %param.15) | copy-start | bytes 1572868
  55.5 1.5 %copy-start.5 = (f32[4,4,8,4]{3,1,2,0:T(4,128)S(1)}, f32[4,4,8,4]{3,1,2,0:T(4,128)}, u32[]{:S(2)}) copy-start(f32[4,4,8,4]{3,1,2,0:T(4,128)} %get-tuple-element.21) | copy-start | bytes 6148
  103.0 1.7 %copy-start.9 = (bf16[2048]{0:T(1024)(128)(2,1)S(1)}, bf16[2048]{0:T(1024)(128)(2,1)}, u32[]{:S(2)}) copy-start(bf16[2048]{0:T(1024)(128)(2,1)} %param.18) | copy-start | bytes 12292
  104.2 1.8 %copy-start.2 = (bf16[128,2048]{1,0:T(8,128)(2,1)S(1)}, bf16[128,2048]{1,0:T(8,128)(2,1)}, u32[]{:S(2)}) copy-start(bf16[128,2048]{1,0:T(8,128)(2,1)} %param.23) | copy-start | bytes 1572868
  104.2 1.8 %copy-start.3 = (bf16[2048,128]{1,0:T(8,128)(2,1)S(1)}, bf16[2048,128]{1,0:T(8,128)(2,1)}, u32[]{:S(2)}) copy-start(bf16[2048,128]{1,0:T(8,128)(2,1)} %param.22) | copy-start | bytes 1572868

commit v9 on v7

--- a/solution.py
+++ b/solution.py
@@ -321,9 +321,25 @@
     ).astype(jnp.bfloat16)
     values_new = qkv_all[..., att_width + kv_width :].reshape(req_all, steps, KVH, HD)
     grouped = queries.reshape(req_all, steps, KVH, group, HD)
-    cache_max, cache_total, cache_out = partial_softmax(
-        grouped, cache_keys, cache_values, cache_valid
-    )
+    pick = (jnp.arange(H, dtype=jnp.int32)[:, None] // group) == jnp.arange(KVH, dtype=jnp.int32)[None, :]
+    widened = jnp.where(
+        pick[None, None, :, :, None], queries[:, :, :, None, :], jnp.zeros((), queries.dtype)
+    ).reshape(req_all, steps * H, kv_width)
+    scores = (
+        jnp.einsum("rqc,rpc->rqp", widened, key_cache, preferred_element_type=jnp.float32)
+        * score_factor
+    )
+    flat_valid = cache_valid.reshape(req_all, 1, ctx_own)
+    flat_max = jnp.max(jnp.where(flat_valid, scores, masked_floor), axis=-1)
+    expo = jnp.exp(jnp.where(flat_valid, scores - flat_max[..., None], masked_floor))
+    flat_total = jnp.sum(expo, axis=-1)
+    spread_out = jnp.einsum(
+        "rqp,rpc->rqc", expo.astype(jnp.bfloat16), value_cache, preferred_element_type=jnp.float32
+    ).reshape(req_all, steps, H, KVH, HD)
+    picked_out = jnp.sum(jnp.where(pick[None, None, :, :, None], spread_out, 0.0), axis=3)
+    cache_max = flat_max.reshape(req_all, steps, KVH, group)
+    cache_total = flat_total.reshape(req_all, steps, KVH, group)
+    cache_out = picked_out.reshape(req_all, steps, KVH, group, HD)
     fresh_valid = (
         jnp.arange(steps, dtype=jnp.int32)[None, :] <= jnp.arange(steps, dtype=jnp.int32)[:, None]
     ).reshape(1, steps, 1, 1, steps)

time: 143 us -> 144 us (level)
  local copies, waits for them, and re-layouts: 11.4 us -> 12.9 us
    dot_general x0 -> x2, matrix products: none -> 2.86 us  [the longest x1 1.49 us: shards(): jnp.einsum('rqp,rpc->rqc', expo.astype(jnp.bfloat16), value_cache, prefer...]
    reduce_sum x0 -> x2, other arithmetic: none -> 2.5 us  [the longest x1 2.34 us: shards(): jnp.sum(jnp.where(pick[None, None, :, :, None], spread_out, 0.0), axis=3)]
    dot_general x2 -> x1, matrix products: 3.84 us -> 1.35 us  [partial_softmax(): jnp.einsum('rskgd,rpkd->rskgp', queries, keys, preferred_element_type=jnp...]
    reshape x2 -> x1, local copies, waits for them, and re-layouts: 0.23 us -> 1.76 us  [shards(): spread_out = jnp.einsum('rqp,rpc->rqc', expo.astype(jnp.bfloat16), value_...]
where the time goes in v9:
time: 144 us; the launch traced here: 143 us
  Pallas kernels  113 us (78%)
  local copies, waits for them, and re-layouts  12.9 us (9%)
  matrix products  9.07 us (6%)
  other arithmetic  7.65 us (5%)
    pallas_call x3, Pallas kernels, exchange(): pl.pallas_call(functools.partial(_exchange_kernel, n, gather), out_shape=...  57.1 us
    pallas_call x2, Pallas kernels, two_phase(): pl.pallas_call(functools.partial(_two_phase_kernel, n, combine, len(extra...  55.8 us

profile of v9, /device:TPU:1, one launch (start us, length us, event | category | flops | bytes accessed | tf_op | source)
XLA Modules:
  0.0 142.9 jit_solution(13918986971242170019)
XLA Ops:
  0.0 0.9 eq.38
  0.9 0.5 copy-done
  1.4 1.2 fusion.2.x_ref
  2.6 24.4 %exchange_0.1 = bf16[64,16,32]{2,1,0:T(8,128)(2,1)} custom-call(bf16[16,32]{1,0:T(8,128)(2,1)} %fusion.2.x_ref), custom_call_target="tpu_custom_call" | custom-call | bytes 131072 | tf_op jit(solution)/shard_map/exchange_0/pallas_call | solution.py:49
  27.1 1.1 convert_bitcast_fusion
  28.3 0.2 reshape.229
  28.8 0.8 convolution_convert_fusion.1.x_ref
  29.7 16.0 %exchange_1.1 = bf16[64,16,48]{2,1,0:T(8,128)(2,1)} custom-call(bf16[16,48]{1,0:T(8,128)(2,1)} %convolution_convert_fusion.1.x_ref), custom_call_target="tpu_custom_call" | custom-call | bytes 196608 | tf_op jit(solution)/shard_map/exchange_1/pallas_call | solution.py:49
  45.7 1.0 copy.39
  46.7 0.3 reshape.220
  47.9 1.4 select_reduce_fusion.1
  49.4 0.4 convolution_bitcast_fusion
  49.9 0.4 fusion.17
  50.7 0.7 maximum_maximum_fusion.1.refs_1_
  51.7 0.6 broadcast_in_dim.110
  52.8 1.4 select_reduce_fusion.2
  54.2 1.5 %fusion.20 = f32[4,128,512]{2,1,0:T(8,128)S(1)} fusion(bf16[4,128,512]{2,1,0:T(8,128)(2,1)} %param.16, f32[4,128,128]{1,2,0:T(8,128)S(1)} %get-tuple-element.18, f32[4,128]{1,0:T(4,128)S(1)} %get-tuple-element.17, pred[4,128]{1,0:T(4,128)(4,1)} %copy-done.8), kind=kOutput, calls=%fused_computation.38 | convolution fusion | flops 67305472 | bytes 1837568 | tf_op jit(solution)/shard_map/rqp,rpc->rqc/dot_general | solution.py:336
  55.7 1.8 %reshape.221 = f32[4,4,32,8,64]{4,3,2,1,0:T(8,128)} reshape(f32[4,128,512]{2,1,0:T(8,128)S(1)} %fusion.20) | data formatting | bytes 2097152 | tf_op jit(solution)/shard_map/reshape | solution.py:338
  57.5 2.3 %select_reduce_fusion = f32[4,4,32,64]{3,2,1,0:T(8,128)S(1)} fusion(f32[4,4,32,8,64]{4,3,2,1,0:T(8,128)} %reshape.221, pred[32,8]{1,0:T(8,128)(4,1)S(1)} %iota_compare_fusion.4), kind=kLoop, calls=%fused_computation | loop fusion | flops 491520 | bytes 1179904 | tf_op jit(solution)/shard_map/reduce_sum | solution.py:339
  60.4 0.9 maximum_maximum_fusion.refs_0_
  61.3 25.5 %two_phase_2.1 = bf16[64,8,64]{2,1,0:T(8,128)(2,1)} custom-call(f32[64,8,128]{2,1,0:T(8,128)} %maximum_maximum_fusion.refs_0_, f32[8,128]{1,0:T(8,128)} %maximum_maximum_fusion.1.refs_1_), custom_call_target="tpu_custom_call" | custom-call | bytes 655360 | tf_op jit(solution)/shard_map/two_phase_2/pallas_call | solution.py:183
  86.8 1.1 reshape.226
  87.9 0.8 convolution_convert_fusion.x_ref
  88.6 16.7 %exchange_3.1 = bf16[64,16,32]{2,1,0:T(8,128)(2,1)} custom-call(bf16[16,32]{1,0:T(8,128)(2,1)} %convolution_convert_fusion.x_ref), custom_call_target="tpu_custom_call" | custom-call | bytes 131072 | tf_op jit(solution)/shard_map/exchange_3/pallas_call | solution.py:49
  105.3 1.2 fusion.10
  107.0 1.3 fusion.47
  108.3 0.4 fusion.4
  108.9 1.1 copy.77
  110.0 0.7 constant_dynamic-slice_fusion.refs_1_
  110.7 30.3 %two_phase_4.1 = bf16[64,16,32]{2,1,0:T(8,128)(2,1)} custom-call(f32[64,16,32]{2,1,0:T(8,128)} %bitcast.48, f32[16,32]{1,0:T(8,128)} %constant_dynamic-slice_fusion.refs_1_), custom_call_target="tpu_custom_call" | custom-call | bytes 393216 | tf_op jit(solution)/shard_map/two_phase_4/pallas_call | solution.py:183
  141.0 1.0 copy.56
  142.0 0.9 reshape.228
  (69 shorter events, 3.8 us)
Async XLA Ops:
  0.0 1.4 copy-start
  2.6 26.2 %copy-start.6 = (bf16[2048]{0:T(1024)(128)(2,1)S(1)}, bf16[2048]{0:T(1024)(128)(2,1)}, u32[]{:S(2)}) copy-start(bf16[2048]{0:T(1024)(128)(2,1)} %param.17) | copy-start | bytes 12292
  2.6 26.2 %copy-start.4 = (bf16[2048,48]{0,1:T(8,128)(2,1)S(1)}, bf16[2048,48]{0,1:T(8,128)(2,1)}, u32[]{:S(2)}) copy-start(bf16[2048,48]{0,1:T(8,128)(2,1)} %param.19) | copy-start | bytes 589828
  27.1 1.5 %copy-start.1 = (bf16[64,16,32]{2,1,0:T(8,128)(2,1)S(1)}, bf16[64,16,32]{2,1,0:T(8,128)(2,1)}, u32[]{:S(2)}) copy-start(bf16[64,16,32]{2,1,0:T(8,128)(2,1)} %exchange_0.1) | copy-start | bytes 196612
  28.3 19.0 %copy-start.12 = (s32[4]{0:T(128)S(1)}, s32[4]{0:T(128)}, u32[]{:S(2)}) copy-start(s32[4]{0:T(128)} %param.13) | copy-start | bytes 52
  50.7 0.7 copy-start.10
  52.4 1.8 %copy-start.8 = (pred[4,128]{1,0:T(4,128)(4,1)}, pred[4,128]{1,0:T(4,128)(4,1)S(1)}, u32[]{:S(2)}) copy-start(pred[4,128]{1,0:T(4,128)(4,1)S(1)} %broadcast_compare_fusion) | copy-start | bytes 1540
  57.4 2.4 %copy-start.9 = (pred[4,128]{1,0:T(4,128)(4,1)S(1)}, pred[4,128]{1,0:T(4,128)(4,1)}, u32[]{:S(2)}) copy-start(pred[4,128]{1,0:T(4,128)(4,1)} %copy-done.8) | copy-start | bytes 1540
  57.5 3.0 %copy-start.11 = (f32[128]{0:T(128)S(1)}, f32[128]{0:T(128)}, u32[]{:S(2)}) copy-start(f32[128]{0:T(128)} %copy-done.10) | copy-start | bytes 1540
  59.8 28.1 %copy-start.5 = (bf16[2048,32]{0,1:T(8,128)(2,1)S(1)}, bf16[2048,32]{0,1:T(8,128)(2,1)}, u32[]{:S(2)}) copy-start(bf16[2048,32]{0,1:T(8,128)(2,1)} %param.20) | copy-start | bytes 393220
  105.3 1.7 %copy-start.7 = (bf16[2048]{0:T(1024)(128)(2,1)S(1)}, bf16[2048]{0:T(1024)(128)(2,1)}, u32[]{:S(2)}) copy-start(bf16[2048]{0:T(1024)(128)(2,1)} %param.18) | copy-start | bytes 12292
  106.5 1.8 %copy-start.2 = (bf16[128,2048]{1,0:T(8,128)(2,1)S(1)}, bf16[128,2048]{1,0:T(8,128)(2,1)}, u32[]{:S(2)}) copy-start(bf16[128,2048]{1,0:T(8,128)(2,1)} %param.23) | copy-start | bytes 1572868
  106.5 1.8 %copy-start.3 = (bf16[2048,128]{1,0:T(8,128)(2,1)S(1)}, bf16[2048,128]{1,0:T(8,128)(2,1)}, u32[]{:S(2)}) copy-start(bf16[2048,128]{1,0:T(8,128)(2,1)} %param.22) | copy-start | bytes 1572868

commit v10 on v7

--- a/solution.py
+++ b/solution.py
@@ -29,7 +29,6 @@
 def _exchange_kernel(n, gather, x_ref, o_ref, buf, send_sems, recv_sems, local_sem):
     me = lax.axis_index("seq")
     rep = lax.axis_index("rep")
-    _greet(n, me, rep)
     source = (lambda peer: x_ref) if gather else (lambda peer: x_ref.at[peer])
     _stage(n, me, lambda j: j, rep, source, buf, send_sems, recv_sems, local_sem)
     o_ref[...] = buf[...]
@@ -57,7 +56,7 @@
             pltpu.SemaphoreType.DMA(()),
             pltpu.SemaphoreType.DMA(()),
         ],
-        compiler_params=pltpu.CompilerParams(collective_id=cid, has_side_effects=True),
+        compiler_params=pltpu.CompilerParams(has_side_effects=True),
         cost_estimate=pl.CostEstimate(flops=0, transcendentals=0, bytes_accessed=2 * nbytes),
         name="exchange_%d" % cid,
     )(x)
@@ -155,7 +154,7 @@
             pltpu.SemaphoreType.DMA(()),
             pltpu.SemaphoreType.DMA(()),
         ],
-        compiler_params=pltpu.CompilerParams(collective_id=cid, has_side_effects=True),
+        compiler_params=pltpu.CompilerParams(has_side_effects=True),
         cost_estimate=pl.CostEstimate(flops=0, transcendentals=0, bytes_accessed=2 * nbytes),
         name="gather2_%d" % cid,
     )(x)
@@ -169,7 +168,6 @@
     buf1, own, buf2, s1, r1, l1, s2, r2, l2 = refs[2 + n_extra :]
     me = lax.axis_index("seq")
     rep = lax.axis_index("rep")
-    _greet(n, me, rep)
     _stage(n, me, lambda j: j, rep, lambda peer: x_ref.at[peer], buf1, s1, r1, l1)
     own[...] = combine(buf1, *extras)
     _stage(n, me, lambda j: j, rep, lambda peer: own, buf2, s2, r2, l2)
@@ -196,7 +194,7 @@
             pltpu.SemaphoreType.DMA(()),
             pltpu.SemaphoreType.DMA(()),
         ],
-        compiler_params=pltpu.CompilerParams(collective_id=cid, has_side_effects=True),
+        compiler_params=pltpu.CompilerParams(has_side_effects=True),
         cost_estimate=pl.CostEstimate(flops=0, transcendentals=0, bytes_accessed=2 * nbytes),
         name="two_phase_%d" % cid,
     )(x, *extras)

time: 143 us -> 189 us (1.32)
  Pallas kernels: 113 us -> 159 us
    pallas_call x3, Pallas kernels: 57.2 us -> 88.1 us  [exchange(): pl.pallas_call(functools.partial(_exchange_kernel, n, gather), out_shape=...]
    pallas_call x2, Pallas kernels: 55.9 us -> 70.9 us  [two_phase(): pl.pallas_call(functools.partial(_two_phase_kernel, n, combine, len(extra...]
where the time goes in v10:
time: 189 us; the launch traced here: 188 us
  Pallas kernels  159 us (84%)
  local copies, waits for them, and re-layouts  11.4 us (6%)
  matrix products  10.1 us (5%)
  other arithmetic  7.15 us (4%)
    pallas_call x3, Pallas kernels, exchange(): pl.pallas_call(functools.partial(_exchange_kernel, n, gather), out_shape=...  88.1 us
    pallas_call x2, Pallas kernels, two_phase(): pl.pallas_call(functools.partial(_two_phase_kernel, n, combine, len(extra...  70.9 us
    dot_general x2, matrix products, partial_softmax(): jnp.einsum('rskgd,rpkd->rskgp', queries, keys, preferred_element_type=jnp...  3.84 us

profile of v10, /device:TPU:1, one launch (start us, length us, event | category | flops | bytes accessed | tf_op | source)
XLA Modules:
  0.0 188.0 jit_solution(12066755845980355541)
XLA Ops:
  0.0 0.9 eq.15
  0.9 0.5 copy-done
  1.4 1.2 fusion.3.x_ref
  2.6 34.9 %exchange_0.1 = bf16[64,16,32]{2,1,0:T(8,128)(2,1)} custom-call(bf16[16,32]{1,0:T(8,128)(2,1)} %fusion.3.x_ref), custom_call_target="tpu_custom_call" | custom-call | bytes 131072 | tf_op jit(solution)/shard_map/exchange_0/pallas_call | solution.py:48
  37.6 1.1 convert_bitcast_fusion
  39.3 0.8 convolution_convert_fusion.1.x_ref
  40.2 25.6 %exchange_1.1 = bf16[64,16,48]{2,1,0:T(8,128)(2,1)} custom-call(bf16[16,48]{1,0:T(8,128)(2,1)} %convolution_convert_fusion.1.x_ref), custom_call_target="tpu_custom_call" | custom-call | bytes 196608 | tf_op jit(solution)/shard_map/exchange_1/pallas_call | solution.py:48
  65.7 1.0 copy.45
  66.7 0.3 reshape.156
  68.2 1.3 select_reduce_fusion
  69.6 0.4 convolution_bitcast_fusion.1
  70.2 1.3 fusion.15
  71.6 0.8 copy.60
  72.7 0.7 maximum_maximum_fusion.1.refs_1_
  73.4 0.7 broadcast_compare_fusion
  74.4 2.5 %select_reduce_fusion.1 = (f32[4,4,8,4]{3,1,2,0:T(4,128)}, f32[4,4,8,4,128]{4,3,1,2,0:T(4,128)}) fusion(pred[4,128]{1,0:T(4,128)(4,1)S(1)} %broadcast_compare_fusion, bf16[4,128,8,64,1]{1,3,4,2,0:T(8,128)(2,1)S(1)} %bitcast.68, bf16[4,4,8,4,64]{4,3,2,1,0:T(4,128)(2,1)} %copy-done.10), kind=kOutput, calls=%fused_computation.29 | convolution fusion | flops 8584704 | bytes 854528 | tf_op jit(solution)/shard_map/rskgd,rpkd->rskgp/dot_general | solution.py:251
  76.9 0.3 copy.49
  77.2 1.4 convolution_bitcast_fusion
  78.7 0.4 fusion.13
  79.5 0.9 maximum_maximum_fusion.refs_0_
  80.4 32.2 %two_phase_2.1 = bf16[64,8,64]{2,1,0:T(8,128)(2,1)} custom-call(f32[64,8,128]{2,1,0:T(8,128)} %maximum_maximum_fusion.refs_0_, f32[8,128]{1,0:T(8,128)} %maximum_maximum_fusion.1.refs_1_), custom_call_target="tpu_custom_call" | custom-call | bytes 655360 | tf_op jit(solution)/shard_map/two_phase_2/pallas_call | solution.py:181
  112.5 1.1 reshape.166
  113.6 0.8 convolution_convert_fusion.x_ref
  114.4 27.6 %exchange_3.1 = bf16[64,16,32]{2,1,0:T(8,128)(2,1)} custom-call(bf16[16,32]{1,0:T(8,128)(2,1)} %convolution_convert_fusion.x_ref), custom_call_target="tpu_custom_call" | custom-call | bytes 131072 | tf_op jit(solution)/shard_map/exchange_3/pallas_call | solution.py:48
  142.0 1.2 fusion.11
  143.7 1.3 fusion.44
  145.0 0.4 fusion.5
  145.6 1.1 copy.92
  146.7 0.7 constant_dynamic-slice_fusion.refs_1_
  147.3 38.7 %two_phase_4.1 = bf16[64,16,32]{2,1,0:T(8,128)(2,1)} custom-call(f32[64,16,32]{2,1,0:T(8,128)} %bitcast.62, f32[16,32]{1,0:T(8,128)} %constant_dynamic-slice_fusion.refs_1_), custom_call_target="tpu_custom_call" | custom-call | bytes 393216 | tf_op jit(solution)/shard_map/two_phase_4/pallas_call | solution.py:181
  186.1 1.0 copy.66
  187.1 0.9 reshape.168
  (70 shorter events, 3.6 us)
Async XLA Ops:
  0.0 1.4 copy-start
  2.6 36.7 %copy-start.12 = (bf16[2048]{0:T(1024)(128)(2,1)S(1)}, bf16[2048]{0:T(1024)(128)(2,1)}, u32[]{:S(2)}) copy-start(bf16[2048]{0:T(1024)(128)(2,1)} %param.17) | copy-start | bytes 12292
  2.6 36.7 %copy-start.9 = (bf16[2048,48]{0,1:T(8,128)(2,1)S(1)}, bf16[2048,48]{0,1:T(8,128)(2,1)}, u32[]{:S(2)}) copy-start(bf16[2048,48]{0,1:T(8,128)(2,1)} %param.19) | copy-start | bytes 589828
  37.6 1.5 copy-start.1
  38.8 28.5 %copy-start.14 = (s32[4]{0:T(128)S(1)}, s32[4]{0:T(128)}, u32[]{:S(2)}) copy-start(s32[4]{0:T(128)} %param.13) | copy-start | bytes 52
  67.9 1.7 copy-start.10
  68.1 6.0 %copy-start.4 = (bf16[4,128,512]{2,1,0:T(8,128)(2,1)S(1)}, bf16[4,128,512]{2,1,0:T(8,128)(2,1)}, u32[]{:S(2)}) copy-start(bf16[4,128,512]{2,1,0:T(8,128)(2,1)} %param.15) | copy-start | bytes 1572868
  69.5 0.6 copy-start.7
  70.2 6.8 %copy-start.5 = (bf16[4,128,512]{2,1,0:T(8,128)(2,1)S(1)}, bf16[4,128,512]{2,1,0:T(8,128)(2,1)}, u32[]{:S(2)}) copy-start(bf16[4,128,512]{2,1,0:T(8,128)(2,1)} %param.16) | copy-start | bytes 1572868
  76.9 1.8 copy-start.6
  76.9 1.8 copy-start.8
  78.7 34.9 %copy-start.11 = (bf16[2048,32]{0,1:T(8,128)(2,1)S(1)}, bf16[2048,32]{0,1:T(8,128)(2,1)}, u32[]{:S(2)}) copy-start(bf16[2048,32]{0,1:T(8,128)(2,1)} %param.20) | copy-start | bytes 393220
  142.0 1.7 copy-start.13
  143.2 1.8 copy-start.2
  143.2 1.8 copy-start.3

commit v11 on v7

--- a/solution.py
+++ b/solution.py
@@ -232,6 +232,11 @@
 def rms_scale(resid, gain):
     mean_square = jnp.mean(resid * resid, axis=-1, keepdims=True)
     return resid * lax.rsqrt(mean_square + norm_epsilon) * gain.astype(jnp.float32)
+
+
+def rms_columns(resid, gain):
+    mean_square = jnp.mean(resid * resid, axis=0, keepdims=True)
+    return resid * lax.rsqrt(mean_square + norm_epsilon) * gain.astype(jnp.float32)[:, None]
 
 
 def rotate(vectors, where):
@@ -292,18 +297,20 @@
         token_ids.reshape(-1)[:, None] == jnp.arange(vocab, dtype=jnp.int32)[None, :]
     ).astype(embed_table.dtype)
     picked = lax.dot_general(
-        onehot, embed_table, (((1,), (1,)), ((), ())), preferred_element_type=jnp.float32
+        embed_table, onehot, (((1,), (1,)), ((), ())), preferred_element_type=jnp.float32
     ).astype(embed_table.dtype)
     whole = exchange(picked, n, True, 0)
-    resid = jnp.transpose(whole, (1, 0, 2)).reshape(rows, width).astype(jnp.float32) * embed_factor
+    resid = whole.reshape(width, rows).astype(jnp.float32) * embed_factor
 
     slot_pos = place * ctx_own + jnp.arange(ctx_own, dtype=jnp.int32)
     cache_valid = (slot_pos[None, :] < cache_lengths[:, None]).reshape(req_all, 1, 1, 1, ctx_own)
     cache_keys = key_cache.reshape(req_all, ctx_own, KVH, HD)
     cache_values = value_cache.reshape(req_all, ctx_own, KVH, HD)
 
-    normed = rms_scale(resid, norm_attn).astype(jnp.bfloat16)
-    qkv_cols = jnp.dot(normed, w_qkv, preferred_element_type=jnp.float32).astype(jnp.bfloat16)
+    normed = rms_columns(resid, norm_attn).astype(jnp.bfloat16)
+    qkv_cols = lax.dot_general(
+        normed, w_qkv, (((0,), (0,)), ((), ())), preferred_element_type=jnp.float32
+    ).astype(jnp.bfloat16)
     qkv_got = exchange(qkv_cols, n, True, 1)
     qkv_all = jnp.transpose(qkv_got, (1, 0, 2)).reshape(req_all, steps, -1)
     where = (cache_lengths[:, None] + jnp.arange(steps, dtype=jnp.int32)[None, :]).astype(
@@ -356,20 +363,28 @@
         packed, [fresh_packed], _merge_combine, (pairs, HD), jnp.bfloat16, n, 2
     ).reshape(rows, att_width)
 
-    proj_cols = jnp.dot(attention, w_out, preferred_element_type=jnp.float32).astype(jnp.bfloat16)
-    proj_got = exchange(proj_cols, n, True, 3)
-    projected = jnp.transpose(proj_got, (1, 0, 2)).reshape(rows, width)
+    proj_cols = lax.dot_general(
+        w_out, attention, (((0,), (1,)), ((), ())), preferred_element_type=jnp.float32
+    ).astype(jnp.bfloat16)
+    projected = exchange(proj_cols, n, True, 3).reshape(width, rows)
     middle = resid + branch_factor * projected.astype(jnp.float32)
-    normed_mlp = rms_scale(middle, norm_mlp).astype(jnp.bfloat16)
-    gate = jnp.dot(normed_mlp, w_gate, preferred_element_type=jnp.float32)
-    upward = jnp.dot(normed_mlp, w_up, preferred_element_type=jnp.float32)
+    normed_mlp = rms_columns(middle, norm_mlp).astype(jnp.bfloat16)
+    gate = lax.dot_general(
+        normed_mlp, w_gate, (((0,), (0,)), ((), ())), preferred_element_type=jnp.float32
+    )
+    upward = lax.dot_general(
+        normed_mlp, w_up, (((0,), (0,)), ((), ())), preferred_element_type=jnp.float32
+    )
     hidden = (jax.nn.silu(gate) * upward).astype(jnp.bfloat16)
-    down_part = jnp.dot(hidden, w_down, preferred_element_type=jnp.float32)
+    down_part = lax.dot_general(
+        w_down, hidden, (((0,), (1,)), ((), ())), preferred_element_type=jnp.float32
+    )
     cols = width // n
-    middle_own = lax.dynamic_slice_in_dim(middle, place * cols, cols, axis=1)
-    down_send = jnp.transpose(down_part.reshape(rows, n, cols), (1, 0, 2))
-    out_got = two_phase(down_send, [middle_own], _down_combine, (rows, cols), jnp.bfloat16, n, 4)
-    return jnp.transpose(out_got, (1, 0, 2)).reshape(req_all, steps, width)
+    middle_own = lax.dynamic_slice_in_dim(middle, place * cols, cols, axis=0)
+    out_got = two_phase(
+        down_part.reshape(n, cols, rows), [middle_own], _down_combine, (cols, rows), jnp.bfloat16, n, 4
+    )
+    return jnp.transpose(out_got.reshape(width, rows), (1, 0)).reshape(req_all, steps, width)
 
 
 def solution(mesh):

time: 143 us -> 168 us (1.17)
  Pallas kernels: 113 us -> 141 us
  matrix products: 10.1 us -> 7.52 us
    pallas_call x2, Pallas kernels: 55.9 us -> 72.2 us  [two_phase(): pl.pallas_call(functools.partial(_two_phase_kernel, n, combine, len(extra...]
    pallas_call x3, Pallas kernels: 57.2 us -> 68.4 us  [exchange(): pl.pallas_call(functools.partial(_exchange_kernel, n, gather), out_shape=...]
where the time goes in v11:
time: 168 us
  Pallas kernels  141 us (84%)
  local copies, waits for them, and re-layouts  11.8 us (7%)
  matrix products  7.52 us (4%)
  other arithmetic  7.25 us (4%)
    pallas_call x2, Pallas kernels, two_phase(): pl.pallas_call(functools.partial(_two_phase_kernel, n, combine, len(extra...  72.2 us
    pallas_call x3, Pallas kernels, exchange(): pl.pallas_call(functools.partial(_exchange_kernel, n, gather), out_shape=...  68.4 us

profile of v11, /device:TPU:1, one launch (start us, length us, event | category | flops | bytes accessed | tf_op | source)
XLA Modules:
  0.0 167.6 jit_solution(5727364681282580362)
XLA Ops:
  0.0 0.9 eq.15
  0.9 0.5 copy-done
  1.4 0.6 fusion.4
  2.0 0.7 copy.69
  2.7 29.7 %exchange_0.1 = bf16[64,32,16]{2,1,0:T(8,128)(2,1)} custom-call(bf16[32,16]{1,0:T(8,128)(2,1)} %bitcast.83), custom_call_target="tpu_custom_call" | custom-call | bytes 131072 | tf_op jit(solution)/shard_map/exchange_0/pallas_call | solution.py:49
  32.5 1.3 fusion.7
  33.8 1.4 fusion.11
  35.2 0.9 convolution_convert_fusion.1.x_ref
  36.1 16.4 %exchange_1.1 = bf16[64,16,48]{2,1,0:T(8,128)(2,1)} custom-call(bf16[16,48]{1,0:T(8,128)(2,1)} %convolution_convert_fusion.1.x_ref), custom_call_target="tpu_custom_call" | custom-call | bytes 196608 | tf_op jit(solution)/shard_map/exchange_1/pallas_call | solution.py:49
  52.5 1.0 copy.70
  54.9 1.3 select_reduce_fusion
  56.3 0.4 convolution_bitcast_fusion.2
  56.8 0.4 fusion.15
  57.6 0.7 maximum_maximum_fusion.1.refs_1_
  58.6 1.3 select_reduce_fusion.1
  60.2 0.5 convolution_bitcast_fusion.1
  60.7 0.4 fusion.13
  61.5 0.9 maximum_maximum_fusion.refs_0_
  62.4 25.4 %two_phase_2.1 = bf16[64,8,64]{2,1,0:T(8,128)(2,1)} custom-call(f32[64,8,128]{2,1,0:T(8,128)} %maximum_maximum_fusion.refs_0_, f32[8,128]{1,0:T(8,128)} %maximum_maximum_fusion.1.refs_1_), custom_call_target="tpu_custom_call" | custom-call | bytes 655360 | tf_op jit(solution)/shard_map/two_phase_2/pallas_call | solution.py:183
  87.8 1.1 reshape.169
  89.0 0.7 copy.89
  89.7 22.4 %exchange_3.1 = bf16[64,32,16]{2,1,0:T(8,128)(2,1)} custom-call(bf16[32,16]{1,0:T(8,128)(2,1)} %bitcast.84), custom_call_target="tpu_custom_call" | custom-call | bytes 131072 | tf_op jit(solution)/shard_map/exchange_3/pallas_call | solution.py:49
  112.1 1.3 fusion.9
  113.6 0.5 copy-done.10
  114.1 0.4 copy-done.5
  114.5 0.6 fusion.42
  115.1 1.9 %convolution_bitcast_fusion = f32[2048,16]{0,1:T(8,128)S(1)} fusion(bf16[128,2048]{1,0:T(8,128)(2,1)S(1)} %copy-done.2, bf16[2048,128]{1,0:T(8,128)(2,1)} %param.22, f32[16,128]{1,0:T(8,128)S(1)} %fusion.42, f32[2048,16]{1,0:T(8,128)S(1)} %bitcast_add_fusion, f32[2048]{0:T(1024)S(1)} %convert_element_type.90, f32[16]{0:T(128)S(1)} %add_rsqrt_fusion), kind=kOutput, calls=%fused_computation | convolution fusion | flops 16887808 | bytes 1327168 | tf_op jit(solution)/shard_map/dot_general | solution.py:379
  116.9 1.3 copy.90
  118.3 0.6 constant_dynamic-slice_fusion.refs_1_
  118.9 46.8 %two_phase_4.1 = bf16[64,32,16]{2,1,0:T(8,128)(2,1)} custom-call(f32[64,32,16]{2,1,0:T(8,128)} %bitcast.74, f32[32,16]{1,0:T(8,128)} %constant_dynamic-slice_fusion.refs_1_), custom_call_target="tpu_custom_call" | custom-call | bytes 393216 | tf_op jit(solution)/shard_map/two_phase_4/pallas_call | solution.py:183
  165.7 1.2 copy.91
  166.9 0.7 reshape.172
  (61 shorter events, 3.2 us)
Async XLA Ops:
  0.0 1.4 copy-start
  0.0 33.8 %copy-start.9 = (bf16[2048]{0:T(1024)(128)(2,1)S(1)}, bf16[2048]{0:T(1024)(128)(2,1)}, u32[]{:S(2)}) copy-start(bf16[2048]{0:T(1024)(128)(2,1)} %param.17) | copy-start | bytes 12292
  1.4 33.8 %copy-start.6 = (bf16[2048,48]{0,1:T(8,128)(2,1)S(1)}, bf16[2048,48]{0,1:T(8,128)(2,1)}, u32[]{:S(2)}) copy-start(bf16[2048,48]{0,1:T(8,128)(2,1)} %param.19) | copy-start | bytes 589828
  33.8 20.2 %copy-start.11 = (s32[4]{0:T(128)S(1)}, s32[4]{0:T(128)}, u32[]{:S(2)}) copy-start(s32[4]{0:T(128)} %param.13) | copy-start | bytes 52
  54.6 1.7 %copy-start.7 = (bf16[4,4,8,4,64]{4,3,2,1,0:T(4,128)(2,1)}, bf16[4,4,8,4,64]{4,3,2,1,0:T(4,128)(2,1)S(1)}, u32[]{:S(2)}) copy-start(bf16[4,4,8,4,64]{4,3,2,1,0:T(4,128)(2,1)S(1)} %pad_maximum_fusion) | copy-start | bytes 196612
  54.8 3.5 %copy-start.3 = (bf16[4,128,512]{2,1,0:T(8,128)(2,1)S(1)}, bf16[4,128,512]{2,1,0:T(8,128)(2,1)}, u32[]{:S(2)}) copy-start(bf16[4,128,512]{2,1,0:T(8,128)(2,1)} %param.15) | copy-start | bytes 1572868
  56.8 3.1 %copy-start.4 = (bf16[4,128,512]{2,1,0:T(8,128)(2,1)S(1)}, bf16[4,128,512]{2,1,0:T(8,128)(2,1)}, u32[]{:S(2)}) copy-start(bf16[4,128,512]{2,1,0:T(8,128)(2,1)} %param.16) | copy-start | bytes 1572868
  60.7 28.1 %copy-start.8 = (bf16[2048,32]{0,1:T(8,128)(2,1)S(1)}, bf16[2048,32]{0,1:T(8,128)(2,1)}, u32[]{:S(2)}) copy-start(bf16[2048,32]{0,1:T(8,128)(2,1)} %param.20) | copy-start | bytes 393220
  61.2 50.9 %copy-start.1 = (bf16[64,32,16]{2,1,0:T(8,128)(2,1)S(1)}, bf16[64,32,16]{2,1,0:T(8,128)(2,1)}, u32[]{:S(2)}) copy-start(bf16[64,32,16]{2,1,0:T(8,128)(2,1)} %exchange_0.1) | copy-start | bytes 196612
  113.4 0.7 copy-start.10
  113.4 1.1 copy-start.5
  113.6 1.5 copy-start.2

commit v12 on v7

--- a/solution.py
+++ b/solution.py
@@ -26,13 +26,13 @@
     pl.semaphore_wait(barrier, n - 1)
 
 
-def _exchange_kernel(n, gather, x_ref, o_ref, buf, send_sems, recv_sems, local_sem):
+def _exchange_kernel(n, gather, x_ref, o_ref, send_sems, recv_sems, local_sem):
+    buf = o_ref
     me = lax.axis_index("seq")
     rep = lax.axis_index("rep")
     _greet(n, me, rep)
     source = (lambda peer: x_ref) if gather else (lambda peer: x_ref.at[peer])
     _stage(n, me, lambda j: j, rep, source, buf, send_sems, recv_sems, local_sem)
-    o_ref[...] = buf[...]
 
 
 def _nbytes(shape, dtype):
@@ -52,7 +52,6 @@
         in_specs=[pl.BlockSpec(memory_space=pltpu.VMEM)],
         out_specs=pl.BlockSpec(memory_space=pltpu.VMEM),
         scratch_shapes=[
-            pltpu.VMEM(shape, x.dtype),
             pltpu.SemaphoreType.DMA(()),
             pltpu.SemaphoreType.DMA(()),
             pltpu.SemaphoreType.DMA(()),
@@ -166,14 +165,14 @@
     x_ref = refs[0]
     extras = refs[1 : 1 + n_extra]
     o_ref = refs[1 + n_extra]
-    buf1, own, buf2, s1, r1, l1, s2, r2, l2 = refs[2 + n_extra :]
+    buf1, own, s1, r1, l1, s2, r2, l2 = refs[2 + n_extra :]
+    buf2 = o_ref
     me = lax.axis_index("seq")
     rep = lax.axis_index("rep")
     _greet(n, me, rep)
     _stage(n, me, lambda j: j, rep, lambda peer: x_ref.at[peer], buf1, s1, r1, l1)
     own[...] = combine(buf1, *extras)
     _stage(n, me, lambda j: j, rep, lambda peer: own, buf2, s2, r2, l2)
-    o_ref[...] = buf2[...]
 
 
 def two_phase(x, extras, combine, own_shape, own_dtype, n, cid):
@@ -188,7 +187,6 @@
         scratch_shapes=[
             pltpu.VMEM(first, x.dtype),
             pltpu.VMEM(tuple(own_shape), own_dtype),
-            pltpu.VMEM(shape, own_dtype),
             pltpu.SemaphoreType.DMA(()),
             pltpu.SemaphoreType.DMA(()),
             pltpu.SemaphoreType.DMA(()),

time: 143 us -> 143 us (level)
  no operation moved by 1% of the time
where the time goes in v12:
time: 143 us; the launch traced here: 142 us
  Pallas kernels  113 us (79%)
  local copies, waits for them, and re-layouts  11.4 us (8%)
  matrix products  10.1 us (7%)
  other arithmetic  7.15 us (5%)
    pallas_call x3, Pallas kernels, exchange(): pl.pallas_call(functools.partial(_exchange_kernel, n, gather), out_shape=...  57.1 us
    pallas_call x2, Pallas kernels, two_phase(): pl.pallas_call(functools.partial(_two_phase_kernel, n, combine, len(extra...  55.8 us
    dot_general x2, matrix products, partial_softmax(): jnp.einsum('rskgd,rpkd->rskgp', queries, keys, preferred_element_type=jnp...  3.84 us

profile of v12, /device:TPU:1, one launch (start us, length us, event | category | flops | bytes accessed | tf_op | source)
XLA Modules:
  0.0 142.0 jit_solution(2586794250404544036)
XLA Ops:
  0.0 0.9 eq.15
  0.9 0.5 copy-done
  1.4 1.2 fusion.3.x_ref
  2.6 24.4 %exchange_0.1 = bf16[64,16,32]{2,1,0:T(8,128)(2,1)} custom-call(bf16[16,32]{1,0:T(8,128)(2,1)} %fusion.3.x_ref), custom_call_target="tpu_custom_call" | custom-call | bytes 131072 | tf_op jit(solution)/shard_map/exchange_0/pallas_call | solution.py:49
  27.1 1.1 convert_bitcast_fusion
  28.8 0.8 convolution_convert_fusion.1.x_ref
  29.6 16.0 %exchange_1.1 = bf16[64,16,48]{2,1,0:T(8,128)(2,1)} custom-call(bf16[16,48]{1,0:T(8,128)(2,1)} %convolution_convert_fusion.1.x_ref), custom_call_target="tpu_custom_call" | custom-call | bytes 196608 | tf_op jit(solution)/shard_map/exchange_1/pallas_call | solution.py:49
  45.7 1.0 copy.45
  46.7 0.3 reshape.156
  48.1 1.3 select_reduce_fusion
  49.5 0.4 convolution_bitcast_fusion.1
  50.1 1.3 fusion.15
  51.5 0.8 copy.60
  52.7 0.7 maximum_maximum_fusion.1.refs_1_
  53.3 0.7 broadcast_compare_fusion
  54.1 0.3 copy.48
  54.3 2.5 %select_reduce_fusion.1 = (f32[4,4,8,4]{3,1,2,0:T(4,128)}, f32[4,4,8,4,128]{4,3,1,2,0:T(4,128)}) fusion(pred[4,128]{1,0:T(4,128)(4,1)S(1)} %broadcast_compare_fusion, bf16[4,128,8,64,1]{1,3,4,2,0:T(8,128)(2,1)S(1)} %bitcast.68, bf16[4,4,8,4,64]{4,3,2,1,0:T(4,128)(2,1)} %copy-done.10), kind=kOutput, calls=%fused_computation.29 | convolution fusion | flops 8584704 | bytes 854528 | tf_op jit(solution)/shard_map/rskgd,rpkd->rskgp/dot_general | solution.py:251
  57.1 1.4 convolution_bitcast_fusion
  58.7 0.4 fusion.13
  59.4 0.9 maximum_maximum_fusion.refs_0_
  60.3 25.4 %two_phase_2.1 = bf16[64,8,64]{2,1,0:T(8,128)(2,1)} custom-call(f32[64,8,128]{2,1,0:T(8,128)} %maximum_maximum_fusion.refs_0_, f32[8,128]{1,0:T(8,128)} %maximum_maximum_fusion.1.refs_1_), custom_call_target="tpu_custom_call" | custom-call | bytes 655360 | tf_op jit(solution)/shard_map/two_phase_2/pallas_call | solution.py:182
  85.7 1.1 reshape.166
  86.8 0.8 convolution_convert_fusion.x_ref
  87.6 16.6 %exchange_3.1 = bf16[64,16,32]{2,1,0:T(8,128)(2,1)} custom-call(bf16[16,32]{1,0:T(8,128)(2,1)} %convolution_convert_fusion.x_ref), custom_call_target="tpu_custom_call" | custom-call | bytes 131072 | tf_op jit(solution)/shard_map/exchange_3/pallas_call | solution.py:49
  104.2 1.2 fusion.11
  106.0 1.3 fusion.44
  107.2 0.4 fusion.5
  107.8 1.1 copy.92
  108.9 0.7 constant_dynamic-slice_fusion.refs_1_
  109.6 30.4 %two_phase_4.1 = bf16[64,16,32]{2,1,0:T(8,128)(2,1)} custom-call(f32[64,16,32]{2,1,0:T(8,128)} %bitcast.62, f32[16,32]{1,0:T(8,128)} %constant_dynamic-slice_fusion.refs_1_), custom_call_target="tpu_custom_call" | custom-call | bytes 393216 | tf_op jit(solution)/shard_map/two_phase_4/pallas_call | solution.py:182
  140.0 1.0 copy.66
  141.0 0.9 reshape.168
  (70 shorter events, 3.6 us)
Async XLA Ops:
  0.0 1.4 %copy-start = (bf16[32,24704]{1,0:T(8,128)(2,1)S(1)}, bf16[32,24704]{1,0:T(8,128)(2,1)}, u32[]{:S(2)}) copy-start(bf16[32,24704]{1,0:T(8,128)(2,1)} %param.14) | copy-start | bytes 4743172
  2.6 26.1 %copy-start.12 = (bf16[2048]{0:T(1024)(128)(2,1)S(1)}, bf16[2048]{0:T(1024)(128)(2,1)}, u32[]{:S(2)}) copy-start(bf16[2048]{0:T(1024)(128)(2,1)} %param.17) | copy-start | bytes 12292
  2.6 26.1 %copy-start.9 = (bf16[2048,48]{0,1:T(8,128)(2,1)S(1)}, bf16[2048,48]{0,1:T(8,128)(2,1)}, u32[]{:S(2)}) copy-start(bf16[2048,48]{0,1:T(8,128)(2,1)} %param.19) | copy-start | bytes 589828
  27.0 1.5 %copy-start.1 = (bf16[64,16,32]{2,1,0:T(8,128)(2,1)S(1)}, bf16[64,16,32]{2,1,0:T(8,128)(2,1)}, u32[]{:S(2)}) copy-start(bf16[64,16,32]{2,1,0:T(8,128)(2,1)} %exchange_0.1) | copy-start | bytes 196612
  28.3 19.0 %copy-start.14 = (s32[4]{0:T(128)S(1)}, s32[4]{0:T(128)}, u32[]{:S(2)}) copy-start(s32[4]{0:T(128)} %param.13) | copy-start | bytes 52
  47.8 1.7 %copy-start.10 = (bf16[4,4,8,4,64]{4,3,2,1,0:T(4,128)(2,1)}, bf16[4,4,8,4,64]{4,3,2,1,0:T(4,128)(2,1)S(1)}, u32[]{:S(2)}) copy-start(bf16[4,4,8,4,64]{4,3,2,1,0:T(4,128)(2,1)S(1)} %pad_maximum_fusion) | copy-start | bytes 196612
  48.0 6.0 %copy-start.4 = (bf16[4,128,512]{2,1,0:T(8,128)(2,1)S(1)}, bf16[4,128,512]{2,1,0:T(8,128)(2,1)}, u32[]{:S(2)}) copy-start(bf16[4,128,512]{2,1,0:T(8,128)(2,1)} %param.15) | copy-start | bytes 1572868
  49.4 0.6 copy-start.7
  50.1 6.8 %copy-start.5 = (bf16[4,128,512]{2,1,0:T(8,128)(2,1)S(1)}, bf16[4,128,512]{2,1,0:T(8,128)(2,1)}, u32[]{:S(2)}) copy-start(bf16[4,128,512]{2,1,0:T(8,128)(2,1)} %param.16) | copy-start | bytes 1572868
  56.9 1.8 %copy-start.6 = (f32[4,4,8,4,128]{4,3,1,2,0:T(4,128)S(1)}, f32[4,4,8,4,128]{4,3,1,2,0:T(4,128)}, u32[]{:S(2)}) copy-start(f32[4,4,8,4,128]{4,3,1,2,0:T(4,128)} %get-tuple-element.18) | copy-start | bytes 786436
  56.9 1.8 %copy-start.8 = (f32[4,4,8,4]{3,1,2,0:T(4,128)S(1)}, f32[4,4,8,4]{3,1,2,0:T(4,128)}, u32[]{:S(2)}) copy-start(f32[4,4,8,4]{3,1,2,0:T(4,128)} %get-tuple-element.17) | copy-start | bytes 6148
  58.6 28.2 %copy-start.11 = (bf16[2048,32]{0,1:T(8,128)(2,1)S(1)}, bf16[2048,32]{0,1:T(8,128)(2,1)}, u32[]{:S(2)}) copy-start(bf16[2048,32]{0,1:T(8,128)(2,1)} %param.20) | copy-start | bytes 393220
  104.2 1.7 %copy-start.13 = (bf16[2048]{0:T(1024)(128)(2,1)S(1)}, bf16[2048]{0:T(1024)(128)(2,1)}, u32[]{:S(2)}) copy-start(bf16[2048]{0:T(1024)(128)(2,1)} %param.18) | copy-start | bytes 12292
  105.5 1.8 %copy-start.2 = (bf16[128,2048]{1,0:T(8,128)(2,1)S(1)}, bf16[128,2048]{1,0:T(8,128)(2,1)}, u32[]{:S(2)}) copy-start(bf16[128,2048]{1,0:T(8,128)(2,1)} %param.23) | copy-start | bytes 1572868
  105.5 1.8 %copy-start.3 = (bf16[2048,128]{1,0:T(8,128)(2,1)S(1)}, bf16[2048,128]{1,0:T(8,128)(2,1)}, u32[]{:S(2)}) copy-start(bf16[2048,128]{1,0:T(8,128)(2,1)} %param.22) | copy-start | bytes 1572868

commit v13 on v9

--- a/solution.py
+++ b/solution.py
@@ -26,13 +26,13 @@
     pl.semaphore_wait(barrier, n - 1)
 
 
-def _exchange_kernel(n, gather, x_ref, o_ref, buf, send_sems, recv_sems, local_sem):
+def _exchange_kernel(n, gather, x_ref, o_ref, send_sems, recv_sems, local_sem):
+    buf = o_ref
     me = lax.axis_index("seq")
     rep = lax.axis_index("rep")
     _greet(n, me, rep)
     source = (lambda peer: x_ref) if gather else (lambda peer: x_ref.at[peer])
     _stage(n, me, lambda j: j, rep, source, buf, send_sems, recv_sems, local_sem)
-    o_ref[...] = buf[...]
 
 
 def _nbytes(shape, dtype):
@@ -52,7 +52,6 @@
         in_specs=[pl.BlockSpec(memory_space=pltpu.VMEM)],
         out_specs=pl.BlockSpec(memory_space=pltpu.VMEM),
         scratch_shapes=[
-            pltpu.VMEM(shape, x.dtype),
             pltpu.SemaphoreType.DMA(()),
             pltpu.SemaphoreType.DMA(()),
             pltpu.SemaphoreType.DMA(()),
@@ -166,14 +165,14 @@
     x_ref = refs[0]
     extras = refs[1 : 1 + n_extra]
     o_ref = refs[1 + n_extra]
-    buf1, own, buf2, s1, r1, l1, s2, r2, l2 = refs[2 + n_extra :]
+    buf1, own, s1, r1, l1, s2, r2, l2 = refs[2 + n_extra :]
+    buf2 = o_ref
     me = lax.axis_index("seq")
     rep = lax.axis_index("rep")
     _greet(n, me, rep)
     _stage(n, me, lambda j: j, rep, lambda peer: x_ref.at[peer], buf1, s1, r1, l1)
     own[...] = combine(buf1, *extras)
     _stage(n, me, lambda j: j, rep, lambda peer: own, buf2, s2, r2, l2)
-    o_ref[...] = buf2[...]
 
 
 def two_phase(x, extras, combine, own_shape, own_dtype, n, cid):
@@ -188,7 +187,6 @@
         scratch_shapes=[
             pltpu.VMEM(first, x.dtype),
             pltpu.VMEM(tuple(own_shape), own_dtype),
-            pltpu.VMEM(shape, own_dtype),
             pltpu.SemaphoreType.DMA(()),
             pltpu.SemaphoreType.DMA(()),
             pltpu.SemaphoreType.DMA(()),

time: 144 us -> 143 us (level)
  no operation moved by 1% of the time
where the time goes in v13:
time: 143 us
  Pallas kernels  113 us (79%)
  local copies, waits for them, and re-layouts  12.9 us (9%)
  matrix products  9.07 us (6%)
  other arithmetic  7.65 us (5%)
    pallas_call x3, Pallas kernels, exchange(): pl.pallas_call(functools.partial(_exchange_kernel, n, gather), out_shape=...  57 us
    pallas_call x2, Pallas kernels, two_phase(): pl.pallas_call(functools.partial(_two_phase_kernel, n, combine, len(extra...  55.8 us

profile of v13, /device:TPU:1, one launch (start us, length us, event | category | flops | bytes accessed | tf_op | source)
XLA Modules:
  0.0 142.8 jit_solution(17640582806539571708)
XLA Ops:
  0.0 0.9 eq.38
  0.9 0.5 copy-done
  1.4 1.2 fusion.2.x_ref
  2.6 24.4 %exchange_0.1 = bf16[64,16,32]{2,1,0:T(8,128)(2,1)} custom-call(bf16[16,32]{1,0:T(8,128)(2,1)} %fusion.2.x_ref), custom_call_target="tpu_custom_call" | custom-call | bytes 131072 | tf_op jit(solution)/shard_map/exchange_0/pallas_call | solution.py:49
  27.0 1.1 convert_bitcast_fusion
  28.3 0.2 reshape.229
  28.8 0.8 convolution_convert_fusion.1.x_ref
  29.6 16.0 %exchange_1.1 = bf16[64,16,48]{2,1,0:T(8,128)(2,1)} custom-call(bf16[16,48]{1,0:T(8,128)(2,1)} %convolution_convert_fusion.1.x_ref), custom_call_target="tpu_custom_call" | custom-call | bytes 196608 | tf_op jit(solution)/shard_map/exchange_1/pallas_call | solution.py:49
  45.6 1.0 copy.39
  46.6 0.3 reshape.220
  47.9 1.4 select_reduce_fusion.1
  49.3 0.4 convolution_bitcast_fusion
  49.8 0.4 fusion.17
  50.6 0.7 maximum_maximum_fusion.1.refs_1_
  51.6 0.6 broadcast_in_dim.110
  52.7 1.4 select_reduce_fusion.2
  54.1 1.5 %fusion.20 = f32[4,128,512]{2,1,0:T(8,128)S(1)} fusion(bf16[4,128,512]{2,1,0:T(8,128)(2,1)} %param.16, f32[4,128,128]{1,2,0:T(8,128)S(1)} %get-tuple-element.18, f32[4,128]{1,0:T(4,128)S(1)} %get-tuple-element.17, pred[4,128]{1,0:T(4,128)(4,1)} %copy-done.8), kind=kOutput, calls=%fused_computation.38 | convolution fusion | flops 67305472 | bytes 1837568 | tf_op jit(solution)/shard_map/rqp,rpc->rqc/dot_general | solution.py:334
  55.6 1.8 %reshape.221 = f32[4,4,32,8,64]{4,3,2,1,0:T(8,128)} reshape(f32[4,128,512]{2,1,0:T(8,128)S(1)} %fusion.20) | data formatting | bytes 2097152 | tf_op jit(solution)/shard_map/reshape | solution.py:336
  57.4 2.3 %select_reduce_fusion = f32[4,4,32,64]{3,2,1,0:T(8,128)S(1)} fusion(f32[4,4,32,8,64]{4,3,2,1,0:T(8,128)} %reshape.221, pred[32,8]{1,0:T(8,128)(4,1)S(1)} %iota_compare_fusion.4), kind=kLoop, calls=%fused_computation | loop fusion | flops 491520 | bytes 1179904 | tf_op jit(solution)/shard_map/reduce_sum | solution.py:337
  60.3 0.9 maximum_maximum_fusion.refs_0_
  61.2 25.4 %two_phase_2.1 = bf16[64,8,64]{2,1,0:T(8,128)(2,1)} custom-call(f32[64,8,128]{2,1,0:T(8,128)} %maximum_maximum_fusion.refs_0_, f32[8,128]{1,0:T(8,128)} %maximum_maximum_fusion.1.refs_1_), custom_call_target="tpu_custom_call" | custom-call | bytes 655360 | tf_op jit(solution)/shard_map/two_phase_2/pallas_call | solution.py:182
  86.7 1.1 reshape.226
  87.8 0.8 convolution_convert_fusion.x_ref
  88.5 16.6 %exchange_3.1 = bf16[64,16,32]{2,1,0:T(8,128)(2,1)} custom-call(bf16[16,32]{1,0:T(8,128)(2,1)} %convolution_convert_fusion.x_ref), custom_call_target="tpu_custom_call" | custom-call | bytes 131072 | tf_op jit(solution)/shard_map/exchange_3/pallas_call | solution.py:49
  105.2 1.2 fusion.10
  106.9 1.3 fusion.47
  108.2 0.4 fusion.4
  108.7 1.1 copy.77
  109.8 0.7 constant_dynamic-slice_fusion.refs_1_
  110.5 30.3 %two_phase_4.1 = bf16[64,16,32]{2,1,0:T(8,128)(2,1)} custom-call(f32[64,16,32]{2,1,0:T(8,128)} %bitcast.48, f32[16,32]{1,0:T(8,128)} %constant_dynamic-slice_fusion.refs_1_), custom_call_target="tpu_custom_call" | custom-call | bytes 393216 | tf_op jit(solution)/shard_map/two_phase_4/pallas_call | solution.py:182
  140.9 1.0 copy.56
  141.9 0.9 reshape.228
  (69 shorter events, 3.8 us)
Async XLA Ops:
  0.0 1.4 copy-start
  2.6 26.1 %copy-start.6 = (bf16[2048]{0:T(1024)(128)(2,1)S(1)}, bf16[2048]{0:T(1024)(128)(2,1)}, u32[]{:S(2)}) copy-start(bf16[2048]{0:T(1024)(128)(2,1)} %param.17) | copy-start | bytes 12292
  2.6 26.1 %copy-start.4 = (bf16[2048,48]{0,1:T(8,128)(2,1)S(1)}, bf16[2048,48]{0,1:T(8,128)(2,1)}, u32[]{:S(2)}) copy-start(bf16[2048,48]{0,1:T(8,128)(2,1)} %param.19) | copy-start | bytes 589828
  27.0 1.5 %copy-start.1 = (bf16[64,16,32]{2,1,0:T(8,128)(2,1)S(1)}, bf16[64,16,32]{2,1,0:T(8,128)(2,1)}, u32[]{:S(2)}) copy-start(bf16[64,16,32]{2,1,0:T(8,128)(2,1)} %exchange_0.1) | copy-start | bytes 196612
  28.3 18.9 %copy-start.12 = (s32[4]{0:T(128)S(1)}, s32[4]{0:T(128)}, u32[]{:S(2)}) copy-start(s32[4]{0:T(128)} %param.13) | copy-start | bytes 52
  50.6 0.7 copy-start.10
  52.3 1.8 %copy-start.8 = (pred[4,128]{1,0:T(4,128)(4,1)}, pred[4,128]{1,0:T(4,128)(4,1)S(1)}, u32[]{:S(2)}) copy-start(pred[4,128]{1,0:T(4,128)(4,1)S(1)} %broadcast_compare_fusion) | copy-start | bytes 1540
  57.4 2.4 %copy-start.9 = (pred[4,128]{1,0:T(4,128)(4,1)S(1)}, pred[4,128]{1,0:T(4,128)(4,1)}, u32[]{:S(2)}) copy-start(pred[4,128]{1,0:T(4,128)(4,1)} %copy-done.8) | copy-start | bytes 1540
  57.4 3.0 %copy-start.11 = (f32[128]{0:T(128)S(1)}, f32[128]{0:T(128)}, u32[]{:S(2)}) copy-start(f32[128]{0:T(128)} %copy-done.10) | copy-start | bytes 1540
  59.7 28.0 %copy-start.5 = (bf16[2048,32]{0,1:T(8,128)(2,1)S(1)}, bf16[2048,32]{0,1:T(8,128)(2,1)}, u32[]{:S(2)}) copy-start(bf16[2048,32]{0,1:T(8,128)(2,1)} %param.20) | copy-start | bytes 393220
  105.2 1.7 %copy-start.7 = (bf16[2048]{0:T(1024)(128)(2,1)S(1)}, bf16[2048]{0:T(1024)(128)(2,1)}, u32[]{:S(2)}) copy-start(bf16[2048]{0:T(1024)(128)(2,1)} %param.18) | copy-start | bytes 12292
  106.4 1.8 %copy-start.2 = (bf16[128,2048]{1,0:T(8,128)(2,1)S(1)}, bf16[128,2048]{1,0:T(8,128)(2,1)}, u32[]{:S(2)}) copy-start(bf16[128,2048]{1,0:T(8,128)(2,1)} %param.23) | copy-start | bytes 1572868
  106.4 1.8 %copy-start.3 = (bf16[2048,128]{1,0:T(8,128)(2,1)S(1)}, bf16[2048,128]{1,0:T(8,128)(2,1)}, u32[]{:S(2)}) copy-start(bf16[2048,128]{1,0:T(8,128)(2,1)} %param.22) | copy-start | bytes 1572868

commit v14 on v12

--- a/solution.py
+++ b/solution.py
@@ -81,12 +81,15 @@
             device_id_type=MESH_ID,
         )
 
-    def send(k, carry):
+    half = m // 2
+
+    def send(t, carry):
+        k = half + ((t + 1) // 2) * (2 * (t % 2) - 1)
         j = lax.rem(mine + k, m)
         copy(j, mine).start()
         return carry
 
-    lax.fori_loop(1, m, send, 0)
+    lax.fori_loop(0, m - 1, send, 0)
     local = pltpu.make_async_copy(source(mine), buf.at[mine], local_sem)
     local.start()
     rest = buf.at[pl.ds(0, m - 1)]

time: 143 us -> 142 us (level)
  no operation moved by 1% of the time
where the time goes in v14:
time: 142 us
  Pallas kernels  113 us (80%)
  local copies, waits for them, and re-layouts  11.4 us (8%)
  matrix products  10.1 us (7%)
  other arithmetic  7.15 us (5%)
    pallas_call x3, Pallas kernels, exchange(): pl.pallas_call(functools.partial(_exchange_kernel, n, gather), out_shape=...  57.7 us
    pallas_call x2, Pallas kernels, two_phase(): pl.pallas_call(functools.partial(_two_phase_kernel, n, combine, len(extra...  55.1 us
    dot_general x2, matrix products, partial_softmax(): jnp.einsum('rskgd,rpkd->rskgp', queries, keys, preferred_element_type=jnp...  3.84 us

profile of v14, /device:TPU:1, one launch (start us, length us, event | category | flops | bytes accessed | tf_op | source)
XLA Modules:
  0.0 141.8 jit_solution(3767303981078026927)
XLA Ops:
  0.0 0.9 eq.15
  0.9 0.5 copy-done
  1.4 1.2 fusion.3.x_ref
  2.6 24.3 %exchange_0.1 = bf16[64,16,32]{2,1,0:T(8,128)(2,1)} custom-call(bf16[16,32]{1,0:T(8,128)(2,1)} %fusion.3.x_ref), custom_call_target="tpu_custom_call" | custom-call | bytes 131072 | tf_op jit(solution)/shard_map/exchange_0/pallas_call | solution.py:49
  27.0 1.1 convert_bitcast_fusion
  28.8 0.8 convolution_convert_fusion.1.x_ref
  29.6 16.1 %exchange_1.1 = bf16[64,16,48]{2,1,0:T(8,128)(2,1)} custom-call(bf16[16,48]{1,0:T(8,128)(2,1)} %convolution_convert_fusion.1.x_ref), custom_call_target="tpu_custom_call" | custom-call | bytes 196608 | tf_op jit(solution)/shard_map/exchange_1/pallas_call | solution.py:49
  45.7 1.0 copy.45
  46.7 0.3 reshape.156
  48.1 1.3 select_reduce_fusion
  49.5 0.4 convolution_bitcast_fusion.1
  50.2 1.3 fusion.15
  51.5 0.8 copy.60
  52.7 0.7 maximum_maximum_fusion.1.refs_1_
  53.4 0.7 broadcast_compare_fusion
  54.4 2.5 %select_reduce_fusion.1 = (f32[4,4,8,4]{3,1,2,0:T(4,128)}, f32[4,4,8,4,128]{4,3,1,2,0:T(4,128)}) fusion(pred[4,128]{1,0:T(4,128)(4,1)S(1)} %broadcast_compare_fusion, bf16[4,128,8,64,1]{1,3,4,2,0:T(8,128)(2,1)S(1)} %bitcast.68, bf16[4,4,8,4,64]{4,3,2,1,0:T(4,128)(2,1)} %copy-done.10), kind=kOutput, calls=%fused_computation.29 | convolution fusion | flops 8584704 | bytes 854528 | tf_op jit(solution)/shard_map/rskgd,rpkd->rskgp/dot_general | solution.py:254
  56.9 0.3 copy.49
  57.2 1.4 %convolution_bitcast_fusion = f32[4,4,8,4,64]{4,3,1,2,0:T(4,128)S(1)} fusion(bf16[4,128,8,64,1]{1,3,4,2,0:T(8,128)(2,1)S(1)} %bitcast.69, f32[4,4,8,4,128]{4,3,1,2,0:T(4,128)} %get-tuple-element.18, f32[4,4,8,4]{3,1,2,0:T(4,128)} %get-tuple-element.17, pred[4,128]{1,0:T(4,128)(4,1)S(1)} %broadcast_compare_fusion), kind=kOutput, calls=%fused_computation.4 | convolution fusion | flops 8585216 | bytes 920064 | tf_op jit(solution)/shard_map/rskgp,rpkd->rskgd/dot_general | solution.py:260
  58.7 0.4 fusion.13
  59.4 0.9 maximum_maximum_fusion.refs_0_
  60.3 24.0 %two_phase_2.1 = bf16[64,8,64]{2,1,0:T(8,128)(2,1)} custom-call(f32[64,8,128]{2,1,0:T(8,128)} %maximum_maximum_fusion.refs_0_, f32[8,128]{1,0:T(8,128)} %maximum_maximum_fusion.1.refs_1_), custom_call_target="tpu_custom_call" | custom-call | bytes 655360 | tf_op jit(solution)/shard_map/two_phase_2/pallas_call | solution.py:185
  84.3 1.1 reshape.166
  85.4 0.8 convolution_convert_fusion.x_ref
  86.2 17.2 %exchange_3.1 = bf16[64,16,32]{2,1,0:T(8,128)(2,1)} custom-call(bf16[16,32]{1,0:T(8,128)(2,1)} %convolution_convert_fusion.x_ref), custom_call_target="tpu_custom_call" | custom-call | bytes 131072 | tf_op jit(solution)/shard_map/exchange_3/pallas_call | solution.py:49
  103.4 1.2 fusion.11
  105.1 1.3 fusion.44
  106.4 0.4 fusion.5
  107.0 1.1 copy.92
  108.1 0.7 constant_dynamic-slice_fusion.refs_1_
  108.8 31.1 %two_phase_4.1 = bf16[64,16,32]{2,1,0:T(8,128)(2,1)} custom-call(f32[64,16,32]{2,1,0:T(8,128)} %bitcast.62, f32[16,32]{1,0:T(8,128)} %constant_dynamic-slice_fusion.refs_1_), custom_call_target="tpu_custom_call" | custom-call | bytes 393216 | tf_op jit(solution)/shard_map/two_phase_4/pallas_call | solution.py:185
  139.9 1.0 copy.66
  140.9 0.9 reshape.168
  (70 shorter events, 3.6 us)
Async XLA Ops:
  0.0 1.4 %copy-start = (bf16[32,24704]{1,0:T(8,128)(2,1)S(1)}, bf16[32,24704]{1,0:T(8,128)(2,1)}, u32[]{:S(2)}) copy-start(bf16[32,24704]{1,0:T(8,128)(2,1)} %param.14) | copy-start | bytes 4743172
  2.6 26.1 %copy-start.12 = (bf16[2048]{0:T(1024)(128)(2,1)S(1)}, bf16[2048]{0:T(1024)(128)(2,1)}, u32[]{:S(2)}) copy-start(bf16[2048]{0:T(1024)(128)(2,1)} %param.17) | copy-start | bytes 12292
  2.6 26.1 %copy-start.9 = (bf16[2048,48]{0,1:T(8,128)(2,1)S(1)}, bf16[2048,48]{0,1:T(8,128)(2,1)}, u32[]{:S(2)}) copy-start(bf16[2048,48]{0,1:T(8,128)(2,1)} %param.19) | copy-start | bytes 589828
  27.0 1.5 %copy-start.1 = (bf16[64,16,32]{2,1,0:T(8,128)(2,1)S(1)}, bf16[64,16,32]{2,1,0:T(8,128)(2,1)}, u32[]{:S(2)}) copy-start(bf16[64,16,32]{2,1,0:T(8,128)(2,1)} %exchange_0.1) | copy-start | bytes 196612
  28.2 19.0 %copy-start.14 = (s32[4]{0:T(128)S(1)}, s32[4]{0:T(128)}, u32[]{:S(2)}) copy-start(s32[4]{0:T(128)} %param.13) | copy-start | bytes 52
  47.8 1.7 %copy-start.10 = (bf16[4,4,8,4,64]{4,3,2,1,0:T(4,128)(2,1)}, bf16[4,4,8,4,64]{4,3,2,1,0:T(4,128)(2,1)S(1)}, u32[]{:S(2)}) copy-start(bf16[4,4,8,4,64]{4,3,2,1,0:T(4,128)(2,1)S(1)} %pad_maximum_fusion) | copy-start | bytes 196612
  48.0 6.0 %copy-start.4 = (bf16[4,128,512]{2,1,0:T(8,128)(2,1)S(1)}, bf16[4,128,512]{2,1,0:T(8,128)(2,1)}, u32[]{:S(2)}) copy-start(bf16[4,128,512]{2,1,0:T(8,128)(2,1)} %param.15) | copy-start | bytes 1572868
  49.4 0.6 copy-start.7
  50.1 6.8 %copy-start.5 = (bf16[4,128,512]{2,1,0:T(8,128)(2,1)S(1)}, bf16[4,128,512]{2,1,0:T(8,128)(2,1)}, u32[]{:S(2)}) copy-start(bf16[4,128,512]{2,1,0:T(8,128)(2,1)} %param.16) | copy-start | bytes 1572868
  56.9 1.8 %copy-start.6 = (f32[4,4,8,4,128]{4,3,1,2,0:T(4,128)S(1)}, f32[4,4,8,4,128]{4,3,1,2,0:T(4,128)}, u32[]{:S(2)}) copy-start(f32[4,4,8,4,128]{4,3,1,2,0:T(4,128)} %get-tuple-element.18) | copy-start | bytes 786436
  56.9 1.8 %copy-start.8 = (f32[4,4,8,4]{3,1,2,0:T(4,128)S(1)}, f32[4,4,8,4]{3,1,2,0:T(4,128)}, u32[]{:S(2)}) copy-start(f32[4,4,8,4]{3,1,2,0:T(4,128)} %get-tuple-element.17) | copy-start | bytes 6148
  58.7 26.7 %copy-start.11 = (bf16[2048,32]{0,1:T(8,128)(2,1)S(1)}, bf16[2048,32]{0,1:T(8,128)(2,1)}, u32[]{:S(2)}) copy-start(bf16[2048,32]{0,1:T(8,128)(2,1)} %param.20) | copy-start | bytes 393220
  103.4 1.7 %copy-start.13 = (bf16[2048]{0:T(1024)(128)(2,1)S(1)}, bf16[2048]{0:T(1024)(128)(2,1)}, u32[]{:S(2)}) copy-start(bf16[2048]{0:T(1024)(128)(2,1)} %param.18) | copy-start | bytes 12292
  104.6 1.8 %copy-start.2 = (bf16[128,2048]{1,0:T(8,128)(2,1)S(1)}, bf16[128,2048]{1,0:T(8,128)(2,1)}, u32[]{:S(2)}) copy-start(bf16[128,2048]{1,0:T(8,128)(2,1)} %param.23) | copy-start | bytes 1572868
  104.6 1.8 %copy-start.3 = (bf16[2048,128]{1,0:T(8,128)(2,1)S(1)}, bf16[2048,128]{1,0:T(8,128)(2,1)}, u32[]{:S(2)}) copy-start(bf16[2048,128]{1,0:T(8,128)(2,1)} %param.22) | copy-start | bytes 1572868

commit v15 on v14

--- a/solution.py
+++ b/solution.py
@@ -17,12 +17,15 @@
 def _greet(n, me, rep):
     barrier = pltpu.get_barrier_semaphore()
 
-    def greet(k, carry):
+    half = n // 2
+
+    def greet(t, carry):
+        k = half + ((t + 1) // 2) * (2 * (t % 2) - 1)
         peer = lax.rem(me + k, n)
         pl.semaphore_signal(barrier, inc=1, device_id=(peer, rep), device_id_type=MESH_ID)
         return carry
 
-    lax.fori_loop(1, n, greet, 0)
+    lax.fori_loop(0, n - 1, greet, 0)
     pl.semaphore_wait(barrier, n - 1)
 
 

time: 142 us -> 145 us (1.021)
  Pallas kernels: 113 us -> 115 us
    pallas_call x2, Pallas kernels: 55.1 us -> 56.9 us  [two_phase(): pl.pallas_call(functools.partial(_two_phase_kernel, n, combine, len(extra...]
where the time goes in v15:
time: 145 us; the launch traced here: 144 us
  Pallas kernels  115 us (79%)
  local copies, waits for them, and re-layouts  11.4 us (8%)
  matrix products  10.1 us (7%)
  other arithmetic  7.15 us (5%)
    pallas_call x3, Pallas kernels, exchange(): pl.pallas_call(functools.partial(_exchange_kernel, n, gather), out_shape=...  58.5 us
    pallas_call x2, Pallas kernels, two_phase(): pl.pallas_call(functools.partial(_two_phase_kernel, n, combine, len(extra...  56.9 us
    dot_general x2, matrix products, partial_softmax(): jnp.einsum('rskgd,rpkd->rskgp', queries, keys, preferred_element_type=jnp...  3.84 us

profile of v15, /device:TPU:1, one launch (start us, length us, event | category | flops | bytes accessed | tf_op | source)
XLA Modules:
  0.0 144.5 jit_solution(953232527386607279)
XLA Ops:
  0.0 0.9 eq.15
  0.9 0.5 copy-done
  1.4 1.2 fusion.3.x_ref
  2.6 24.8 %exchange_0.1 = bf16[64,16,32]{2,1,0:T(8,128)(2,1)} custom-call(bf16[16,32]{1,0:T(8,128)(2,1)} %fusion.3.x_ref), custom_call_target="tpu_custom_call" | custom-call | bytes 131072 | tf_op jit(solution)/shard_map/exchange_0/pallas_call | solution.py:52
  27.5 1.1 convert_bitcast_fusion
  29.2 0.8 convolution_convert_fusion.1.x_ref
  30.1 16.6 %exchange_1.1 = bf16[64,16,48]{2,1,0:T(8,128)(2,1)} custom-call(bf16[16,48]{1,0:T(8,128)(2,1)} %convolution_convert_fusion.1.x_ref), custom_call_target="tpu_custom_call" | custom-call | bytes 196608 | tf_op jit(solution)/shard_map/exchange_1/pallas_call | solution.py:52
  46.7 1.0 copy.45
  47.7 0.3 reshape.156
  49.1 1.3 select_reduce_fusion
  50.5 0.4 convolution_bitcast_fusion.1
  51.1 1.3 fusion.15
  52.5 0.8 copy.60
  53.7 0.7 maximum_maximum_fusion.1.refs_1_
  54.3 0.7 broadcast_compare_fusion
  55.1 0.3 copy.48
  55.4 2.5 %select_reduce_fusion.1 = (f32[4,4,8,4]{3,1,2,0:T(4,128)}, f32[4,4,8,4,128]{4,3,1,2,0:T(4,128)}) fusion(pred[4,128]{1,0:T(4,128)(4,1)S(1)} %broadcast_compare_fusion, bf16[4,128,8,64,1]{1,3,4,2,0:T(8,128)(2,1)S(1)} %bitcast.68, bf16[4,4,8,4,64]{4,3,2,1,0:T(4,128)(2,1)} %copy-done.10), kind=kOutput, calls=%fused_computation.29 | convolution fusion | flops 8584704 | bytes 854528 | tf_op jit(solution)/shard_map/rskgd,rpkd->rskgp/dot_general | solution.py:257
  58.2 1.4 convolution_bitcast_fusion
  59.7 0.4 fusion.13
  60.4 0.9 maximum_maximum_fusion.refs_0_
  61.3 25.8 %two_phase_2.1 = bf16[64,8,64]{2,1,0:T(8,128)(2,1)} custom-call(f32[64,8,128]{2,1,0:T(8,128)} %maximum_maximum_fusion.refs_0_, f32[8,128]{1,0:T(8,128)} %maximum_maximum_fusion.1.refs_1_), custom_call_target="tpu_custom_call" | custom-call | bytes 655360 | tf_op jit(solution)/shard_map/two_phase_2/pallas_call | solution.py:188
  87.2 1.1 reshape.166
  88.2 0.8 convolution_convert_fusion.x_ref
  89.0 17.1 %exchange_3.1 = bf16[64,16,32]{2,1,0:T(8,128)(2,1)} custom-call(bf16[16,32]{1,0:T(8,128)(2,1)} %convolution_convert_fusion.x_ref), custom_call_target="tpu_custom_call" | custom-call | bytes 131072 | tf_op jit(solution)/shard_map/exchange_3/pallas_call | solution.py:52
  106.1 1.2 fusion.11
  107.8 1.3 fusion.44
  109.1 0.4 fusion.5
  109.7 1.1 copy.92
  110.8 0.7 constant_dynamic-slice_fusion.refs_1_
  111.5 31.1 %two_phase_4.1 = bf16[64,16,32]{2,1,0:T(8,128)(2,1)} custom-call(f32[64,16,32]{2,1,0:T(8,128)} %bitcast.62, f32[16,32]{1,0:T(8,128)} %constant_dynamic-slice_fusion.refs_1_), custom_call_target="tpu_custom_call" | custom-call | bytes 393216 | tf_op jit(solution)/shard_map/two_phase_4/pallas_call | solution.py:188
  142.5 1.0 copy.66
  143.6 0.9 reshape.168
  (70 shorter events, 3.6 us)
Async XLA Ops:
  0.0 1.4 copy-start
  2.6 26.6 %copy-start.12 = (bf16[2048]{0:T(1024)(128)(2,1)S(1)}, bf16[2048]{0:T(1024)(128)(2,1)}, u32[]{:S(2)}) copy-start(bf16[2048]{0:T(1024)(128)(2,1)} %param.17) | copy-start | bytes 12292
  2.6 26.6 %copy-start.9 = (bf16[2048,48]{0,1:T(8,128)(2,1)S(1)}, bf16[2048,48]{0,1:T(8,128)(2,1)}, u32[]{:S(2)}) copy-start(bf16[2048,48]{0,1:T(8,128)(2,1)} %param.19) | copy-start | bytes 589828
  27.5 1.5 %copy-start.1 = (bf16[64,16,32]{2,1,0:T(8,128)(2,1)S(1)}, bf16[64,16,32]{2,1,0:T(8,128)(2,1)}, u32[]{:S(2)}) copy-start(bf16[64,16,32]{2,1,0:T(8,128)(2,1)} %exchange_0.1) | copy-start | bytes 196612
  28.7 19.5 %copy-start.14 = (s32[4]{0:T(128)S(1)}, s32[4]{0:T(128)}, u32[]{:S(2)}) copy-start(s32[4]{0:T(128)} %param.13) | copy-start | bytes 52
  48.8 1.7 %copy-start.10 = (bf16[4,4,8,4,64]{4,3,2,1,0:T(4,128)(2,1)}, bf16[4,4,8,4,64]{4,3,2,1,0:T(4,128)(2,1)S(1)}, u32[]{:S(2)}) copy-start(bf16[4,4,8,4,64]{4,3,2,1,0:T(4,128)(2,1)S(1)} %pad_maximum_fusion) | copy-start | bytes 196612
  49.0 6.0 %copy-start.4 = (bf16[4,128,512]{2,1,0:T(8,128)(2,1)S(1)}, bf16[4,128,512]{2,1,0:T(8,128)(2,1)}, u32[]{:S(2)}) copy-start(bf16[4,128,512]{2,1,0:T(8,128)(2,1)} %param.15) | copy-start | bytes 1572868
  50.4 0.6 copy-start.7
  51.1 6.8 %copy-start.5 = (bf16[4,128,512]{2,1,0:T(8,128)(2,1)S(1)}, bf16[4,128,512]{2,1,0:T(8,128)(2,1)}, u32[]{:S(2)}) copy-start(bf16[4,128,512]{2,1,0:T(8,128)(2,1)} %param.16) | copy-start | bytes 1572868
  57.9 1.8 %copy-start.6 = (f32[4,4,8,4,128]{4,3,1,2,0:T(4,128)S(1)}, f32[4,4,8,4,128]{4,3,1,2,0:T(4,128)}, u32[]{:S(2)}) copy-start(f32[4,4,8,4,128]{4,3,1,2,0:T(4,128)} %get-tuple-element.18) | copy-start | bytes 786436
  57.9 1.8 %copy-start.8 = (f32[4,4,8,4]{3,1,2,0:T(4,128)S(1)}, f32[4,4,8,4]{3,1,2,0:T(4,128)}, u32[]{:S(2)}) copy-start(f32[4,4,8,4]{3,1,2,0:T(4,128)} %get-tuple-element.17) | copy-start | bytes 6148
  59.7 28.6 %copy-start.11 = (bf16[2048,32]{0,1:T(8,128)(2,1)S(1)}, bf16[2048,32]{0,1:T(8,128)(2,1)}, u32[]{:S(2)}) copy-start(bf16[2048,32]{0,1:T(8,128)(2,1)} %param.20) | copy-start | bytes 393220
  106.1 1.7 %copy-start.13 = (bf16[2048]{0:T(1024)(128)(2,1)S(1)}, bf16[2048]{0:T(1024)(128)(2,1)}, u32[]{:S(2)}) copy-start(bf16[2048]{0:T(1024)(128)(2,1)} %param.18) | copy-start | bytes 12292
  107.3 1.8 %copy-start.2 = (bf16[128,2048]{1,0:T(8,128)(2,1)S(1)}, bf16[128,2048]{1,0:T(8,128)(2,1)}, u32[]{:S(2)}) copy-start(bf16[128,2048]{1,0:T(8,128)(2,1)} %param.23) | copy-start | bytes 1572868
  107.3 1.8 %copy-start.3 = (bf16[2048,128]{1,0:T(8,128)(2,1)S(1)}, bf16[2048,128]{1,0:T(8,128)(2,1)}, u32[]{:S(2)}) copy-start(bf16[2048,128]{1,0:T(8,128)(2,1)} %param.22) | copy-start | bytes 1572868

commit v16 on v14

--- a/solution.py
+++ b/solution.py
@@ -89,9 +89,9 @@
         copy(j, mine).start()
         return carry
 
-    lax.fori_loop(0, m - 1, send, 0)
     local = pltpu.make_async_copy(source(mine), buf.at[mine], local_sem)
     local.start()
+    lax.fori_loop(0, m - 1, send, 0)
     rest = buf.at[pl.ds(0, m - 1)]
     every = pltpu.make_async_remote_copy(
         src_ref=rest,

time: 142 us -> 142 us (level)
  no operation moved by 1% of the time
where the time goes in v16:
time: 142 us
  Pallas kernels  112 us (79%)
  local copies, waits for them, and re-layouts  11.4 us (8%)
  matrix products  10.1 us (7%)
  other arithmetic  7.15 us (5%)
    pallas_call x3, Pallas kernels, exchange(): pl.pallas_call(functools.partial(_exchange_kernel, n, gather), out_shape=...  57.7 us
    pallas_call x2, Pallas kernels, two_phase(): pl.pallas_call(functools.partial(_two_phase_kernel, n, combine, len(extra...  54.8 us
    dot_general x2, matrix products, partial_softmax(): jnp.einsum('rskgd,rpkd->rskgp', queries, keys, preferred_element_type=jnp...  3.84 us

profile of v16, /device:TPU:1, one launch (start us, length us, event | category | flops | bytes accessed | tf_op | source)
XLA Modules:
  0.0 141.5 jit_solution(15879286481123940595)
XLA Ops:
  0.0 0.9 eq.15
  0.9 0.5 copy-done
  1.4 1.2 fusion.3.x_ref
  2.6 24.3 %exchange_0.1 = bf16[64,16,32]{2,1,0:T(8,128)(2,1)} custom-call(bf16[16,32]{1,0:T(8,128)(2,1)} %fusion.3.x_ref), custom_call_target="tpu_custom_call" | custom-call | bytes 131072 | tf_op jit(solution)/shard_map/exchange_0/pallas_call | solution.py:49
  27.0 1.1 convert_bitcast_fusion
  28.8 0.8 convolution_convert_fusion.1.x_ref
  29.6 16.1 %exchange_1.1 = bf16[64,16,48]{2,1,0:T(8,128)(2,1)} custom-call(bf16[16,48]{1,0:T(8,128)(2,1)} %convolution_convert_fusion.1.x_ref), custom_call_target="tpu_custom_call" | custom-call | bytes 196608 | tf_op jit(solution)/shard_map/exchange_1/pallas_call | solution.py:49
  45.7 1.0 copy.45
  46.7 0.3 reshape.156
  48.1 1.3 select_reduce_fusion
  49.5 0.4 convolution_bitcast_fusion.1
  50.2 1.3 fusion.15
  51.5 0.8 copy.60
  52.7 0.7 maximum_maximum_fusion.1.refs_1_
  53.4 0.7 broadcast_compare_fusion
  54.1 0.3 copy.48
  54.4 2.5 %select_reduce_fusion.1 = (f32[4,4,8,4]{3,1,2,0:T(4,128)}, f32[4,4,8,4,128]{4,3,1,2,0:T(4,128)}) fusion(pred[4,128]{1,0:T(4,128)(4,1)S(1)} %broadcast_compare_fusion, bf16[4,128,8,64,1]{1,3,4,2,0:T(8,128)(2,1)S(1)} %bitcast.68, bf16[4,4,8,4,64]{4,3,2,1,0:T(4,128)(2,1)} %copy-done.10), kind=kOutput, calls=%fused_computation.29 | convolution fusion | flops 8584704 | bytes 854528 | tf_op jit(solution)/shard_map/rskgd,rpkd->rskgp/dot_general | solution.py:254
  57.2 1.4 %convolution_bitcast_fusion = f32[4,4,8,4,64]{4,3,1,2,0:T(4,128)S(1)} fusion(bf16[4,128,8,64,1]{1,3,4,2,0:T(8,128)(2,1)S(1)} %bitcast.69, f32[4,4,8,4,128]{4,3,1,2,0:T(4,128)} %get-tuple-element.18, f32[4,4,8,4]{3,1,2,0:T(4,128)} %get-tuple-element.17, pred[4,128]{1,0:T(4,128)(4,1)S(1)} %broadcast_compare_fusion), kind=kOutput, calls=%fused_computation.4 | convolution fusion | flops 8585216 | bytes 920064 | tf_op jit(solution)/shard_map/rskgp,rpkd->rskgd/dot_general | solution.py:260
  58.7 0.4 fusion.13
  59.4 0.9 maximum_maximum_fusion.refs_0_
  60.3 24.0 %two_phase_2.1 = bf16[64,8,64]{2,1,0:T(8,128)(2,1)} custom-call(f32[64,8,128]{2,1,0:T(8,128)} %maximum_maximum_fusion.refs_0_, f32[8,128]{1,0:T(8,128)} %maximum_maximum_fusion.1.refs_1_), custom_call_target="tpu_custom_call" | custom-call | bytes 655360 | tf_op jit(solution)/shard_map/two_phase_2/pallas_call | solution.py:185
  84.3 1.1 reshape.166
  85.4 0.8 convolution_convert_fusion.x_ref
  86.2 17.2 %exchange_3.1 = bf16[64,16,32]{2,1,0:T(8,128)(2,1)} custom-call(bf16[16,32]{1,0:T(8,128)(2,1)} %convolution_convert_fusion.x_ref), custom_call_target="tpu_custom_call" | custom-call | bytes 131072 | tf_op jit(solution)/shard_map/exchange_3/pallas_call | solution.py:49
  103.4 1.2 fusion.11
  105.1 1.3 fusion.44
  106.4 0.4 fusion.5
  107.0 1.1 copy.92
  108.1 0.7 constant_dynamic-slice_fusion.refs_1_
  108.8 30.8 %two_phase_4.1 = bf16[64,16,32]{2,1,0:T(8,128)(2,1)} custom-call(f32[64,16,32]{2,1,0:T(8,128)} %bitcast.62, f32[16,32]{1,0:T(8,128)} %constant_dynamic-slice_fusion.refs_1_), custom_call_target="tpu_custom_call" | custom-call | bytes 393216 | tf_op jit(solution)/shard_map/two_phase_4/pallas_call | solution.py:185
  139.6 1.0 copy.66
  140.6 0.9 reshape.168
  (70 shorter events, 3.6 us)
Async XLA Ops:
  0.0 1.4 %copy-start = (bf16[32,24704]{1,0:T(8,128)(2,1)S(1)}, bf16[32,24704]{1,0:T(8,128)(2,1)}, u32[]{:S(2)}) copy-start(bf16[32,24704]{1,0:T(8,128)(2,1)} %param.14) | copy-start | bytes 4743172
  2.6 26.1 %copy-start.12 = (bf16[2048]{0:T(1024)(128)(2,1)S(1)}, bf16[2048]{0:T(1024)(128)(2,1)}, u32[]{:S(2)}) copy-start(bf16[2048]{0:T(1024)(128)(2,1)} %param.17) | copy-start | bytes 12292
  2.6 26.1 %copy-start.9 = (bf16[2048,48]{0,1:T(8,128)(2,1)S(1)}, bf16[2048,48]{0,1:T(8,128)(2,1)}, u32[]{:S(2)}) copy-start(bf16[2048,48]{0,1:T(8,128)(2,1)} %param.19) | copy-start | bytes 589828
  27.0 1.5 %copy-start.1 = (bf16[64,16,32]{2,1,0:T(8,128)(2,1)S(1)}, bf16[64,16,32]{2,1,0:T(8,128)(2,1)}, u32[]{:S(2)}) copy-start(bf16[64,16,32]{2,1,0:T(8,128)(2,1)} %exchange_0.1) | copy-start | bytes 196612
  28.2 19.0 %copy-start.14 = (s32[4]{0:T(128)S(1)}, s32[4]{0:T(128)}, u32[]{:S(2)}) copy-start(s32[4]{0:T(128)} %param.13) | copy-start | bytes 52
  47.8 1.7 %copy-start.10 = (bf16[4,4,8,4,64]{4,3,2,1,0:T(4,128)(2,1)}, bf16[4,4,8,4,64]{4,3,2,1,0:T(4,128)(2,1)S(1)}, u32[]{:S(2)}) copy-start(bf16[4,4,8,4,64]{4,3,2,1,0:T(4,128)(2,1)S(1)} %pad_maximum_fusion) | copy-start | bytes 196612
  48.0 6.0 %copy-start.4 = (bf16[4,128,512]{2,1,0:T(8,128)(2,1)S(1)}, bf16[4,128,512]{2,1,0:T(8,128)(2,1)}, u32[]{:S(2)}) copy-start(bf16[4,128,512]{2,1,0:T(8,128)(2,1)} %param.15) | copy-start | bytes 1572868
  49.4 0.6 copy-start.7
  50.1 6.8 %copy-start.5 = (bf16[4,128,512]{2,1,0:T(8,128)(2,1)S(1)}, bf16[4,128,512]{2,1,0:T(8,128)(2,1)}, u32[]{:S(2)}) copy-start(bf16[4,128,512]{2,1,0:T(8,128)(2,1)} %param.16) | copy-start | bytes 1572868
  56.9 1.8 %copy-start.6 = (f32[4,4,8,4,128]{4,3,1,2,0:T(4,128)S(1)}, f32[4,4,8,4,128]{4,3,1,2,0:T(4,128)}, u32[]{:S(2)}) copy-start(f32[4,4,8,4,128]{4,3,1,2,0:T(4,128)} %get-tuple-element.18) | copy-start | bytes 786436
  56.9 1.8 %copy-start.8 = (f32[4,4,8,4]{3,1,2,0:T(4,128)S(1)}, f32[4,4,8,4]{3,1,2,0:T(4,128)}, u32[]{:S(2)}) copy-start(f32[4,4,8,4]{3,1,2,0:T(4,128)} %get-tuple-element.17) | copy-start | bytes 6148
  58.7 26.7 %copy-start.11 = (bf16[2048,32]{0,1:T(8,128)(2,1)S(1)}, bf16[2048,32]{0,1:T(8,128)(2,1)}, u32[]{:S(2)}) copy-start(bf16[2048,32]{0,1:T(8,128)(2,1)} %param.20) | copy-start | bytes 393220
  103.4 1.7 %copy-start.13 = (bf16[2048]{0:T(1024)(128)(2,1)S(1)}, bf16[2048]{0:T(1024)(128)(2,1)}, u32[]{:S(2)}) copy-start(bf16[2048]{0:T(1024)(128)(2,1)} %param.18) | copy-start | bytes 12292
  104.6 1.8 %copy-start.2 = (bf16[128,2048]{1,0:T(8,128)(2,1)S(1)}, bf16[128,2048]{1,0:T(8,128)(2,1)}, u32[]{:S(2)}) copy-start(bf16[128,2048]{1,0:T(8,128)(2,1)} %param.23) | copy-start | bytes 1572868
  104.6 1.8 %copy-start.3 = (bf16[2048,128]{1,0:T(8,128)(2,1)S(1)}, bf16[2048,128]{1,0:T(8,128)(2,1)}, u32[]{:S(2)}) copy-start(bf16[2048,128]{1,0:T(8,128)(2,1)} %param.22) | copy-start | bytes 1572868
